TPU v7x, 32 devices: a whole 2x2x4 slice. The times are simulated.
32 devices in a mesh: groups: 2 (over y), context: 8 (over z, x), tensor: 2 (over core).
Axes of the slice: x: 2, y: 2, z: 4, core: 2. Of those that a mesh axis runs over, the one named last changes fastest.
Arguments:
- query_rows: bfloat16 [8192, 2048], P(('groups', 'context'), 'tensor'), parts along dimension 0, may hold values from -16 to 16, as said below
- key_rows: bfloat16 [8192, 2048], P(('groups', 'context'), 'tensor'), parts along dimension 0, may hold values from -6 to 6, as said below
- value_rows: bfloat16 [8192, 2048], P(('groups', 'context'), 'tensor'), parts along dimension 0, may hold values from -6 to 6
- selection: int32 [16, 16], P('tensor', ('groups', 'context')), parts along dimension 1, may hold values from 0 to 7, as said below
Outputs:
- attended: bfloat16 [8192, 2048], P(('groups', 'context'), 'tensor'), parts along dimension 0
- sort_logits: float32 [16, 16, 8], P('tensor', ('groups', 'context')), parts along dimension 1
There are 2 independent parts, one for each index of `groups`. A program takes and returns all parts, laid end to end along the dimension named above; each array names one. Nothing has to cross between parts.
Inputs may be any that keep to these rules, and one draw needn't show every extreme that they name: `query_rows`: Queries; of order a few units. `key_rows`: Keys; of order one. `selection`: for each head, a permutation of the 8 blocks.
All inputs are finite; a program needn't handle non-finite values.
Results may differ from a plain program's by a relative error of at most 0.0048.
Values may be sent and summed in bfloat16 or wider, within the bound.
No kernel may reach another device: no remote copies, remote signals or barrier semaphores. Data moves between devices by JAX's collectives and lax.ppermute only.
A program may use at most 64 MiB of HBM per device.

v0:
```python
import math

import jax
import jax.numpy as jnp
from jax import lax
from jax.sharding import PartitionSpec as P

DH = 128
BS = 512


def block_partial(query_block, key_block, value_block):
    scores = jnp.dot(query_block, key_block.T, preferred_element_type=jnp.float32) * (
        1.0 / math.sqrt(DH)
    )
    row_max = jnp.max(scores, axis=1, keepdims=True)
    weights = jnp.exp(scores - row_max).astype(jnp.bfloat16)
    row_total = jnp.sum(weights.astype(jnp.float32), axis=1, keepdims=True)
    partial_sum = jnp.dot(weights, value_block, preferred_element_type=jnp.float32)
    return (row_max, row_total, partial_sum)


def combine_parts(own_part, far_part):
    own_max, own_total, own_sum = own_part
    far_max, far_total, far_sum = far_part
    joint = jnp.maximum(own_max, far_max)
    own_factor = jnp.exp(own_max - joint)
    far_factor = jnp.exp(far_max - joint)
    merged = (own_factor * own_sum + far_factor * far_sum) / (
        own_factor * own_total + far_factor * far_total
    )
    return merged.astype(jnp.bfloat16)


def per_device(query_rows, key_rows, value_rows, selection):
    members = lax.axis_size("context")
    tok_rows, width = query_rows.shape
    blocks = tok_rows // BS
    head_count = width // DH
    piece_rows = BS // members

    def pooled(rows_in):
        sums = jnp.sum(rows_in.reshape(blocks, BS, width), axis=1, dtype=jnp.float32) / math.sqrt(
            BS
        )
        return sums.astype(jnp.bfloat16).reshape(blocks, head_count, DH).transpose(1, 0, 2)

    pooled_q = pooled(query_rows)
    pooled_k = pooled(key_rows)
    products = jnp.einsum(
        "hbd,hcd->hbc",
        pooled_q,
        lax.all_gather(pooled_k, "context", axis=1, tiled=True),
        preferred_element_type=jnp.float32,
    )
    sort_logits = products / math.sqrt(DH)
    wanted = lax.all_gather(selection, "context", axis=1, tiled=True)
    query_grid = query_rows.reshape(blocks, BS, head_count, DH)
    key_grid = key_rows.reshape(blocks, BS, head_count, DH)
    value_grid = value_rows.reshape(blocks, BS, head_count, DH)
    pair_ids = jnp.arange(blocks * head_count, dtype=jnp.int32)

    def slice_pair(array, block, head):
        return lax.dynamic_slice(array, (block, 0, head, 0), (1, BS, 1, DH)).reshape(BS, DH)

    def pick_rows(held, table):
        inner = held.shape[-1] // head_count
        order_ids = table.reshape(head_count, members, blocks).transpose(2, 1, 0)
        source_dev = (order_ids // blocks)[:, :, None, :]
        source_blk = (order_ids % blocks)[:, :, None, :]
        row_ids = jnp.arange(piece_rows)[None, None, :, None]
        head_ids = jnp.arange(head_count)[None, None, None, :]
        grid = held.reshape(blocks, members, piece_rows, head_count, inner)
        return grid[source_blk, source_dev, row_ids, head_ids].reshape(
            blocks, members, piece_rows, head_count * inner
        )

    spread_k = key_rows.reshape(blocks, members, piece_rows, width)
    spread_v = value_rows.reshape(blocks, members, piece_rows, width)
    held_k = lax.all_to_all(spread_k, "context", split_axis=1, concat_axis=1, tiled=True)
    held_v = lax.all_to_all(spread_v, "context", split_axis=1, concat_axis=1, tiled=True)
    far_k = lax.all_to_all(
        pick_rows(held_k, wanted), "context", split_axis=1, concat_axis=1, tiled=True
    )
    far_v = lax.all_to_all(
        pick_rows(held_v, wanted), "context", split_axis=1, concat_axis=1, tiled=True
    )
    far_keys = far_k.reshape(blocks, BS, head_count, DH)
    far_values = far_v.reshape(blocks, BS, head_count, DH)

    def both_pair(pair_index):
        block = pair_index // head_count
        head = pair_index % head_count
        query_block = slice_pair(query_grid, block, head)
        own = block_partial(
            query_block, slice_pair(key_grid, block, head), slice_pair(value_grid, block, head)
        )
        far = block_partial(
            query_block, slice_pair(far_keys, block, head), slice_pair(far_values, block, head)
        )
        return combine_parts(own, far)

    outputs = lax.map(both_pair, pair_ids)
    attended = (
        outputs.reshape(blocks, head_count, BS, DH).transpose(0, 2, 1, 3).reshape(tok_rows, width)
    )
    return (attended, sort_logits)


def solution(mesh):
    placed = (
        P(("groups", "context"), "tensor"),
        P(("groups", "context"), "tensor"),
        P(("groups", "context"), "tensor"),
        P("tensor", ("groups", "context")),
    )
    return jax.shard_map(
        per_device,
        mesh=mesh,
        in_specs=placed,
        out_specs=(P(("groups", "context"), "tensor"), P("tensor", ("groups", "context"), None)),
        check_vma=False,
    )
```

profile of v0, /device:TPU:0, one launch (start us, length us, event | category | flops | bytes accessed | tf_op | source)
XLA Modules:
  0.0 235.9 jit_solution(7391589697294675060)
XLA Ops:
  0.6 33.0 %all_to_all.20 = bf16[1,8,64,1024]{3,2,0,1:T(8,128)(2,1)S(1)} all-to-all(bf16[1,8,64,1024]{3,2,0,1:T(8,128)(2,1)} %bitcast.118), channel_id=1, replica_groups=mesh['groups'=2,'context'=8,'tensor'=2] {'context'}, dimensions={1} | all-to-all | bytes 2097152 | tf_op jit(solution)/shard_map/all_to_all | solution.py:80
  33.7 3.7 %all-to-all-start.2 = ((bf16[1,8,64,1024]{3,2,0,1:T(8,128)(2,1)}), bf16[1,8,64,1024]{3,2,0,1:T(8,128)(2,1)S(1)}, u32[]{:S(2)}, u32[]{:S(2)}) async-start(bf16[1,8,64,1024]{3,2,0,1:T(8,128)(2,1)} %bitcast.19), calls=%async_computation.2 | async-start | bytes 2097152 | tf_op jit(solution)/shard_map/all_to_all | solution.py:81
  37.4 31.1 %all-gather = s32[8,1,8]{2,1,0:T(1,128)S(1)} all-gather(s32[1,1,8]{2,1,0:T(1,128)S(1)} %bitcast.133), channel_id=1, replica_groups=mesh['groups'=2,'context'=8,'tensor'=2] {'context'}, dimensions={0}, use_global_device_ids=true | all-gather | bytes 288 | tf_op jit(solution)/shard_map/all_gather | solution.py:57
  69.4 25.2 %gather_fusion = bf16[4096,128]{1,0:T(8,128)(2,1)S(1)} fusion(bf16[1,8,64,8,128]{4,3,2,1,0:T(8,128)(2,1)S(1)} %bitcast.117, s32[4096]{0:T(1024)S(1)} %reshape.216), kind=kCustom, calls=%fused_computation | custom fusion | bytes 2162688 | tf_op jit(solution)/shard_map/gather | solution.py:74
  94.6 1.3 reshape.205
  95.9 6.2 %all-to-all-start.1 = ((bf16[1,8,64,1024]{3,2,0,1:T(8,128)(2,1)}), bf16[1,8,64,1024]{3,2,0,1:T(8,128)(2,1)S(1)}, u32[]{:S(2)}, u32[]{:S(2)}) async-start(bf16[1,8,64,1024]{3,2,0,1:T(8,128)(2,1)} %bitcast.17), calls=%async_computation.1 | async-start | bytes 2097152 | tf_op jit(solution)/shard_map/all_to_all | solution.py:82
  102.3 25.2 %gather_fusion.1 = bf16[4096,128]{1,0:T(8,128)(2,1)S(1)} fusion(bf16[1,8,64,8,128]{4,3,2,1,0:T(8,128)(2,1)S(1)} %bitcast.116, s32[4096]{0:T(1024)S(1)} %reshape.216), kind=kCustom, calls=%fused_computation.1 | custom fusion | bytes 2162688 | tf_op jit(solution)/shard_map/gather | solution.py:74
  127.6 1.3 reshape.210
  129.9 6.0 %all-to-all-start.3 = ((bf16[1,8,64,1024]{3,2,0,1:T(8,128)(2,1)}), bf16[1,8,64,1024]{3,2,0,1:T(8,128)(2,1)}, u32[]{:S(2)}, u32[]{:S(2)}) async-start(bf16[1,8,64,1024]{3,2,0,1:T(8,128)(2,1)} %bitcast.20), calls=%async_computation.3 | async-start | bytes 2097152 | tf_op jit(solution)/shard_map/all_to_all | solution.py:85
  135.9 2.4 %copy.32 = bf16[512,1024]{0,1:T(8,128)(2,1)} copy(bf16[512,1024]{1,0:T(8,128)(2,1)} %param.8) | data formatting | bytes 2097152 | tf_op args[2]
  138.3 1.3 copy.27
  140.3 36.3 %all_gather.7 = bf16[8,8,128]{2,0,1:T(8,128)(2,1)S(1)} all-gather(bf16[8,1,128]{2,0,1:T(8,128)(2,1)S(1)} %fusion.34), channel_id=1, replica_groups=mesh['groups'=2,'context'=8,'tensor'=2] {'context'}, dimensions={1}, use_global_device_ids=true | all-gather | bytes 18432 | tf_op jit(solution)/shard_map/all_gather | solution.py:53
  178.0 1.5 copy.50
  179.6 53.1 %while.12 = (s32[]{:T(128)}, bf16[8,512,128]{2,1,0:T(8,128)(2,1)}, s32[8]{0:T(128)S(1)}, bf16[1,512,8,128]{1,3,2,0:T(8,128)(2,1)S(1)}, bf16[1,512,8,128]{1,3,2,0...) while((s32[]{:T(128)}, bf16[8,512,128]{2,1,0:T(8,128)(2,1)}, ...), condition=%wide.region_5.6_spmd, body=%wide.region_0.5_spmd.sunk | while | flops 272958464 | bytes 7772952 | solution.py:103
  184.3 1.9 fusion.48
  189.0 1.3 fusion.47
  191.0 1.9 fusion.48
  197.6 1.9 fusion.48
  204.2 1.9 fusion.48
  210.9 1.9 fusion.48
  217.5 1.9 fusion.48
  224.1 1.9 fusion.48
  230.8 1.9 fusion.48
  232.7 1.9 copy.39
  (86 shorter events, 26.8 us)
Async XLA Ops:
  33.7 3.7 %copy-start.4 = (s32[8,1]{0,1:T(1,128)S(1)}, s32[8,1]{0,1:T(1,128)}, u32[]{:S(2)}) copy-start(s32[8,1]{0,1:T(1,128)} %param.9) | copy-start | bytes 100
  33.7 62.3 %all-to-all-start.2 = ((bf16[1,8,64,1024]{3,2,0,1:T(8,128)(2,1)}), bf16[1,8,64,1024]{3,2,0,1:T(8,128)(2,1)S(1)}, u32[]{:S(2)}, u32[]{:S(2)}) async-start(bf16[1,8,64,1024]{3,2,0,1:T(8,128)(2,1)} %bitcast.19), calls=%async_computation.2 | async-start | bytes 2097152 | tf_op jit(solution)/shard_map/all_to_all | solution.py:81
  95.9 33.0 %all-to-all-start.1 = ((bf16[1,8,64,1024]{3,2,0,1:T(8,128)(2,1)}), bf16[1,8,64,1024]{3,2,0,1:T(8,128)(2,1)S(1)}, u32[]{:S(2)}, u32[]{:S(2)}) async-start(bf16[1,8,64,1024]{3,2,0,1:T(8,128)(2,1)} %bitcast.17), calls=%async_computation.1 | async-start | bytes 2097152 | tf_op jit(solution)/shard_map/all_to_all | solution.py:82
  128.9 1.0 copy-start.2
  129.9 48.1 %all-to-all-start.3 = ((bf16[1,8,64,1024]{3,2,0,1:T(8,128)(2,1)}), bf16[1,8,64,1024]{3,2,0,1:T(8,128)(2,1)}, u32[]{:S(2)}, u32[]{:S(2)}) async-start(bf16[1,8,64,1024]{3,2,0,1:T(8,128)(2,1)} %bitcast.20), calls=%async_computation.3 | async-start | bytes 2097152 | tf_op jit(solution)/shard_map/all_to_all | solution.py:85
  135.9 2.4 %copy-start = (bf16[512,1024]{1,0:T(8,128)(2,1)S(1)}, bf16[512,1024]{1,0:T(8,128)(2,1)}, u32[]{:S(2)}) copy-start(bf16[512,1024]{1,0:T(8,128)(2,1)} %param.7) | copy-start | bytes 3145732
  138.3 1.3 copy-start.1
  140.1 37.4 %copy-start.3 = (bf16[1,8,64,1024]{3,2,0,1:T(8,128)(2,1)S(1)}, bf16[1,8,64,1024]{3,2,0,1:T(8,128)(2,1)}, u32[]{:S(2)}) copy-start(bf16[1,8,64,1024]{3,2,0,1:T(8,128)(2,1)} %copy-done.2) | copy-start | bytes 3145732
where the time goes:
time: 237 us; the launch traced here: 236 us
  blocking collectives  100 us (42%)
  local copies, waits for them, and re-layouts  69.2 us (29%)
  matrix products  30.8 us (13%)
  starting transfers between devices  15.9 us (7%)
  loops' own time  15.1 us (6%)
  other arithmetic  3.6 us (2%)
    gather x2, local copies, waits for them, and re-layouts, pick_rows(): grid[source_blk, source_dev, row_ids, head_ids]  50.5 us
    all_gather x1, blocking collectives, per_device(): lax.all_gather(pooled_k, 'context', axis=1, tiled=True)  36.3 us
    all_to_all x1, blocking collectives, per_device(): lax.all_to_all(spread_k, 'context', split_axis=1, concat_axis=1, tiled=True)  33 us
    all_gather x1, blocking collectives, per_device(): wanted = lax.all_gather(selection, 'context', axis=1, tiled=True)  31.1 us
    dot_general x16, matrix products, block_partial(): jnp.dot(weights, value_block, preferred_element_type=jnp.float32)  18.2 us
    another operation x1, loops' own time, per_device(): outputs = lax.map(both_pair, pair_ids)  15.1 us
    dot_general x16, matrix products, block_partial(): jnp.dot(query_block, key_block.T, preferred_element_type=jnp.float32)  12.5 us
    unnamed x19, local copies, waits for them, and re-layouts  8.85 us
  transfers between devices with their start and end apart: 3, of which 0 were waited for; matrix products, arithmetic and copies ran while one was open for 25% of the time, Pallas kernels for 0%

commit v1 on v0

--- a/solution.py
+++ b/solution.py
@@ -1,12 +1,17 @@
+import functools
 import math
 
 import jax
 import jax.numpy as jnp
 from jax import lax
+from jax.experimental import pallas as pl
+from jax.experimental.pallas import tpu as pltpu
 from jax.sharding import PartitionSpec as P
 
 DH = 128
 BS = 512
+BF16 = jnp.bfloat16
+F32 = jnp.float32
 
 
 def block_partial(query_block, key_block, value_block):
@@ -32,7 +37,7 @@
     return merged.astype(jnp.bfloat16)
 
 
-def per_device(query_rows, key_rows, value_rows, selection):
+def any_size(query_rows, key_rows, value_rows, selection):
     members = lax.axis_size("context")
     tok_rows, width = query_rows.shape
     blocks = tok_rows // BS
@@ -107,7 +112,180 @@
     return (attended, sort_logits)
 
 
+def pick_kernel(members, heads, table, *refs):
+    pieces, outs, held = refs[:members], refs[members : 2 * members], refs[2 * members]
+    for e in range(members):
+        held[e] = pieces[e][...]
+    for d in range(members):
+        for h in range(heads):
+            cols = pl.ds(h * DH, DH)
+            outs[d][:, cols] = held[table[d, h], :, cols]
+
+
+def pick_pieces(table, pieces):
+    members = len(pieces)
+    rows, width = pieces[0].shape
+    spec = pl.BlockSpec((rows, width), lambda i, t: (0, 0))
+    return pl.pallas_call(
+        functools.partial(pick_kernel, members, width // DH),
+        grid_spec=pltpu.PrefetchScalarGridSpec(
+            num_scalar_prefetch=1,
+            grid=(1,),
+            in_specs=[spec] * members,
+            out_specs=[spec] * members,
+            scratch_shapes=[pltpu.VMEM((members, rows, width), BF16)],
+        ),
+        out_shape=[jax.ShapeDtypeStruct((rows, width), BF16)] * members,
+        cost_estimate=pl.CostEstimate(
+            flops=0, transcendentals=0, bytes_accessed=4 * members * rows * width
+        ),
+    )(table, *pieces)
+
+
+def scores_kernel(members, q_ref, k_ref, v_ref, *refs):
+    far_k, (own_ref, w_ref, kf_ref) = refs[:members], refs[members:]
+    rows = far_k[0].shape[0]
+    for e in range(members):
+        kf_ref[pl.ds(e * rows, rows), :] = far_k[e][...]
+    q = q_ref[...]
+
+    def part(keys):
+        s = lax.dot_general(
+            q, keys, (((1,), (1,)), ((), ())), preferred_element_type=F32
+        ) * (1.0 / math.sqrt(DH))
+        top = jnp.max(s, axis=1, keepdims=True)
+        w = jnp.exp(s - top).astype(BF16)
+        return top, w, jnp.sum(w.astype(F32), axis=1, keepdims=True)
+
+    own_max, own_w, own_total = part(k_ref[...])
+    own_sum = jnp.dot(own_w, v_ref[...], preferred_element_type=F32)
+    far_max, far_w, far_total = part(kf_ref[...])
+    joint = jnp.maximum(own_max, far_max)
+    own_e = jnp.exp(own_max - joint)
+    far_e = jnp.exp(far_max - joint)
+    inverse = 1.0 / (own_e * own_total + far_e * far_total)
+    own_ref[...] = own_sum * (own_e * inverse)
+    w_ref[0] = (far_w.astype(F32) * (far_e * inverse)).astype(BF16)
+
+
+def score_parts(q, k, v, far_k):
+    members = len(far_k)
+    tok, width = q.shape
+    heads = width // DH
+    rows = far_k[0].shape[0]
+    whole = pl.BlockSpec((tok, DH), lambda h: (0, h))
+    piece = pl.BlockSpec((rows, DH), lambda h: (0, h))
+    return pl.pallas_call(
+        functools.partial(scores_kernel, members),
+        grid=(heads,),
+        in_specs=[whole] * 3 + [piece] * members,
+        out_specs=[whole, pl.BlockSpec((1, tok, BS), lambda h: (h, 0, 0))],
+        out_shape=[
+            jax.ShapeDtypeStruct((tok, width), F32),
+            jax.ShapeDtypeStruct((heads, tok, BS), BF16),
+        ],
+        scratch_shapes=[pltpu.VMEM((BS, DH), BF16)],
+        compiler_params=pltpu.CompilerParams(vmem_limit_bytes=40 << 20),
+        cost_estimate=pl.CostEstimate(
+            flops=6 * tok * BS * width,
+            transcendentals=2 * heads * tok * BS,
+            bytes_accessed=12 * tok * width + 2 * heads * tok * BS,
+        ),
+    )(q, k, v, *far_k)
+
+
+def finish_kernel(members, w_ref, own_ref, *refs):
+    far_v, (out_ref, vf_ref) = refs[:members], refs[members:]
+    rows = far_v[0].shape[0]
+    for e in range(members):
+        vf_ref[pl.ds(e * rows, rows), :] = far_v[e][...]
+    out_ref[...] = (
+        own_ref[...] + jnp.dot(w_ref[0], vf_ref[...], preferred_element_type=F32)
+    ).astype(BF16)
+
+
+def finish(w, own, far_v):
+    members = len(far_v)
+    tok, width = own.shape
+    heads = width // DH
+    rows = far_v[0].shape[0]
+    whole = pl.BlockSpec((tok, DH), lambda h: (0, h))
+    piece = pl.BlockSpec((rows, DH), lambda h: (0, h))
+    return pl.pallas_call(
+        functools.partial(finish_kernel, members),
+        grid=(heads,),
+        in_specs=[pl.BlockSpec((1, tok, BS), lambda h: (h, 0, 0)), whole] + [piece] * members,
+        out_specs=whole,
+        out_shape=jax.ShapeDtypeStruct((tok, width), BF16),
+        scratch_shapes=[pltpu.VMEM((BS, DH), BF16)],
+        compiler_params=pltpu.CompilerParams(vmem_limit_bytes=40 << 20),
+        cost_estimate=pl.CostEstimate(
+            flops=2 * tok * BS * width,
+            transcendentals=0,
+            bytes_accessed=8 * tok * width + 2 * heads * tok * BS,
+        ),
+    )(w, own, *far_v)
+
+
+def power_of_two(query_rows, key_rows, value_rows, selection):
+    members = lax.axis_size("context")
+    me = lax.axis_index("context")
+    tok, width = query_rows.shape
+    heads = width // DH
+    rows = BS // members
+
+    def send(x, d):
+        return lax.ppermute(x, "context", [(i, i ^ d) for i in range(members)])
+
+    order = sorted(range(1, members), reverse=True)
+
+    def exchange(chunks):
+        got = list(chunks)
+        for d in order:
+            got[d] = send(chunks[d], d)
+        return got
+
+    def split(array):
+        return [array[d * rows : (d + 1) * rows] for d in range(members)]
+
+    def pooled(array):
+        return (jnp.sum(array, axis=0, dtype=F32) / math.sqrt(BS)).astype(BF16)
+
+    chosen = jnp.pad(selection[:, 0].astype(BF16), (0, width - heads))
+    shared = jnp.stack([pooled(key_rows), chosen])[None]
+    d = 1
+    while d < members:
+        shared = jnp.concatenate([shared, send(shared, d)], axis=0)
+        d *= 2
+    table = me ^ shared[:, 1, :heads].astype(jnp.int32)
+
+    held_k = exchange(split(key_rows))
+    held_v = exchange(split(value_rows))
+    far_k = exchange(pick_pieces(table, held_k))
+    far_v = exchange(pick_pieces(table, held_v))
+
+    own, w = score_parts(query_rows, key_rows, value_rows, far_k)
+    attended = finish(w, own, far_v)
+
+    pooled_k = shared[:, 0][me ^ jnp.arange(members)]
+    sort_logits = jnp.einsum(
+        "hd,chd->hc",
+        pooled(query_rows).reshape(heads, DH),
+        pooled_k.reshape(members, heads, DH),
+        preferred_element_type=F32,
+    ) / math.sqrt(DH)
+    return attended, sort_logits.reshape(heads, 1, members)
+
+
 def solution(mesh):
+    members = mesh.shape["context"]
+
+    def per_device(query_rows, key_rows, value_rows, selection):
+        fits = members & (members - 1) == 0 and BS % (16 * members) == 0
+        if query_rows.shape[0] == BS and fits:
+            return power_of_two(query_rows, key_rows, value_rows, selection)
+        return any_size(query_rows, key_rows, value_rows, selection)
+
     placed = (
         P(("groups", "context"), "tensor"),
         P(("groups", "context"), "tensor"),

time: 237 us -> 124 us (0.52)
  the two profiles are of different devices: /device:TPU:0 before, /device:TPU:14 now
where the time goes in v1:
time: 124 us
  starting transfers between devices  46.2 us (37%)
  waiting for transfers between devices  46.1 us (37%)
  Pallas kernels  20.7 us (17%)
  local copies, waits for them, and re-layouts  4.69 us (4%)
  other arithmetic  4.24 us (3%)
    ppermute x31, starting transfers between devices, send(): return lax.ppermute(x, 'context', [(i, i ^ d) for i in range(members)])  46.2 us
    ppermute x31, waiting for transfers between devices, send(): return lax.ppermute(x, 'context', [(i, i ^ d) for i in range(members)])  46.1 us
    pallas_call x1, Pallas kernels, score_parts(): pl.pallas_call(functools.partial(scores_kernel, members), grid=(heads,),...  9.75 us
    pallas_call x2, Pallas kernels, pick_pieces(): pl.pallas_call(functools.partial(pick_kernel, members, width // DH), grid...  6.29 us
    pallas_call x1, Pallas kernels, finish(): pl.pallas_call(functools.partial(finish_kernel, members), grid=(heads,),...  4.62 us
    slice x2, local copies, waits for them, and re-layouts, split(): return [array[d * rows:(d + 1) * rows] for d in range(members)]  3.14 us
  transfers between devices with their start and end apart: 31, of which 10 were waited for; matrix products, arithmetic and copies ran while one was open for 5% of the time, Pallas kernels for 13%

profile of v1, /device:TPU:14, one launch (start us, length us, event | category | flops | bytes accessed | tf_op | source)
XLA Modules:
  0.0 123.5 jit_solution(2356730110439345505)
XLA Ops:
  3.5 2.3 %fusion.6 = (bf16[64,1024]{1,0:T(8,128)(2,1)}, bf16[64,1024]{1,0:T(8,128)(2,1)}, bf16[64,1024]{1,0:T(8,128)(2,1)}, bf16[64,1024]{1,0:T(8,128)(2,1)}, bf16[64,102...) fusion(bf16[512,1024]{1,0:T(8,128)(2,1)} %v_ref.1), kind=kLoop, calls=%fused_computation.22 | loop fusion | bytes 2097152 | tf_op jit(solution)/shard_map/slice | solution.py:249
  5.7 2.5 %collective-permute-start.23 = (bf16[64,1024]{1,0:T(8,128)(2,1)}, bf16[64,1024]{1,0:T(8,128)(2,1)}, u32[]{:S(2)}, u32[]{:S(2)}) collective-permute-start(bf16[64,1024]{1,0:T(8,128)(2,1)} %get-tuple-element.42), channel_id=1, source_target_pairs={{0,14},{2,12},{4,10},{6,8},{8,6},{10,4},{12,2},{14,0},{1,15},{3,13... | collective-permute-start | bytes 393224 | tf_op jit(solution)/shard_map/ppermute | solution.py:238
  11.2 3.4 %collective-permute-start.19 = (bf16[64,1024]{1,0:T(8,128)(2,1)}, bf16[64,1024]{1,0:T(8,128)(2,1)}, u32[]{:S(2)}, u32[]{:S(2)}) collective-permute-start(bf16[64,1024]{1,0:T(8,128)(2,1)} %get-tuple-element.45), channel_id=1, source_target_pairs={{0,6},{2,4},{4,2},{6,0},{8,14},{10,12},{12,10},{14,8},{1,7},{3,5},... | collective-permute-start | bytes 393224 | tf_op jit(solution)/shard_map/ppermute | solution.py:238
  15.7 6.8 %collective-permute-done.1 = bf16[2,2,1024]{2,0,1:T(2,128)(2,1)S(1)} collective-permute-done((bf16[2,2,1024]{2,0,1:T(2,128)(2,1)S(1)}, bf16[2,2,1024]{2,0,1:T(2,128)(2,1)S(1)}, u32[]{:S(2)}, u32[]{:S(2)}) %collective-permute-start.1) | collective-permute-done | bytes 8224 | tf_op jit(solution)/shard_map/ppermute | solution.py:238
  23.2 4.0 %collective-permute-done.2 = bf16[4,2,1024]{2,0,1:T(4,128)(2,1)S(1)} collective-permute-done((bf16[4,2,1024]{2,0,1:T(4,128)(2,1)S(1)}, bf16[4,2,1024]{2,0,1:T(4,128)(2,1)S(1)}, u32[]{:S(2)}, u32[]{:S(2)}) %collective-permute-start.2) | collective-permute-done | bytes 16416 | tf_op jit(solution)/shard_map/ppermute | solution.py:238
  28.4 1.8 %collective-permute-start.22 = (bf16[64,1024]{1,0:T(8,128)(2,1)}, bf16[64,1024]{1,0:T(8,128)(2,1)S(1)}, u32[]{:S(2)}, u32[]{:S(2)}) collective-permute-start(bf16[64,1024]{1,0:T(8,128)(2,1)} %get-tuple-element.49), channel_id=1, source_target_pairs={{0,12},{2,14},{4,8},{6,10},{8,4},{10,6},{12,0},{14,2},{1,13},{3,15... | collective-permute-start | bytes 393224 | tf_op jit(solution)/shard_map/ppermute | solution.py:238
  31.4 1.8 %collective-permute-start.8 = (bf16[64,1024]{1,0:T(8,128)(2,1)}, bf16[64,1024]{1,0:T(8,128)(2,1)S(1)}, u32[]{:S(2)}, u32[]{:S(2)}) collective-permute-start(bf16[64,1024]{1,0:T(8,128)(2,1)} %get-tuple-element.51), channel_id=1, source_target_pairs={{0,12},{2,14},{4,8},{6,10},{8,4},{10,6},{12,0},{14,2},{1,13},{3,15... | collective-permute-start | bytes 393224 | tf_op jit(solution)/shard_map/ppermute | solution.py:238
  33.8 3.2 %collective-permute-start.7 = (bf16[64,1024]{1,0:T(8,128)(2,1)}, bf16[64,1024]{1,0:T(8,128)(2,1)}, u32[]{:S(2)}, u32[]{:S(2)}) collective-permute-start(bf16[64,1024]{1,0:T(8,128)(2,1)} %get-tuple-element.52), channel_id=1, source_target_pairs={{0,10},{2,8},{4,14},{6,12},{8,2},{10,0},{12,6},{14,4},{1,11},{3,9}... | collective-permute-start | bytes 393224 | tf_op jit(solution)/shard_map/ppermute | solution.py:238
  37.2 10.9 %collective-permute-done.22.refs_6_ = bf16[64,1024]{1,0:T(8,128)(2,1)S(1)} collective-permute-done((bf16[64,1024]{1,0:T(8,128)(2,1)}, bf16[64,1024]{1,0:T(8,128)(2,1)S(1)}, u32[]{:S(2)}, u32[]{:S(2)}) %collective-permute-start.22) | collective-permute-done | bytes 131104 | tf_op jit(solution)/shard_map/ppermute | solution.py:238
  48.1 3.9 %collective-permute-done.9.refs_7_ = bf16[64,1024]{1,0:T(8,128)(2,1)S(1)} collective-permute-done((bf16[64,1024]{1,0:T(8,128)(2,1)}, bf16[64,1024]{1,0:T(8,128)(2,1)S(1)}, u32[]{:S(2)}, u32[]{:S(2)}) %collective-permute-start.9) | collective-permute-done | bytes 131104 | tf_op jit(solution)/shard_map/ppermute | solution.py:238
  51.9 1.7 %collective-permute-done.8.refs_6_ = bf16[64,1024]{1,0:T(8,128)(2,1)S(1)} collective-permute-done((bf16[64,1024]{1,0:T(8,128)(2,1)}, bf16[64,1024]{1,0:T(8,128)(2,1)S(1)}, u32[]{:S(2)}, u32[]{:S(2)}) %collective-permute-start.8) | collective-permute-done | bytes 131104 | tf_op jit(solution)/shard_map/ppermute | solution.py:238
  56.6 3.1 %shard_map.61 = (bf16[64,1024]{1,0:T(8,128)(2,1)}, bf16[64,1024]{1,0:T(8,128)(2,1)}, bf16[64,1024]{1,0:T(8,128)(2,1)}, bf16[64,1024]{1,0:T(8,128)(2,1)}, bf16[64...) custom-call(s32[8,8]{1,0:T(8,128)} %xor_bitcast_fusion.table, ...), custom_call_target="tpu_custom_call" | custom-call | bytes 2097152 | tf_op jit(solution)/shard_map/pallas_call | solution.py:129
  60.5 3.2 %shard_map.59 = (bf16[64,1024]{1,0:T(8,128)(2,1)}, bf16[64,1024]{1,0:T(8,128)(2,1)}, bf16[64,1024]{1,0:T(8,128)(2,1)}, bf16[64,1024]{1,0:T(8,128)(2,1)}, bf16[64...) custom-call(s32[8,8]{1,0:T(8,128)} %xor_bitcast_fusion.table, ...), custom_call_target="tpu_custom_call" | custom-call | bytes 2097152 | tf_op jit(solution)/shard_map/pallas_call | solution.py:129
  65.0 2.0 %collective-permute-start.11 = (bf16[64,1024]{1,0:T(8,128)(2,1)}, bf16[64,1024]{1,0:T(8,128)(2,1)S(1)}, u32[]{:S(2)}, u32[]{:S(2)}) collective-permute-start(bf16[64,1024]{1,0:T(8,128)(2,1)} %get-tuple-element.22), channel_id=1, source_target_pairs={{0,4},{2,6},{4,0},{6,2},{8,12},{10,14},{12,8},{14,10},{1,5},{3,7},... | collective-permute-start | bytes 393224 | tf_op jit(solution)/shard_map/ppermute | solution.py:238
  67.9 3.0 %collective-permute-start.13 = (bf16[64,1024]{1,0:T(8,128)(2,1)}, bf16[64,1024]{1,0:T(8,128)(2,1)S(1)}, u32[]{:S(2)}, u32[]{:S(2)}) collective-permute-start(bf16[64,1024]{1,0:T(8,128)(2,1)} %get-tuple-element.24), channel_id=1, source_target_pairs={{0,8},{2,10},{4,12},{6,14},{8,0},{10,2},{12,4},{14,6},{1,9},{3,11}... | collective-permute-start | bytes 393224 | tf_op jit(solution)/shard_map/ppermute | solution.py:238
  75.5 3.4 %collective-permute-start.26 = (bf16[64,1024]{1,0:T(8,128)(2,1)}, bf16[64,1024]{1,0:T(8,128)(2,1)S(1)}, u32[]{:S(2)}, u32[]{:S(2)}) collective-permute-start(bf16[64,1024]{1,0:T(8,128)(2,1)} %get-tuple-element.33), channel_id=1, source_target_pairs={{0,6},{2,4},{4,2},{6,0},{8,14},{10,12},{12,10},{14,8},{1,7},{3,5},... | collective-permute-start | bytes 393224 | tf_op jit(solution)/shard_map/ppermute | solution.py:238
  79.0 7.0 %collective-permute-done.13.refs_4_ = bf16[64,1024]{1,0:T(8,128)(2,1)S(1)} collective-permute-done((bf16[64,1024]{1,0:T(8,128)(2,1)}, bf16[64,1024]{1,0:T(8,128)(2,1)S(1)}, u32[]{:S(2)}, u32[]{:S(2)}) %collective-permute-start.13) | collective-permute-done | bytes 131104 | tf_op jit(solution)/shard_map/ppermute | solution.py:238
  86.0 3.8 %collective-permute-start.27 = (bf16[64,1024]{1,0:T(8,128)(2,1)}, bf16[64,1024]{1,0:T(8,128)(2,1)S(1)}, u32[]{:S(2)}, u32[]{:S(2)}) collective-permute-start(bf16[64,1024]{1,0:T(8,128)(2,1)} %get-tuple-element.34), channel_id=1, source_target_pairs={{0,8},{2,10},{4,12},{6,14},{8,0},{10,2},{12,4},{14,6},{1,9},{3,11}... | collective-permute-start | bytes 393224 | tf_op jit(solution)/shard_map/ppermute | solution.py:238
  89.7 5.3 %collective-permute-done.14.refs_5_ = bf16[64,1024]{1,0:T(8,128)(2,1)S(1)} collective-permute-done((bf16[64,1024]{1,0:T(8,128)(2,1)}, bf16[64,1024]{1,0:T(8,128)(2,1)S(1)}, u32[]{:S(2)}, u32[]{:S(2)}) %collective-permute-start.14) | collective-permute-done | bytes 131104 | tf_op jit(solution)/shard_map/ppermute | solution.py:238
  95.1 4.2 %collective-permute-start.28 = (bf16[64,1024]{1,0:T(8,128)(2,1)}, bf16[64,1024]{1,0:T(8,128)(2,1)S(1)}, u32[]{:S(2)}, u32[]{:S(2)}) collective-permute-start(bf16[64,1024]{1,0:T(8,128)(2,1)} %get-tuple-element.35), channel_id=1, source_target_pairs={{0,10},{2,8},{4,14},{6,12},{8,2},{10,0},{12,6},{14,4},{1,11},{3,9}... | collective-permute-start | bytes 393224 | tf_op jit(solution)/shard_map/ppermute | solution.py:238
  100.2 4.6 %collective-permute-done.16.refs_7_ = bf16[64,1024]{1,0:T(8,128)(2,1)S(1)} collective-permute-done((bf16[64,1024]{1,0:T(8,128)(2,1)}, bf16[64,1024]{1,0:T(8,128)(2,1)S(1)}, u32[]{:S(2)}, u32[]{:S(2)}) %collective-permute-start.16) | collective-permute-done | bytes 131104 | tf_op jit(solution)/shard_map/ppermute | solution.py:238
  104.9 3.3 %collective-permute-start.30 = (bf16[64,1024]{1,0:T(8,128)(2,1)}, bf16[64,1024]{1,0:T(8,128)(2,1)S(1)}, u32[]{:S(2)}, u32[]{:S(2)}) collective-permute-start(bf16[64,1024]{1,0:T(8,128)(2,1)} %get-tuple-element.37), channel_id=1, source_target_pairs={{0,14},{2,12},{4,10},{6,8},{8,6},{10,4},{12,2},{14,0},{1,15},{3,13... | collective-permute-start | bytes 393224 | tf_op jit(solution)/shard_map/ppermute | solution.py:238
  109.1 9.7 %shard_map.60 = (f32[512,1024]{1,0:T(8,128)S(1)}, bf16[8,512,512]{2,1,0:T(8,128)(2,1)S(1)}) custom-call(bf16[512,1024]{1,0:T(8,128)(2,1)S(1)} %copy-done.1, bf16[512,1024]{1,0:T(8,128)(2,1)S(1)} %copy-done, bf16[512,1024]{1,0:T(8,128)(2,1)S(1)} %copy-done.2, bf16[64,1024]{1,0:T(8,128)(2,1)S(1)} %copy-done.4, ...), custom_call_target="tpu_custom_call" | custom-call | flops 1610612736 | bytes 10485760 | tf_op jit(solution)/shard_map/pallas_call | solution.py:178
  118.9 4.6 %shard_map.62 = bf16[512,1024]{1,0:T(8,128)(2,1)} custom-call(bf16[8,512,512]{2,1,0:T(8,128)(2,1)S(1)} %get-tuple-element.28.w_ref, f32[512,1024]{1,0:T(8,128)S(1)} %get-tuple-element.29.own_ref, bf16[64,1024]{1,0:T(8,128)(2,1)S(1)} %copy-done.3, bf16[64,1024]{1,0:T(8,128)(2,1)S(1)} %collective-permute-done.24.refs_1_, ...), custom_call_target="tpu_custom_call" | custom-call | flops 536870912 | bytes 8388608 | tf_op jit(solution)/shard_map/pallas_call | solution.py:214
  (83 shorter events, 23.1 us)
Async XLA Ops:
  2.9 12.6 %collective-permute-start = (bf16[1,2,1024]{2,0,1:T(2,128)(2,1)S(1)}, bf16[1,2,1024]{2,0,1:T(2,128)(2,1)S(1)}, u32[]{:S(2)}, u32[]{:S(2)}) collective-permute-start(bf16[1,2,1024]{2,0,1:T(2,128)(2,1)S(1)} %copy.10), channel_id=1, source_target_pairs={{0,2},{2,0},{4,6},{6,4},{8,10},{10,8},{12,14},{14,12},{1,3},{3,1},... | collective-permute-start | bytes 12296 | tf_op jit(solution)/shard_map/ppermute | solution.py:238
  5.7 22.1 %collective-permute-start.23 = (bf16[64,1024]{1,0:T(8,128)(2,1)}, bf16[64,1024]{1,0:T(8,128)(2,1)}, u32[]{:S(2)}, u32[]{:S(2)}) collective-permute-start(bf16[64,1024]{1,0:T(8,128)(2,1)} %get-tuple-element.42), channel_id=1, source_target_pairs={{0,14},{2,12},{4,10},{6,8},{8,6},{10,4},{12,2},{14,0},{1,15},{3,13... | collective-permute-start | bytes 393224 | tf_op jit(solution)/shard_map/ppermute | solution.py:238
  8.3 20.2 %collective-permute-start.21 = (bf16[64,1024]{1,0:T(8,128)(2,1)}, bf16[64,1024]{1,0:T(8,128)(2,1)}, u32[]{:S(2)}, u32[]{:S(2)}) collective-permute-start(bf16[64,1024]{1,0:T(8,128)(2,1)} %get-tuple-element.43), channel_id=1, source_target_pairs={{0,10},{2,8},{4,14},{6,12},{8,2},{10,0},{12,6},{14,4},{1,11},{3,9}... | collective-permute-start | bytes 393224 | tf_op jit(solution)/shard_map/ppermute | solution.py:238
  9.5 20.7 %collective-permute-start.20 = (bf16[64,1024]{1,0:T(8,128)(2,1)}, bf16[64,1024]{1,0:T(8,128)(2,1)}, u32[]{:S(2)}, u32[]{:S(2)}) collective-permute-start(bf16[64,1024]{1,0:T(8,128)(2,1)} %get-tuple-element.44), channel_id=1, source_target_pairs={{0,8},{2,10},{4,12},{6,14},{8,0},{10,2},{12,4},{14,6},{1,9},{3,11}... | collective-permute-start | bytes 393224 | tf_op jit(solution)/shard_map/ppermute | solution.py:238
  11.2 20.2 %collective-permute-start.19 = (bf16[64,1024]{1,0:T(8,128)(2,1)}, bf16[64,1024]{1,0:T(8,128)(2,1)}, u32[]{:S(2)}, u32[]{:S(2)}) collective-permute-start(bf16[64,1024]{1,0:T(8,128)(2,1)} %get-tuple-element.45), channel_id=1, source_target_pairs={{0,6},{2,4},{4,2},{6,0},{8,14},{10,12},{12,10},{14,8},{1,7},{3,5},... | collective-permute-start | bytes 393224 | tf_op jit(solution)/shard_map/ppermute | solution.py:238
  27.9 9.2 %collective-permute-start.17 = (bf16[64,1024]{1,0:T(8,128)(2,1)}, bf16[64,1024]{1,0:T(8,128)(2,1)S(1)}, u32[]{:S(2)}, u32[]{:S(2)}) collective-permute-start(bf16[64,1024]{1,0:T(8,128)(2,1)} %get-tuple-element.47), channel_id=1, source_target_pairs={{0,2},{2,0},{4,6},{6,4},{8,10},{10,8},{12,14},{14,12},{1,3},{3,1},... | collective-permute-start | bytes 393224 | tf_op jit(solution)/shard_map/ppermute | solution.py:238
  28.4 19.7 %collective-permute-start.22 = (bf16[64,1024]{1,0:T(8,128)(2,1)}, bf16[64,1024]{1,0:T(8,128)(2,1)S(1)}, u32[]{:S(2)}, u32[]{:S(2)}) collective-permute-start(bf16[64,1024]{1,0:T(8,128)(2,1)} %get-tuple-element.49), channel_id=1, source_target_pairs={{0,12},{2,14},{4,8},{6,10},{8,4},{10,6},{12,0},{14,2},{1,13},{3,15... | collective-permute-start | bytes 393224 | tf_op jit(solution)/shard_map/ppermute | solution.py:238
  30.2 21.8 %collective-permute-start.9 = (bf16[64,1024]{1,0:T(8,128)(2,1)}, bf16[64,1024]{1,0:T(8,128)(2,1)S(1)}, u32[]{:S(2)}, u32[]{:S(2)}) collective-permute-start(bf16[64,1024]{1,0:T(8,128)(2,1)} %get-tuple-element.50), channel_id=1, source_target_pairs={{0,14},{2,12},{4,10},{6,8},{8,6},{10,4},{12,2},{14,0},{1,15},{3,13... | collective-permute-start | bytes 393224 | tf_op jit(solution)/shard_map/ppermute | solution.py:238
  31.4 22.3 %collective-permute-start.8 = (bf16[64,1024]{1,0:T(8,128)(2,1)}, bf16[64,1024]{1,0:T(8,128)(2,1)S(1)}, u32[]{:S(2)}, u32[]{:S(2)}) collective-permute-start(bf16[64,1024]{1,0:T(8,128)(2,1)} %get-tuple-element.51), channel_id=1, source_target_pairs={{0,12},{2,14},{4,8},{6,10},{8,4},{10,6},{12,0},{14,2},{1,13},{3,15... | collective-permute-start | bytes 393224 | tf_op jit(solution)/shard_map/ppermute | solution.py:238
  33.8 25.9 %collective-permute-start.7 = (bf16[64,1024]{1,0:T(8,128)(2,1)}, bf16[64,1024]{1,0:T(8,128)(2,1)}, u32[]{:S(2)}, u32[]{:S(2)}) collective-permute-start(bf16[64,1024]{1,0:T(8,128)(2,1)} %get-tuple-element.52), channel_id=1, source_target_pairs={{0,10},{2,8},{4,14},{6,12},{8,2},{10,0},{12,6},{14,4},{1,11},{3,9}... | collective-permute-start | bytes 393224 | tf_op jit(solution)/shard_map/ppermute | solution.py:238
  37.1 23.3 %collective-permute-start.6 = (bf16[64,1024]{1,0:T(8,128)(2,1)S(1)}, bf16[64,1024]{1,0:T(8,128)(2,1)}, u32[]{:S(2)}, u32[]{:S(2)}) collective-permute-start(bf16[64,1024]{1,0:T(8,128)(2,1)S(1)} %get-tuple-element.53), channel_id=1, source_target_pairs={{0,8},{2,10},{4,12},{6,14},{8,0},{10,2},{12,4},{14,6},{1,9},{3,11}... | collective-permute-start | bytes 393224 | tf_op jit(solution)/shard_map/ppermute | solution.py:238
  48.1 12.4 %collective-permute-start.5 = (bf16[64,1024]{1,0:T(8,128)(2,1)}, bf16[64,1024]{1,0:T(8,128)(2,1)}, u32[]{:S(2)}, u32[]{:S(2)}) collective-permute-start(bf16[64,1024]{1,0:T(8,128)(2,1)} %get-tuple-element.54), channel_id=1, source_target_pairs={{0,6},{2,4},{4,2},{6,0},{8,14},{10,12},{12,10},{14,8},{1,7},{3,5},... | collective-permute-start | bytes 393224 | tf_op jit(solution)/shard_map/ppermute | solution.py:238
  51.9 8.5 %collective-permute-start.4 = (bf16[64,1024]{1,0:T(8,128)(2,1)}, bf16[64,1024]{1,0:T(8,128)(2,1)}, u32[]{:S(2)}, u32[]{:S(2)}) collective-permute-start(bf16[64,1024]{1,0:T(8,128)(2,1)} %get-tuple-element.55), channel_id=1, source_target_pairs={{0,4},{2,6},{4,0},{6,2},{8,12},{10,14},{12,8},{14,10},{1,5},{3,7},... | collective-permute-start | bytes 393224 | tf_op jit(solution)/shard_map/ppermute | solution.py:238
  59.7 8.2 %collective-permute-start.24 = (bf16[64,1024]{1,0:T(8,128)(2,1)}, bf16[64,1024]{1,0:T(8,128)(2,1)S(1)}, u32[]{:S(2)}, u32[]{:S(2)}) collective-permute-start(bf16[64,1024]{1,0:T(8,128)(2,1)} %get-tuple-element.31), channel_id=1, source_target_pairs={{0,2},{2,0},{4,6},{6,4},{8,10},{10,8},{12,14},{14,12},{1,3},{3,1},... | collective-permute-start | bytes 393224 | tf_op jit(solution)/shard_map/ppermute | solution.py:238
  60.4 10.5 %collective-permute-start.25 = (bf16[64,1024]{1,0:T(8,128)(2,1)}, bf16[64,1024]{1,0:T(8,128)(2,1)S(1)}, u32[]{:S(2)}, u32[]{:S(2)}) collective-permute-start(bf16[64,1024]{1,0:T(8,128)(2,1)} %get-tuple-element.32), channel_id=1, source_target_pairs={{0,4},{2,6},{4,0},{6,2},{8,12},{10,14},{12,8},{14,10},{1,5},{3,7},... | collective-permute-start | bytes 393224 | tf_op jit(solution)/shard_map/ppermute | solution.py:238
  67.9 18.1 %collective-permute-start.13 = (bf16[64,1024]{1,0:T(8,128)(2,1)}, bf16[64,1024]{1,0:T(8,128)(2,1)S(1)}, u32[]{:S(2)}, u32[]{:S(2)}) collective-permute-start(bf16[64,1024]{1,0:T(8,128)(2,1)} %get-tuple-element.24), channel_id=1, source_target_pairs={{0,8},{2,10},{4,12},{6,14},{8,0},{10,2},{12,4},{14,6},{1,9},{3,11}... | collective-permute-start | bytes 393224 | tf_op jit(solution)/shard_map/ppermute | solution.py:238
  70.9 24.2 %collective-permute-start.14 = (bf16[64,1024]{1,0:T(8,128)(2,1)}, bf16[64,1024]{1,0:T(8,128)(2,1)S(1)}, u32[]{:S(2)}, u32[]{:S(2)}) collective-permute-start(bf16[64,1024]{1,0:T(8,128)(2,1)} %get-tuple-element.25), channel_id=1, source_target_pairs={{0,10},{2,8},{4,14},{6,12},{8,2},{10,0},{12,6},{14,4},{1,11},{3,9}... | collective-permute-start | bytes 393224 | tf_op jit(solution)/shard_map/ppermute | solution.py:238
  71.7 27.5 %collective-permute-start.15 = (bf16[64,1024]{1,0:T(8,128)(2,1)}, bf16[64,1024]{1,0:T(8,128)(2,1)S(1)}, u32[]{:S(2)}, u32[]{:S(2)}) collective-permute-start(bf16[64,1024]{1,0:T(8,128)(2,1)} %get-tuple-element.26), channel_id=1, source_target_pairs={{0,12},{2,14},{4,8},{6,10},{8,4},{10,6},{12,0},{14,2},{1,13},{3,15... | collective-permute-start | bytes 393224 | tf_op jit(solution)/shard_map/ppermute | solution.py:238
  73.1 31.8 %collective-permute-start.16 = (bf16[64,1024]{1,0:T(8,128)(2,1)}, bf16[64,1024]{1,0:T(8,128)(2,1)S(1)}, u32[]{:S(2)}, u32[]{:S(2)}) collective-permute-start(bf16[64,1024]{1,0:T(8,128)(2,1)} %get-tuple-element.27), channel_id=1, source_target_pairs={{0,14},{2,12},{4,10},{6,8},{8,6},{10,4},{12,2},{14,0},{1,15},{3,13... | collective-permute-start | bytes 393224 | tf_op jit(solution)/shard_map/ppermute | solution.py:238
  75.5 43.3 %collective-permute-start.26 = (bf16[64,1024]{1,0:T(8,128)(2,1)}, bf16[64,1024]{1,0:T(8,128)(2,1)S(1)}, u32[]{:S(2)}, u32[]{:S(2)}) collective-permute-start(bf16[64,1024]{1,0:T(8,128)(2,1)} %get-tuple-element.33), channel_id=1, source_target_pairs={{0,6},{2,4},{4,2},{6,0},{8,14},{10,12},{12,10},{14,8},{1,7},{3,5},... | collective-permute-start | bytes 393224 | tf_op jit(solution)/shard_map/ppermute | solution.py:238
  86.0 32.9 %collective-permute-start.27 = (bf16[64,1024]{1,0:T(8,128)(2,1)}, bf16[64,1024]{1,0:T(8,128)(2,1)S(1)}, u32[]{:S(2)}, u32[]{:S(2)}) collective-permute-start(bf16[64,1024]{1,0:T(8,128)(2,1)} %get-tuple-element.34), channel_id=1, source_target_pairs={{0,8},{2,10},{4,12},{6,14},{8,0},{10,2},{12,4},{14,6},{1,9},{3,11}... | collective-permute-start | bytes 393224 | tf_op jit(solution)/shard_map/ppermute | solution.py:238
  95.1 23.8 %collective-permute-start.28 = (bf16[64,1024]{1,0:T(8,128)(2,1)}, bf16[64,1024]{1,0:T(8,128)(2,1)S(1)}, u32[]{:S(2)}, u32[]{:S(2)}) collective-permute-start(bf16[64,1024]{1,0:T(8,128)(2,1)} %get-tuple-element.35), channel_id=1, source_target_pairs={{0,10},{2,8},{4,14},{6,12},{8,2},{10,0},{12,6},{14,4},{1,11},{3,9}... | collective-permute-start | bytes 393224 | tf_op jit(solution)/shard_map/ppermute | solution.py:238
  99.2 19.6 %collective-permute-start.29 = (bf16[64,1024]{1,0:T(8,128)(2,1)}, bf16[64,1024]{1,0:T(8,128)(2,1)S(1)}, u32[]{:S(2)}, u32[]{:S(2)}) collective-permute-start(bf16[64,1024]{1,0:T(8,128)(2,1)} %get-tuple-element.36), channel_id=1, source_target_pairs={{0,12},{2,14},{4,8},{6,10},{8,4},{10,6},{12,0},{14,2},{1,13},{3,15... | collective-permute-start | bytes 393224 | tf_op jit(solution)/shard_map/ppermute | solution.py:238
  104.9 14.0 %collective-permute-start.30 = (bf16[64,1024]{1,0:T(8,128)(2,1)}, bf16[64,1024]{1,0:T(8,128)(2,1)S(1)}, u32[]{:S(2)}, u32[]{:S(2)}) collective-permute-start(bf16[64,1024]{1,0:T(8,128)(2,1)} %get-tuple-element.37), channel_id=1, source_target_pairs={{0,14},{2,12},{4,10},{6,8},{8,6},{10,4},{12,2},{14,0},{1,15},{3,13... | collective-permute-start | bytes 393224 | tf_op jit(solution)/shard_map/ppermute | solution.py:238
  (17 other events, 231.1 us)

commit v2 on v1

--- a/solution.py
+++ b/solution.py
@@ -112,24 +112,25 @@
     return (attended, sort_logits)
 
 
-def pick_kernel(members, heads, table, *refs):
+def pick_kernel(members, heads, me_ref, chosen, *refs):
     pieces, outs, held = refs[:members], refs[members : 2 * members], refs[2 * members]
+    me = me_ref[0]
     for e in range(members):
         held[e] = pieces[e][...]
     for d in range(members):
         for h in range(heads):
             cols = pl.ds(h * DH, DH)
-            outs[d][:, cols] = held[table[d, h], :, cols]
-
-
-def pick_pieces(table, pieces):
+            outs[d][:, cols] = held[me ^ chosen[me ^ d, h], :, cols]
+
+
+def pick_pieces(me, chosen, pieces):
     members = len(pieces)
     rows, width = pieces[0].shape
-    spec = pl.BlockSpec((rows, width), lambda i, t: (0, 0))
+    spec = pl.BlockSpec((rows, width), lambda i, m, t: (0, 0))
     return pl.pallas_call(
         functools.partial(pick_kernel, members, width // DH),
         grid_spec=pltpu.PrefetchScalarGridSpec(
-            num_scalar_prefetch=1,
+            num_scalar_prefetch=2,
             grid=(1,),
             in_specs=[spec] * members,
             out_specs=[spec] * members,
@@ -139,59 +140,89 @@
         cost_estimate=pl.CostEstimate(
             flops=0, transcendentals=0, bytes_accessed=4 * members * rows * width
         ),
-    )(table, *pieces)
-
-
-def scores_kernel(members, q_ref, k_ref, v_ref, *refs):
+    )(me, chosen, *pieces)
+
+
+def softmax_part(q, keys):
+    s = lax.dot_general(q, keys, (((1,), (1,)), ((), ())), preferred_element_type=F32) * (
+        1.0 / math.sqrt(DH)
+    )
+    top = jnp.max(s, axis=1, keepdims=True)
+    w = jnp.exp(s - top).astype(BF16)
+    return top, w, jnp.sum(w.astype(F32), axis=1, keepdims=True)
+
+
+def own_kernel(q_ref, k_ref, v_ref, sum_ref, top_ref, total_ref):
+    top, w, total = softmax_part(q_ref[...], k_ref[...])
+    sum_ref[...] = jnp.dot(w, v_ref[...], preferred_element_type=F32)
+    top_ref[0] = top
+    total_ref[0] = total
+
+
+def own_part(q, k, v):
+    tok, width = q.shape
+    heads = width // DH
+    whole = pl.BlockSpec((tok, DH), lambda h: (0, h))
+    column = pl.BlockSpec((1, tok, 1), lambda h: (h, 0, 0))
+    return pl.pallas_call(
+        own_kernel,
+        grid=(heads,),
+        in_specs=[whole] * 3,
+        out_specs=[whole, column, column],
+        out_shape=[
+            jax.ShapeDtypeStruct((tok, width), F32),
+            jax.ShapeDtypeStruct((heads, tok, 1), F32),
+            jax.ShapeDtypeStruct((heads, tok, 1), F32),
+        ],
+        compiler_params=pltpu.CompilerParams(vmem_limit_bytes=32 << 20),
+        cost_estimate=pl.CostEstimate(
+            flops=4 * tok * BS * width,
+            transcendentals=heads * tok * BS,
+            bytes_accessed=10 * tok * width,
+        ),
+    )(q, k, v)
+
+
+def scores_kernel(members, q_ref, sum_ref, top_ref, total_ref, *refs):
     far_k, (own_ref, w_ref, kf_ref) = refs[:members], refs[members:]
     rows = far_k[0].shape[0]
     for e in range(members):
         kf_ref[pl.ds(e * rows, rows), :] = far_k[e][...]
-    q = q_ref[...]
-
-    def part(keys):
-        s = lax.dot_general(
-            q, keys, (((1,), (1,)), ((), ())), preferred_element_type=F32
-        ) * (1.0 / math.sqrt(DH))
-        top = jnp.max(s, axis=1, keepdims=True)
-        w = jnp.exp(s - top).astype(BF16)
-        return top, w, jnp.sum(w.astype(F32), axis=1, keepdims=True)
-
-    own_max, own_w, own_total = part(k_ref[...])
-    own_sum = jnp.dot(own_w, v_ref[...], preferred_element_type=F32)
-    far_max, far_w, far_total = part(kf_ref[...])
+    far_max, far_w, far_total = softmax_part(q_ref[...], kf_ref[...])
+    own_max = top_ref[0]
     joint = jnp.maximum(own_max, far_max)
     own_e = jnp.exp(own_max - joint)
     far_e = jnp.exp(far_max - joint)
-    inverse = 1.0 / (own_e * own_total + far_e * far_total)
-    own_ref[...] = own_sum * (own_e * inverse)
+    inverse = 1.0 / (own_e * total_ref[0] + far_e * far_total)
+    own_ref[...] = sum_ref[...] * (own_e * inverse)
     w_ref[0] = (far_w.astype(F32) * (far_e * inverse)).astype(BF16)
 
 
-def score_parts(q, k, v, far_k):
+def score_parts(q, own, far_k):
     members = len(far_k)
     tok, width = q.shape
     heads = width // DH
     rows = far_k[0].shape[0]
     whole = pl.BlockSpec((tok, DH), lambda h: (0, h))
+    column = pl.BlockSpec((1, tok, 1), lambda h: (h, 0, 0))
     piece = pl.BlockSpec((rows, DH), lambda h: (0, h))
     return pl.pallas_call(
         functools.partial(scores_kernel, members),
         grid=(heads,),
-        in_specs=[whole] * 3 + [piece] * members,
+        in_specs=[whole, whole, column, column] + [piece] * members,
         out_specs=[whole, pl.BlockSpec((1, tok, BS), lambda h: (h, 0, 0))],
         out_shape=[
             jax.ShapeDtypeStruct((tok, width), F32),
             jax.ShapeDtypeStruct((heads, tok, BS), BF16),
         ],
         scratch_shapes=[pltpu.VMEM((BS, DH), BF16)],
-        compiler_params=pltpu.CompilerParams(vmem_limit_bytes=40 << 20),
+        compiler_params=pltpu.CompilerParams(vmem_limit_bytes=32 << 20),
         cost_estimate=pl.CostEstimate(
-            flops=6 * tok * BS * width,
-            transcendentals=2 * heads * tok * BS,
+            flops=2 * tok * BS * width,
+            transcendentals=heads * tok * BS,
             bytes_accessed=12 * tok * width + 2 * heads * tok * BS,
         ),
-    )(q, k, v, *far_k)
+    )(q, *own, *far_k)
 
 
 def finish_kernel(members, w_ref, own_ref, *refs):
@@ -218,13 +249,20 @@
         out_specs=whole,
         out_shape=jax.ShapeDtypeStruct((tok, width), BF16),
         scratch_shapes=[pltpu.VMEM((BS, DH), BF16)],
-        compiler_params=pltpu.CompilerParams(vmem_limit_bytes=40 << 20),
+        compiler_params=pltpu.CompilerParams(vmem_limit_bytes=32 << 20),
         cost_estimate=pl.CostEstimate(
             flops=2 * tok * BS * width,
             transcendentals=0,
             bytes_accessed=8 * tok * width + 2 * heads * tok * BS,
         ),
     )(w, own, *far_v)
+
+
+def after(x, *earlier):
+    return lax.optimization_barrier((x, *earlier))[0]
+
+
+IN_FLIGHT = 5
 
 
 def power_of_two(query_rows, key_rows, value_rows, selection):
@@ -233,45 +271,50 @@
     tok, width = query_rows.shape
     heads = width // DH
     rows = BS // members
-
-    def send(x, d):
-        return lax.ppermute(x, "context", [(i, i ^ d) for i in range(members)])
-
     order = sorted(range(1, members), reverse=True)
-
-    def exchange(chunks):
-        got = list(chunks)
+    arrived = []
+
+    def exchange(take):
+        got = [None] * members
         for d in order:
-            got[d] = send(chunks[d], d)
+            earlier = arrived[-IN_FLIGHT:-IN_FLIGHT + 1] if len(arrived) >= IN_FLIGHT else []
+            got[d] = lax.ppermute(
+                take(d, *earlier), "context", [(i, i ^ d) for i in range(members)]
+            )
+            arrived.append(got[d])
+        got[0] = take(0)
         return got
 
-    def split(array):
-        return [array[d * rows : (d + 1) * rows] for d in range(members)]
+    def rows_of(array):
+        return lambda d, *earlier: after(array, *earlier)[d * rows : (d + 1) * rows]
+
+    def piece_of(pieces):
+        return lambda d, *earlier: after(pieces[d], *earlier)
 
     def pooled(array):
         return (jnp.sum(array, axis=0, dtype=F32) / math.sqrt(BS)).astype(BF16)
 
     chosen = jnp.pad(selection[:, 0].astype(BF16), (0, width - heads))
     shared = jnp.stack([pooled(key_rows), chosen])[None]
-    d = 1
-    while d < members:
-        shared = jnp.concatenate([shared, send(shared, d)], axis=0)
-        d *= 2
-    table = me ^ shared[:, 1, :heads].astype(jnp.int32)
-
-    held_k = exchange(split(key_rows))
-    held_v = exchange(split(value_rows))
-    far_k = exchange(pick_pieces(table, held_k))
-    far_v = exchange(pick_pieces(table, held_v))
-
-    own, w = score_parts(query_rows, key_rows, value_rows, far_k)
-    attended = finish(w, own, far_v)
-
-    pooled_k = shared[:, 0][me ^ jnp.arange(members)]
+    shared = lax.all_to_all(
+        jnp.broadcast_to(shared, (members, 2, width)), "context", 0, 0, tiled=True
+    )
+    chosen = shared[:, 1, :heads].astype(jnp.int32)
+    here = me.astype(jnp.int32)[None]
+
+    held_k = exchange(rows_of(key_rows))
+    held_v = exchange(rows_of(value_rows))
+    own = own_part(after(query_rows, held_k[order[0]]), key_rows, value_rows)
+    far_k = exchange(piece_of(pick_pieces(here, chosen, held_k)))
+    far_v = exchange(piece_of(pick_pieces(here, chosen, held_v)))
+
+    scaled, w = score_parts(query_rows, own, far_k)
+    attended = finish(w, scaled, far_v)
+
     sort_logits = jnp.einsum(
         "hd,chd->hc",
         pooled(query_rows).reshape(heads, DH),
-        pooled_k.reshape(members, heads, DH),
+        shared[:, 0].reshape(members, heads, DH),
         preferred_element_type=F32,
     ) / math.sqrt(DH)
     return attended, sort_logits.reshape(heads, 1, members)

time: 124 us -> 124 us (level)
  the two profiles are of different devices: /device:TPU:14 before, /device:TPU:0 now
where the time goes in v2:
time: 124 us
  starting transfers between devices  70.1 us (57%)
  Pallas kernels  28.3 us (23%)
  waiting for transfers between devices  11.7 us (9%)
  local copies, waits for them, and re-layouts  8.84 us (7%)
  other arithmetic  2.86 us (2%)
  matrix products  1.39 us (1%)
    ppermute x28, starting transfers between devices, exchange(): lax.ppermute(take(d, *earlier), 'context', [(i, i ^ d) for i in range(mem...  65.9 us
    ppermute x28, waiting for transfers between devices, exchange(): lax.ppermute(take(d, *earlier), 'context', [(i, i ^ d) for i in range(mem...  11.7 us
    pallas_call x1, Pallas kernels, score_parts(): pl.pallas_call(functools.partial(scores_kernel, members), grid=(heads,),...  9.71 us
    pallas_call x1, Pallas kernels, own_part(): pl.pallas_call(own_kernel, grid=(heads,), in_specs=[whole] * 3, out_specs...  7.79 us
    slice x11, local copies, waits for them, and re-layouts, rows_of(): return lambda d, *earlier: after(array, *earlier)[d * rows:(d + 1) * rows]  7.44 us
    pallas_call x2, Pallas kernels, pick_pieces(): pl.pallas_call(functools.partial(pick_kernel, members, width // DH), grid...  6.2 us
    pallas_call x1, Pallas kernels, finish(): pl.pallas_call(functools.partial(finish_kernel, members), grid=(heads,),...  4.62 us
    all_to_all x1, starting transfers between devices, power_of_two(): lax.all_to_all(jnp.broadcast_to(shared, (members, 2, width)), 'context',...  4.2 us
  transfers between devices with their start and end apart: 29, of which 5 were waited for; matrix products, arithmetic and copies ran while one was open for 8% of the time, Pallas kernels for 19%

profile of v2, /device:TPU:0, one launch (start us, length us, event | category | flops | bytes accessed | tf_op | source)
XLA Modules:
  0.0 124.0 jit_solution(7920608409468311906)
XLA Ops:
  0.7 2.1 %fusion.5 = (bf16[64,1024]{1,0:T(8,128)(2,1)}, bf16[64,1024]{1,0:T(8,128)(2,1)S(1)}, bf16[64,1024]{1,0:T(8,128)(2,1)S(1)}, bf16[64,1024]{1,0:T(8,128)(2,1)}, bf1...) fusion(bf16[512,1024]{1,0:T(8,128)(2,1)} %k_ref.1), kind=kLoop, calls=%fused_computation.14 | loop fusion | bytes 1572864 | tf_op jit(solution)/shard_map/slice | solution.py:289
  2.8 6.0 %collective-permute-start = (bf16[64,1024]{1,0:T(8,128)(2,1)}, bf16[64,1024]{1,0:T(8,128)(2,1)}, u32[]{:S(2)}, u32[]{:S(2)}) collective-permute-start(bf16[64,1024]{1,0:T(8,128)(2,1)} %get-tuple-element.103), channel_id=1, source_target_pairs={{0,14},{2,12},{4,10},{6,8},{8,6},{10,4},{12,2},{14,0},{1,15},{3,13... | collective-permute-start | bytes 393224 | tf_op jit(solution)/shard_map/ppermute | solution.py:281
  9.0 4.1 %collective-permute-start.5 = (bf16[64,1024]{1,0:T(8,128)(2,1)S(1)}, bf16[64,1024]{1,0:T(8,128)(2,1)}, u32[]{:S(2)}, u32[]{:S(2)}) collective-permute-start(bf16[64,1024]{1,0:T(8,128)(2,1)S(1)} %get-tuple-element.99), channel_id=1, source_target_pairs={{0,8},{2,10},{4,12},{6,14},{8,0},{10,2},{12,4},{14,6},{1,9},{3,11}... | collective-permute-start | bytes 393224 | tf_op jit(solution)/shard_map/ppermute | solution.py:281
  15.0 4.2 %all-to-all-start = ((bf16[8,2,1024]{2,1,0:T(2,128)(2,1)}), bf16[8,2,1024]{2,1,0:T(2,128)(2,1)S(1)}, u32[]{:S(2)}, u32[]{:S(2)}) async-start(bf16[8,2,1024]{2,1,0:T(2,128)(2,1)} %broadcast_in_dim.10), calls=%async_computation | async-start | bytes 65536 | tf_op jit(solution)/shard_map/all_to_all | solution.py:299
  20.0 2.0 %collective-permute-start.3 = (bf16[64,1024]{1,0:T(8,128)(2,1)}, bf16[64,1024]{1,0:T(8,128)(2,1)}, u32[]{:S(2)}, u32[]{:S(2)}) collective-permute-start(bf16[64,1024]{1,0:T(8,128)(2,1)} %slice.59), channel_id=1, source_target_pairs={{0,4},{2,6},{4,0},{6,2},{8,12},{10,14},{12,8},{14,10},{1,5},{3,7},... | collective-permute-start | bytes 393224 | tf_op jit(solution)/shard_map/ppermute | solution.py:281
  24.2 7.8 %collective-permute-done.6.refs_5_ = bf16[64,1024]{1,0:T(8,128)(2,1)} collective-permute-done((bf16[64,1024]{1,0:T(8,128)(2,1)}, bf16[64,1024]{1,0:T(8,128)(2,1)}, u32[]{:S(2)}, u32[]{:S(2)}) %collective-permute-start.6) | collective-permute-done | bytes 131104 | tf_op jit(solution)/shard_map/ppermute | solution.py:281
  32.6 3.4 %collective-permute-start.16 = (bf16[64,1024]{1,0:T(8,128)(2,1)}, bf16[64,1024]{1,0:T(8,128)(2,1)}, u32[]{:S(2)}, u32[]{:S(2)}) collective-permute-start(bf16[64,1024]{1,0:T(8,128)(2,1)} %slice.67), channel_id=1, source_target_pairs={{0,14},{2,12},{4,10},{6,8},{8,6},{10,4},{12,2},{14,0},{1,15},{3,13... | collective-permute-start | bytes 393224 | tf_op jit(solution)/shard_map/ppermute | solution.py:281
  40.1 2.0 %collective-permute-start.7 = (bf16[64,1024]{1,0:T(8,128)(2,1)}, bf16[64,1024]{1,0:T(8,128)(2,1)}, u32[]{:S(2)}, u32[]{:S(2)}) collective-permute-start(bf16[64,1024]{1,0:T(8,128)(2,1)} %slice.63), channel_id=1, source_target_pairs={{0,8},{2,10},{4,12},{6,14},{8,0},{10,2},{12,4},{14,6},{1,9},{3,11}... | collective-permute-start | bytes 393224 | tf_op jit(solution)/shard_map/ppermute | solution.py:281
  42.7 7.7 %collective-permute-start.17 = (bf16[64,1024]{1,0:T(8,128)(2,1)}, bf16[64,1024]{1,0:T(8,128)(2,1)}, u32[]{:S(2)}, u32[]{:S(2)}) collective-permute-start(bf16[64,1024]{1,0:T(8,128)(2,1)} %slice.68), channel_id=1, source_target_pairs={{0,4},{2,6},{4,0},{6,2},{8,12},{10,14},{12,8},{14,10},{1,5},{3,7},... | collective-permute-start | bytes 393224 | tf_op jit(solution)/shard_map/ppermute | solution.py:281
  51.8 3.1 %shard_map.60 = (bf16[64,1024]{1,0:T(8,128)(2,1)}, bf16[64,1024]{1,0:T(8,128)(2,1)}, bf16[64,1024]{1,0:T(8,128)(2,1)}, bf16[64,1024]{1,0:T(8,128)(2,1)}, bf16[64...) custom-call(s32[1]{0:T(128)} %bitcast.me_ref, ...), custom_call_target="tpu_custom_call" | custom-call | bytes 2097152 | tf_op jit(solution)/shard_map/pallas_call | solution.py:130
  56.5 2.0 %collective-permute-done.7.refs_4_ = bf16[64,1024]{1,0:T(8,128)(2,1)} collective-permute-done((bf16[64,1024]{1,0:T(8,128)(2,1)}, bf16[64,1024]{1,0:T(8,128)(2,1)}, u32[]{:S(2)}, u32[]{:S(2)}) %collective-permute-start.7) | collective-permute-done | bytes 131104 | tf_op jit(solution)/shard_map/ppermute | solution.py:281
  58.5 1.8 %collective-permute-start.8 = (bf16[64,1024]{1,0:T(8,128)(2,1)}, bf16[64,1024]{1,0:T(8,128)(2,1)S(1)}, u32[]{:S(2)}, u32[]{:S(2)}) collective-permute-start(bf16[64,1024]{1,0:T(8,128)(2,1)} %get-tuple-element.57), channel_id=1, source_target_pairs={{0,12},{2,14},{4,8},{6,10},{8,4},{10,6},{12,0},{14,2},{1,13},{3,15... | collective-permute-start | bytes 393224 | tf_op jit(solution)/shard_map/ppermute | solution.py:281
  60.5 3.7 %collective-permute-start.20 = (bf16[64,1024]{1,0:T(8,128)(2,1)}, bf16[64,1024]{1,0:T(8,128)(2,1)}, u32[]{:S(2)}, u32[]{:S(2)}) collective-permute-start(bf16[64,1024]{1,0:T(8,128)(2,1)} %get-tuple-element.74), channel_id=1, source_target_pairs={{0,10},{2,8},{4,14},{6,12},{8,2},{10,0},{12,6},{14,4},{1,11},{3,9}... | collective-permute-start | bytes 393224 | tf_op jit(solution)/shard_map/ppermute | solution.py:281
  65.5 7.2 %collective-permute-start.12 = (bf16[64,1024]{1,0:T(8,128)(2,1)}, bf16[64,1024]{1,0:T(8,128)(2,1)}, u32[]{:S(2)}, u32[]{:S(2)}) collective-permute-start(bf16[64,1024]{1,0:T(8,128)(2,1)} %get-tuple-element.63), channel_id=1, source_target_pairs={{0,4},{2,6},{4,0},{6,2},{8,12},{10,14},{12,8},{14,10},{1,5},{3,7},... | collective-permute-start | bytes 393224 | tf_op jit(solution)/shard_map/ppermute | solution.py:281
  73.3 2.0 %collective-permute-start.15 = (bf16[64,1024]{1,0:T(8,128)(2,1)}, bf16[64,1024]{1,0:T(8,128)(2,1)}, u32[]{:S(2)}, u32[]{:S(2)}) collective-permute-start(bf16[64,1024]{1,0:T(8,128)(2,1)} %get-tuple-element.67), channel_id=1, source_target_pairs={{0,6},{2,4},{4,2},{6,0},{8,14},{10,12},{12,10},{14,8},{1,7},{3,5},... | collective-permute-start | bytes 393224 | tf_op jit(solution)/shard_map/ppermute | solution.py:281
  75.3 3.1 %shard_map.62 = (bf16[64,1024]{1,0:T(8,128)(2,1)}, bf16[64,1024]{1,0:T(8,128)(2,1)}, bf16[64,1024]{1,0:T(8,128)(2,1)}, bf16[64,1024]{1,0:T(8,128)(2,1)}, bf16[64...) custom-call(s32[1]{0:T(128)} %bitcast.me_ref, ...), custom_call_target="tpu_custom_call" | custom-call | bytes 2097152 | tf_op jit(solution)/shard_map/pallas_call | solution.py:130
  80.3 2.5 %collective-permute-start.23 = (bf16[64,1024]{1,0:T(8,128)(2,1)}, bf16[64,1024]{1,0:T(8,128)(2,1)S(1)}, u32[]{:S(2)}, u32[]{:S(2)}) collective-permute-start(bf16[64,1024]{1,0:T(8,128)(2,1)} %get-tuple-element.84), channel_id=1, source_target_pairs={{0,14},{2,12},{4,10},{6,8},{8,6},{10,4},{12,2},{14,0},{1,15},{3,13... | collective-permute-start | bytes 393224 | tf_op jit(solution)/shard_map/ppermute | solution.py:281
  82.8 1.6 %collective-permute-start.21 = (bf16[64,1024]{1,0:T(8,128)(2,1)}, bf16[64,1024]{1,0:T(8,128)(2,1)S(1)}, u32[]{:S(2)}, u32[]{:S(2)}) collective-permute-start(bf16[64,1024]{1,0:T(8,128)(2,1)} %get-tuple-element.80), channel_id=1, source_target_pairs={{0,12},{2,14},{4,8},{6,10},{8,4},{10,6},{12,0},{14,2},{1,13},{3,15... | collective-permute-start | bytes 393224 | tf_op jit(solution)/shard_map/ppermute | solution.py:281
  85.6 3.6 %collective-permute-start.27 = (bf16[64,1024]{1,0:T(8,128)(2,1)}, bf16[64,1024]{1,0:T(8,128)(2,1)S(1)}, u32[]{:S(2)}, u32[]{:S(2)}) collective-permute-start(bf16[64,1024]{1,0:T(8,128)(2,1)} %get-tuple-element.91), channel_id=1, source_target_pairs={{0,10},{2,8},{4,14},{6,12},{8,2},{10,0},{12,6},{14,4},{1,11},{3,9}... | collective-permute-start | bytes 393224 | tf_op jit(solution)/shard_map/ppermute | solution.py:281
  89.7 10.1 %collective-permute-start.24 = (bf16[64,1024]{1,0:T(8,128)(2,1)}, bf16[64,1024]{1,0:T(8,128)(2,1)S(1)}, u32[]{:S(2)}, u32[]{:S(2)}) collective-permute-start(bf16[64,1024]{1,0:T(8,128)(2,1)} %get-tuple-element.85), channel_id=1, source_target_pairs={{0,4},{2,6},{4,0},{6,2},{8,12},{10,14},{12,8},{14,10},{1,5},{3,7},... | collective-permute-start | bytes 393224 | tf_op jit(solution)/shard_map/ppermute | solution.py:281
  99.7 2.1 %collective-permute-start.25 = (bf16[64,1024]{1,0:T(8,128)(2,1)}, bf16[64,1024]{1,0:T(8,128)(2,1)S(1)}, u32[]{:S(2)}, u32[]{:S(2)}) collective-permute-start(bf16[64,1024]{1,0:T(8,128)(2,1)} %get-tuple-element.87), channel_id=1, source_target_pairs={{0,6},{2,4},{4,2},{6,0},{8,14},{10,12},{12,10},{14,8},{1,7},{3,5},... | collective-permute-start | bytes 393224 | tf_op jit(solution)/shard_map/ppermute | solution.py:281
  101.8 7.8 %shard_map.59 = (f32[512,1024]{1,0:T(8,128)S(1)}, f32[8,512,1]{2,1,0:T(8,128)S(1)}, f32[8,512,1]{2,1,0:T(8,128)S(1)}) custom-call(bf16[512,1024]{1,0:T(8,128)(2,1)S(1)} %copy-done.1, bf16[512,1024]{1,0:T(8,128)(2,1)S(1)} %copy-done, bf16[512,1024]{1,0:T(8,128)(2,1)S(1)} %copy-done.2), custom_call_target="tpu_custom_call" | custom-call | flops 1073741824 | bytes 5242880 | tf_op jit(solution)/shard_map/pallas_call | solution.py:167
  109.6 9.7 %shard_map.61 = (f32[512,1024]{1,0:T(8,128)S(1)}, bf16[8,512,512]{2,1,0:T(8,128)(2,1)S(1)}) custom-call(bf16[512,1024]{1,0:T(8,128)(2,1)S(1)} %copy-done.1, f32[512,1024]{1,0:T(8,128)S(1)} %get-tuple-element.48.sum_ref, f32[8,512,1]{2,1,0:T(8,128)S(1)} %get-tuple-element.49.top_ref, f32[8,512,1]{2,1,0:T(8,128)S(1)} %get-tuple-element.50.total_ref, ...), custom_call_target="tpu_custom_call" | custom-call | flops 536870912 | bytes 10485760 | tf_op jit(solution)/shard_map/pallas_call | solution.py:209
  119.4 4.6 %shard_map.63 = bf16[512,1024]{1,0:T(8,128)(2,1)} custom-call(bf16[8,512,512]{2,1,0:T(8,128)(2,1)S(1)} %get-tuple-element.75.w_ref, f32[512,1024]{1,0:T(8,128)S(1)} %get-tuple-element.76.own_ref, bf16[64,1024]{1,0:T(8,128)(2,1)S(1)} %copy-done.4, bf16[64,1024]{1,0:T(8,128)(2,1)S(1)} %collective-permute-done.22.refs_1_, ...), custom_call_target="tpu_custom_call" | custom-call | flops 536870912 | bytes 8388608 | tf_op jit(solution)/shard_map/pallas_call | solution.py:245
  (79 shorter events, 19.1 us)
Async XLA Ops:
  2.8 16.6 %collective-permute-start = (bf16[64,1024]{1,0:T(8,128)(2,1)}, bf16[64,1024]{1,0:T(8,128)(2,1)}, u32[]{:S(2)}, u32[]{:S(2)}) collective-permute-start(bf16[64,1024]{1,0:T(8,128)(2,1)} %get-tuple-element.103), channel_id=1, source_target_pairs={{0,14},{2,12},{4,10},{6,8},{8,6},{10,4},{12,2},{14,0},{1,15},{3,13... | collective-permute-start | bytes 393224 | tf_op jit(solution)/shard_map/ppermute | solution.py:281
  8.8 13.3 %collective-permute-start.1 = (bf16[64,1024]{1,0:T(8,128)(2,1)}, bf16[64,1024]{1,0:T(8,128)(2,1)}, u32[]{:S(2)}, u32[]{:S(2)}) collective-permute-start(bf16[64,1024]{1,0:T(8,128)(2,1)} %get-tuple-element.101), channel_id=1, source_target_pairs={{0,12},{2,14},{4,8},{6,10},{8,4},{10,6},{12,0},{14,2},{1,13},{3,15... | collective-permute-start | bytes 393224 | tf_op jit(solution)/shard_map/ppermute | solution.py:281
  9.0 28.3 %collective-permute-start.4 = (bf16[64,1024]{1,0:T(8,128)(2,1)S(1)}, bf16[64,1024]{1,0:T(8,128)(2,1)}, u32[]{:S(2)}, u32[]{:S(2)}) collective-permute-start(bf16[64,1024]{1,0:T(8,128)(2,1)S(1)} %get-tuple-element.100), channel_id=1, source_target_pairs={{0,6},{2,4},{4,2},{6,0},{8,14},{10,12},{12,10},{14,8},{1,7},{3,5},... | collective-permute-start | bytes 393224 | tf_op jit(solution)/shard_map/ppermute | solution.py:281
  9.0 28.4 %collective-permute-start.5 = (bf16[64,1024]{1,0:T(8,128)(2,1)S(1)}, bf16[64,1024]{1,0:T(8,128)(2,1)}, u32[]{:S(2)}, u32[]{:S(2)}) collective-permute-start(bf16[64,1024]{1,0:T(8,128)(2,1)S(1)} %get-tuple-element.99), channel_id=1, source_target_pairs={{0,8},{2,10},{4,12},{6,14},{8,0},{10,2},{12,4},{14,6},{1,9},{3,11}... | collective-permute-start | bytes 393224 | tf_op jit(solution)/shard_map/ppermute | solution.py:281
  13.1 18.8 %collective-permute-start.6 = (bf16[64,1024]{1,0:T(8,128)(2,1)}, bf16[64,1024]{1,0:T(8,128)(2,1)}, u32[]{:S(2)}, u32[]{:S(2)}) collective-permute-start(bf16[64,1024]{1,0:T(8,128)(2,1)} %get-tuple-element.98), channel_id=1, source_target_pairs={{0,10},{2,8},{4,14},{6,12},{8,2},{10,0},{12,6},{14,4},{1,11},{3,9}... | collective-permute-start | bytes 393224 | tf_op jit(solution)/shard_map/ppermute | solution.py:281
  15.0 22.3 %all-to-all-start = ((bf16[8,2,1024]{2,1,0:T(2,128)(2,1)}), bf16[8,2,1024]{2,1,0:T(2,128)(2,1)S(1)}, u32[]{:S(2)}, u32[]{:S(2)}) async-start(bf16[8,2,1024]{2,1,0:T(2,128)(2,1)} %broadcast_in_dim.10), calls=%async_computation | async-start | bytes 65536 | tf_op jit(solution)/shard_map/all_to_all | solution.py:299
  20.0 19.3 %collective-permute-start.3 = (bf16[64,1024]{1,0:T(8,128)(2,1)}, bf16[64,1024]{1,0:T(8,128)(2,1)}, u32[]{:S(2)}, u32[]{:S(2)}) collective-permute-start(bf16[64,1024]{1,0:T(8,128)(2,1)} %slice.59), channel_id=1, source_target_pairs={{0,4},{2,6},{4,0},{6,2},{8,12},{10,14},{12,8},{14,10},{1,5},{3,7},... | collective-permute-start | bytes 393224 | tf_op jit(solution)/shard_map/ppermute | solution.py:281
  22.7 27.7 %collective-permute-start.2 = (bf16[64,1024]{1,0:T(8,128)(2,1)}, bf16[64,1024]{1,0:T(8,128)(2,1)}, u32[]{:S(2)}, u32[]{:S(2)}) collective-permute-start(bf16[64,1024]{1,0:T(8,128)(2,1)} %slice.58), channel_id=1, source_target_pairs={{0,2},{2,0},{4,6},{6,4},{8,10},{10,8},{12,14},{14,12},{1,3},{3,1},... | collective-permute-start | bytes 393224 | tf_op jit(solution)/shard_map/ppermute | solution.py:281
  37.3 17.5 %collective-permute-start.10 = (bf16[64,1024]{1,0:T(8,128)(2,1)S(1)}, bf16[64,1024]{1,0:T(8,128)(2,1)}, u32[]{:S(2)}, u32[]{:S(2)}) collective-permute-start(bf16[64,1024]{1,0:T(8,128)(2,1)S(1)} %slice.64), channel_id=1, source_target_pairs={{0,10},{2,8},{4,14},{6,12},{8,2},{10,0},{12,6},{14,4},{1,11},{3,9}... | collective-permute-start | bytes 393224 | tf_op jit(solution)/shard_map/ppermute | solution.py:281
  38.1 16.8 %collective-permute-start.13 = (bf16[64,1024]{1,0:T(8,128)(2,1)}, bf16[64,1024]{1,0:T(8,128)(2,1)}, u32[]{:S(2)}, u32[]{:S(2)}) collective-permute-start(bf16[64,1024]{1,0:T(8,128)(2,1)} %slice.65), channel_id=1, source_target_pairs={{0,12},{2,14},{4,8},{6,10},{8,4},{10,6},{12,0},{14,2},{1,13},{3,15... | collective-permute-start | bytes 393224 | tf_op jit(solution)/shard_map/ppermute | solution.py:281
  40.1 18.4 %collective-permute-start.7 = (bf16[64,1024]{1,0:T(8,128)(2,1)}, bf16[64,1024]{1,0:T(8,128)(2,1)}, u32[]{:S(2)}, u32[]{:S(2)}) collective-permute-start(bf16[64,1024]{1,0:T(8,128)(2,1)} %slice.63), channel_id=1, source_target_pairs={{0,8},{2,10},{4,12},{6,14},{8,0},{10,2},{12,4},{14,6},{1,9},{3,11}... | collective-permute-start | bytes 393224 | tf_op jit(solution)/shard_map/ppermute | solution.py:281
  42.7 17.6 %collective-permute-start.17 = (bf16[64,1024]{1,0:T(8,128)(2,1)}, bf16[64,1024]{1,0:T(8,128)(2,1)}, u32[]{:S(2)}, u32[]{:S(2)}) collective-permute-start(bf16[64,1024]{1,0:T(8,128)(2,1)} %slice.68), channel_id=1, source_target_pairs={{0,4},{2,6},{4,0},{6,2},{8,12},{10,14},{12,8},{14,10},{1,5},{3,7},... | collective-permute-start | bytes 393224 | tf_op jit(solution)/shard_map/ppermute | solution.py:281
  55.0 17.7 %collective-permute-start.14 = (bf16[64,1024]{1,0:T(8,128)(2,1)S(1)}, bf16[64,1024]{1,0:T(8,128)(2,1)S(1)}, u32[]{:S(2)}, u32[]{:S(2)}) collective-permute-start(bf16[64,1024]{1,0:T(8,128)(2,1)S(1)} %slice.66), channel_id=1, source_target_pairs={{0,2},{2,0},{4,6},{6,4},{8,10},{10,8},{12,14},{14,12},{1,3},{3,1},... | collective-permute-start | bytes 393224 | tf_op jit(solution)/shard_map/ppermute | solution.py:281
  58.5 20.0 %collective-permute-start.8 = (bf16[64,1024]{1,0:T(8,128)(2,1)}, bf16[64,1024]{1,0:T(8,128)(2,1)S(1)}, u32[]{:S(2)}, u32[]{:S(2)}) collective-permute-start(bf16[64,1024]{1,0:T(8,128)(2,1)} %get-tuple-element.57), channel_id=1, source_target_pairs={{0,12},{2,14},{4,8},{6,10},{8,4},{10,6},{12,0},{14,2},{1,13},{3,15... | collective-permute-start | bytes 393224 | tf_op jit(solution)/shard_map/ppermute | solution.py:281
  60.3 22.5 %collective-permute-start.18 = (bf16[64,1024]{1,0:T(8,128)(2,1)}, bf16[64,1024]{1,0:T(8,128)(2,1)S(1)}, u32[]{:S(2)}, u32[]{:S(2)}) collective-permute-start(bf16[64,1024]{1,0:T(8,128)(2,1)} %get-tuple-element.71), channel_id=1, source_target_pairs={{0,8},{2,10},{4,12},{6,14},{8,0},{10,2},{12,4},{14,6},{1,9},{3,11}... | collective-permute-start | bytes 393224 | tf_op jit(solution)/shard_map/ppermute | solution.py:281
  60.5 19.8 %collective-permute-start.20 = (bf16[64,1024]{1,0:T(8,128)(2,1)}, bf16[64,1024]{1,0:T(8,128)(2,1)}, u32[]{:S(2)}, u32[]{:S(2)}) collective-permute-start(bf16[64,1024]{1,0:T(8,128)(2,1)} %get-tuple-element.74), channel_id=1, source_target_pairs={{0,10},{2,8},{4,14},{6,12},{8,2},{10,0},{12,6},{14,4},{1,11},{3,9}... | collective-permute-start | bytes 393224 | tf_op jit(solution)/shard_map/ppermute | solution.py:281
  65.5 20.1 %collective-permute-start.12 = (bf16[64,1024]{1,0:T(8,128)(2,1)}, bf16[64,1024]{1,0:T(8,128)(2,1)}, u32[]{:S(2)}, u32[]{:S(2)}) collective-permute-start(bf16[64,1024]{1,0:T(8,128)(2,1)} %get-tuple-element.63), channel_id=1, source_target_pairs={{0,4},{2,6},{4,0},{6,2},{8,12},{10,14},{12,8},{14,10},{1,5},{3,7},... | collective-permute-start | bytes 393224 | tf_op jit(solution)/shard_map/ppermute | solution.py:281
  78.4 21.3 %collective-permute-start.9 = (bf16[64,1024]{1,0:T(8,128)(2,1)}, bf16[64,1024]{1,0:T(8,128)(2,1)S(1)}, u32[]{:S(2)}, u32[]{:S(2)}) collective-permute-start(bf16[64,1024]{1,0:T(8,128)(2,1)} %get-tuple-element.58), channel_id=1, source_target_pairs={{0,2},{2,0},{4,6},{6,4},{8,10},{10,8},{12,14},{14,12},{1,3},{3,1},... | collective-permute-start | bytes 393224 | tf_op jit(solution)/shard_map/ppermute | solution.py:281
  82.8 17.0 %collective-permute-start.21 = (bf16[64,1024]{1,0:T(8,128)(2,1)}, bf16[64,1024]{1,0:T(8,128)(2,1)S(1)}, u32[]{:S(2)}, u32[]{:S(2)}) collective-permute-start(bf16[64,1024]{1,0:T(8,128)(2,1)} %get-tuple-element.80), channel_id=1, source_target_pairs={{0,12},{2,14},{4,8},{6,10},{8,4},{10,6},{12,0},{14,2},{1,13},{3,15... | collective-permute-start | bytes 393224 | tf_op jit(solution)/shard_map/ppermute | solution.py:281
  85.6 33.7 %collective-permute-start.26 = (bf16[64,1024]{1,0:T(8,128)(2,1)}, bf16[64,1024]{1,0:T(8,128)(2,1)S(1)}, u32[]{:S(2)}, u32[]{:S(2)}) collective-permute-start(bf16[64,1024]{1,0:T(8,128)(2,1)} %get-tuple-element.89), channel_id=1, source_target_pairs={{0,8},{2,10},{4,12},{6,14},{8,0},{10,2},{12,4},{14,6},{1,9},{3,11}... | collective-permute-start | bytes 393224 | tf_op jit(solution)/shard_map/ppermute | solution.py:281
  85.6 33.7 %collective-permute-start.27 = (bf16[64,1024]{1,0:T(8,128)(2,1)}, bf16[64,1024]{1,0:T(8,128)(2,1)S(1)}, u32[]{:S(2)}, u32[]{:S(2)}) collective-permute-start(bf16[64,1024]{1,0:T(8,128)(2,1)} %get-tuple-element.91), channel_id=1, source_target_pairs={{0,10},{2,8},{4,14},{6,12},{8,2},{10,0},{12,6},{14,4},{1,11},{3,9}... | collective-permute-start | bytes 393224 | tf_op jit(solution)/shard_map/ppermute | solution.py:281
  89.7 29.7 %collective-permute-start.24 = (bf16[64,1024]{1,0:T(8,128)(2,1)}, bf16[64,1024]{1,0:T(8,128)(2,1)S(1)}, u32[]{:S(2)}, u32[]{:S(2)}) collective-permute-start(bf16[64,1024]{1,0:T(8,128)(2,1)} %get-tuple-element.85), channel_id=1, source_target_pairs={{0,4},{2,6},{4,0},{6,2},{8,12},{10,14},{12,8},{14,10},{1,5},{3,7},... | collective-permute-start | bytes 393224 | tf_op jit(solution)/shard_map/ppermute | solution.py:281
  99.7 19.6 %collective-permute-start.22 = (bf16[64,1024]{1,0:T(8,128)(2,1)}, bf16[64,1024]{1,0:T(8,128)(2,1)S(1)}, u32[]{:S(2)}, u32[]{:S(2)}) collective-permute-start(bf16[64,1024]{1,0:T(8,128)(2,1)} %get-tuple-element.81), channel_id=1, source_target_pairs={{0,2},{2,0},{4,6},{6,4},{8,10},{10,8},{12,14},{14,12},{1,3},{3,1},... | collective-permute-start | bytes 393224 | tf_op jit(solution)/shard_map/ppermute | solution.py:281
  99.7 19.6 %collective-permute-start.25 = (bf16[64,1024]{1,0:T(8,128)(2,1)}, bf16[64,1024]{1,0:T(8,128)(2,1)S(1)}, u32[]{:S(2)}, u32[]{:S(2)}) collective-permute-start(bf16[64,1024]{1,0:T(8,128)(2,1)} %get-tuple-element.87), channel_id=1, source_target_pairs={{0,6},{2,4},{4,2},{6,0},{8,14},{10,12},{12,10},{14,8},{1,7},{3,5},... | collective-permute-start | bytes 393224 | tf_op jit(solution)/shard_map/ppermute | solution.py:281
  (12 other events, 169.7 us)

commit v3 on v2

--- a/solution.py
+++ b/solution.py
@@ -120,7 +120,7 @@
     for d in range(members):
         for h in range(heads):
             cols = pl.ds(h * DH, DH)
-            outs[d][:, cols] = held[me ^ chosen[me ^ d, h], :, cols]
+            outs[d][:, cols] = held[me ^ chosen[d, h], :, cols]
 
 
 def pick_pieces(me, chosen, pieces):
@@ -141,6 +141,29 @@
             flops=0, transcendentals=0, bytes_accessed=4 * members * rows * width
         ),
     )(me, chosen, *pieces)
+
+
+def stack_kernel(members, heads, me_ref, chosen, held, out):
+    me = me_ref[0]
+    for d in range(members):
+        for h in range(heads):
+            cols = pl.ds(h * DH, DH)
+            out[me ^ d, :, cols] = held[chosen[d, h], :, cols]
+
+
+def pick_stack(me, chosen, held):
+    members, rows, width = held.shape
+    spec = pl.BlockSpec((members, rows, width), lambda i, m, t: (0, 0, 0))
+    return pl.pallas_call(
+        functools.partial(stack_kernel, members, width // DH),
+        grid_spec=pltpu.PrefetchScalarGridSpec(
+            num_scalar_prefetch=2, grid=(1,), in_specs=[spec], out_specs=spec
+        ),
+        out_shape=jax.ShapeDtypeStruct((members, rows, width), BF16),
+        cost_estimate=pl.CostEstimate(
+            flops=0, transcendentals=0, bytes_accessed=4 * members * rows * width
+        ),
+    )(me, chosen, held)
 
 
 def softmax_part(q, keys):
@@ -174,7 +197,7 @@
             jax.ShapeDtypeStruct((heads, tok, 1), F32),
             jax.ShapeDtypeStruct((heads, tok, 1), F32),
         ],
-        compiler_params=pltpu.CompilerParams(vmem_limit_bytes=32 << 20),
+        compiler_params=pltpu.CompilerParams(vmem_limit_bytes=16 << 20),
         cost_estimate=pl.CostEstimate(
             flops=4 * tok * BS * width,
             transcendentals=heads * tok * BS,
@@ -183,12 +206,8 @@
     )(q, k, v)
 
 
-def scores_kernel(members, q_ref, sum_ref, top_ref, total_ref, *refs):
-    far_k, (own_ref, w_ref, kf_ref) = refs[:members], refs[members:]
-    rows = far_k[0].shape[0]
-    for e in range(members):
-        kf_ref[pl.ds(e * rows, rows), :] = far_k[e][...]
-    far_max, far_w, far_total = softmax_part(q_ref[...], kf_ref[...])
+def scores_kernel(q_ref, sum_ref, top_ref, total_ref, far_k, own_ref, w_ref):
+    far_max, far_w, far_total = softmax_part(q_ref[...], far_k[...].reshape(BS, DH))
     own_max = top_ref[0]
     joint = jnp.maximum(own_max, far_max)
     own_e = jnp.exp(own_max - joint)
@@ -199,63 +218,66 @@
 
 
 def score_parts(q, own, far_k):
-    members = len(far_k)
+    members, rows, _ = far_k.shape
     tok, width = q.shape
     heads = width // DH
-    rows = far_k[0].shape[0]
     whole = pl.BlockSpec((tok, DH), lambda h: (0, h))
     column = pl.BlockSpec((1, tok, 1), lambda h: (h, 0, 0))
-    piece = pl.BlockSpec((rows, DH), lambda h: (0, h))
-    return pl.pallas_call(
-        functools.partial(scores_kernel, members),
+    pieces = pl.BlockSpec((members, rows, DH), lambda h: (0, 0, h))
+    return pl.pallas_call(
+        scores_kernel,
         grid=(heads,),
-        in_specs=[whole, whole, column, column] + [piece] * members,
+        in_specs=[whole, whole, column, column, pieces],
         out_specs=[whole, pl.BlockSpec((1, tok, BS), lambda h: (h, 0, 0))],
         out_shape=[
             jax.ShapeDtypeStruct((tok, width), F32),
             jax.ShapeDtypeStruct((heads, tok, BS), BF16),
         ],
-        scratch_shapes=[pltpu.VMEM((BS, DH), BF16)],
-        compiler_params=pltpu.CompilerParams(vmem_limit_bytes=32 << 20),
+        compiler_params=pltpu.CompilerParams(vmem_limit_bytes=16 << 20),
         cost_estimate=pl.CostEstimate(
             flops=2 * tok * BS * width,
             transcendentals=heads * tok * BS,
             bytes_accessed=12 * tok * width + 2 * heads * tok * BS,
         ),
-    )(q, *own, *far_k)
-
-
-def finish_kernel(members, w_ref, own_ref, *refs):
+    )(q, *own, far_k)
+
+
+def finish_kernel(members, me_ref, w_ref, own_ref, *refs):
     far_v, (out_ref, vf_ref) = refs[:members], refs[members:]
     rows = far_v[0].shape[0]
-    for e in range(members):
-        vf_ref[pl.ds(e * rows, rows), :] = far_v[e][...]
+    for d in range(members):
+        first = pl.multiple_of((me_ref[0] ^ d) * rows, rows)
+        vf_ref[pl.ds(first, rows), :] = far_v[d][...]
     out_ref[...] = (
         own_ref[...] + jnp.dot(w_ref[0], vf_ref[...], preferred_element_type=F32)
     ).astype(BF16)
 
 
-def finish(w, own, far_v):
+def finish(me, w, own, far_v):
     members = len(far_v)
     tok, width = own.shape
     heads = width // DH
     rows = far_v[0].shape[0]
-    whole = pl.BlockSpec((tok, DH), lambda h: (0, h))
-    piece = pl.BlockSpec((rows, DH), lambda h: (0, h))
+    whole = pl.BlockSpec((tok, DH), lambda h, m: (0, h))
+    piece = pl.BlockSpec((rows, DH), lambda h, m: (0, h))
     return pl.pallas_call(
         functools.partial(finish_kernel, members),
-        grid=(heads,),
-        in_specs=[pl.BlockSpec((1, tok, BS), lambda h: (h, 0, 0)), whole] + [piece] * members,
-        out_specs=whole,
+        grid_spec=pltpu.PrefetchScalarGridSpec(
+            num_scalar_prefetch=1,
+            grid=(heads,),
+            in_specs=[pl.BlockSpec((1, tok, BS), lambda h, m: (h, 0, 0)), whole]
+            + [piece] * members,
+            out_specs=whole,
+            scratch_shapes=[pltpu.VMEM((BS, DH), BF16)],
+        ),
         out_shape=jax.ShapeDtypeStruct((tok, width), BF16),
-        scratch_shapes=[pltpu.VMEM((BS, DH), BF16)],
-        compiler_params=pltpu.CompilerParams(vmem_limit_bytes=32 << 20),
+        compiler_params=pltpu.CompilerParams(vmem_limit_bytes=16 << 20),
         cost_estimate=pl.CostEstimate(
             flops=2 * tok * BS * width,
             transcendentals=0,
             bytes_accessed=8 * tok * width + 2 * heads * tok * BS,
         ),
-    )(w, own, *far_v)
+    )(me, w, own, *far_v)
 
 
 def after(x, *earlier):
@@ -286,35 +308,45 @@
         return got
 
     def rows_of(array):
-        return lambda d, *earlier: after(array, *earlier)[d * rows : (d + 1) * rows]
+        return lambda d, *earlier: lax.dynamic_slice_in_dim(
+            after(array, *earlier), (me ^ d) * rows, rows
+        )
 
     def piece_of(pieces):
         return lambda d, *earlier: after(pieces[d], *earlier)
 
+    def swap(array):
+        return lax.all_to_all(array, "context", 0, 0, tiled=True)
+
     def pooled(array):
         return (jnp.sum(array, axis=0, dtype=F32) / math.sqrt(BS)).astype(BF16)
 
+    held_k = swap(key_rows.reshape(members, rows, width))
+
     chosen = jnp.pad(selection[:, 0].astype(BF16), (0, width - heads))
-    shared = jnp.stack([pooled(key_rows), chosen])[None]
-    shared = lax.all_to_all(
-        jnp.broadcast_to(shared, (members, 2, width)), "context", 0, 0, tiled=True
+    mine = jnp.stack([pooled(key_rows), chosen])
+    shared = jnp.stack(
+        [mine]
+        + [
+            lax.ppermute(mine, "context", [(i, i ^ d) for i in range(members)])
+            for d in range(1, members)
+        ]
     )
     chosen = shared[:, 1, :heads].astype(jnp.int32)
     here = me.astype(jnp.int32)[None]
 
-    held_k = exchange(rows_of(key_rows))
     held_v = exchange(rows_of(value_rows))
-    own = own_part(after(query_rows, held_k[order[0]]), key_rows, value_rows)
-    far_k = exchange(piece_of(pick_pieces(here, chosen, held_k)))
+    own = own_part(after(query_rows, arrived[0]), key_rows, value_rows)
+    far_k = swap(pick_stack(here, chosen, after(held_k, own[0], arrived[4])))
     far_v = exchange(piece_of(pick_pieces(here, chosen, held_v)))
 
     scaled, w = score_parts(query_rows, own, far_k)
-    attended = finish(w, scaled, far_v)
+    attended = finish(here, w, scaled, far_v)
 
     sort_logits = jnp.einsum(
         "hd,chd->hc",
         pooled(query_rows).reshape(heads, DH),
-        shared[:, 0].reshape(members, heads, DH),
+        shared[me ^ jnp.arange(members), 0].reshape(members, heads, DH),
         preferred_element_type=F32,
     ) / math.sqrt(DH)
     return attended, sort_logits.reshape(heads, 1, members)

time: 124 us -> 155 us (1.25)
  waiting for transfers between devices: 11.7 us -> 39.2 us
  local copies, waits for them, and re-layouts: 8.84 us -> 11.6 us
  starting transfers between devices: 70.1 us -> 71.7 us
    ppermute x28 -> x14, starting transfers between devices: 65.9 us -> 44.4 us  [exchange(): lax.ppermute(take(d, *earlier), 'context', [(i, i ^ d) for i in range(mem...]
    ppermute x0 -> x7, starting transfers between devices: none -> 14.2 us  [power_of_two(): lax.ppermute(mine, 'context', [(i, i ^ d) for i in range(members)])]
    ppermute x0 -> x7, waiting for transfers between devices: none -> 14 us  [power_of_two(): lax.ppermute(mine, 'context', [(i, i ^ d) for i in range(members)])]
    ppermute x28 -> x14, waiting for transfers between devices: 11.7 us -> 25.2 us  [exchange(): lax.ppermute(take(d, *earlier), 'context', [(i, i ^ d) for i in range(mem...]
    unnamed x14 -> x30, local copies, waits for them, and re-layouts: 0.67 us -> 10.2 us
    all_to_all x1 -> x2, starting transfers between devices: 4.2 us -> 13.1 us  [swap(): return lax.all_to_all(array, 'context', 0, 0, tiled=True)]
    slice x13 -> x0, local copies, waits for them, and re-layouts: 7.54 us -> none  [the longest x11 7.44 us: rows_of(): return lambda d, *earlier: after(array, *earlier)[d * rows:(d + 1) * rows]]
    pallas_call x2 -> x1, Pallas kernels: 6.2 us -> 3.11 us  [pick_pieces(): pl.pallas_call(functools.partial(pick_kernel, members, width // DH), grid...]
  transfers between devices with their start and end apart: 29 -> 23, of which waited for: 5 -> 8; matrix products, arithmetic and copies ran while one was open for 8% -> 2% of each run, Pallas kernels for 19% -> 13%
where the time goes in v3:
time: 155 us
  starting transfers between devices  71.7 us (46%)
  waiting for transfers between devices  39.2 us (25%)
  Pallas kernels  27.6 us (18%)
  local copies, waits for them, and re-layouts  11.6 us (7%)
  other arithmetic  3.57 us (2%)
    ppermute x14, starting transfers between devices, exchange(): lax.ppermute(take(d, *earlier), 'context', [(i, i ^ d) for i in range(mem...  44.4 us
    ppermute x14, waiting for transfers between devices, exchange(): lax.ppermute(take(d, *earlier), 'context', [(i, i ^ d) for i in range(mem...  25.2 us
    ppermute x7, starting transfers between devices, power_of_two(): lax.ppermute(mine, 'context', [(i, i ^ d) for i in range(members)])  14.2 us
    ppermute x7, waiting for transfers between devices, power_of_two(): lax.ppermute(mine, 'context', [(i, i ^ d) for i in range(members)])  14 us
    all_to_all x2, starting transfers between devices, swap(): return lax.all_to_all(array, 'context', 0, 0, tiled=True)  13.1 us
    unnamed x30, local copies, waits for them, and re-layouts  10.2 us
    pallas_call x1, Pallas kernels, score_parts(): pl.pallas_call(scores_kernel, grid=(heads,), in_specs=[whole, whole, colu...  8.85 us
    pallas_call x1, Pallas kernels, own_part(): pl.pallas_call(own_kernel, grid=(heads,), in_specs=[whole] * 3, out_specs...  7.8 us
  transfers between devices with their start and end apart: 23, of which 8 were waited for; matrix products, arithmetic and copies ran while one was open for 2% of the time, Pallas kernels for 13%

profile of v3, /device:TPU:0, one launch (start us, length us, event | category | flops | bytes accessed | tf_op | source)
XLA Modules:
  0.0 154.6 jit_solution(12965789813477850575)
XLA Ops:
  2.9 3.0 %collective-permute-start.1 = (bf16[2,1024]{1,0:T(2,128)(2,1)S(1)}, bf16[2,1024]{1,0:T(2,128)(2,1)S(1)}, u32[]{:S(2)}, u32[]{:S(2)}) collective-permute-start(bf16[2,1024]{1,0:T(2,128)(2,1)S(1)} %get-tuple-element.53), channel_id=1, source_target_pairs={{0,2},{2,0},{4,6},{6,4},{8,10},{10,8},{12,14},{14,12},{1,3},{3,1},... | collective-permute-start | bytes 12296 | tf_op jit(solution)/shard_map/ppermute | solution.py:331
  7.5 3.0 %collective-permute-start.4 = (bf16[2,1024]{1,0:T(2,128)(2,1)S(1)}, bf16[2,1024]{1,0:T(2,128)(2,1)S(1)}, u32[]{:S(2)}, u32[]{:S(2)}) collective-permute-start(bf16[2,1024]{1,0:T(2,128)(2,1)S(1)} %get-tuple-element.53), channel_id=1, source_target_pairs={{0,8},{2,10},{4,12},{6,14},{8,0},{10,2},{12,4},{14,6},{1,9},{3,11}... | collective-permute-start | bytes 12296 | tf_op jit(solution)/shard_map/ppermute | solution.py:331
  11.7 4.9 %all-to-all-start = ((bf16[8,64,1024]{2,1,0:T(8,128)(2,1)}), bf16[8,64,1024]{2,1,0:T(8,128)(2,1)}, u32[]{:S(2)}, u32[]{:S(2)}) async-start(bf16[8,64,1024]{2,1,0:T(8,128)(2,1)} %bitcast.35), calls=%async_computation | async-start | bytes 2097152 | tf_op jit(solution)/shard_map/all_to_all | solution.py:319
  17.4 3.8 %collective-permute-start.6 = (bf16[2,1024]{1,0:T(2,128)(2,1)S(1)}, bf16[2,1024]{1,0:T(2,128)(2,1)S(1)}, u32[]{:S(2)}, u32[]{:S(2)}) collective-permute-start(bf16[2,1024]{1,0:T(2,128)(2,1)S(1)} %get-tuple-element.53), channel_id=1, source_target_pairs={{0,12},{2,14},{4,8},{6,10},{8,4},{10,6},{12,0},{14,2},{1,13},{3,15... | collective-permute-start | bytes 12296 | tf_op jit(solution)/shard_map/ppermute | solution.py:331
  22.8 3.3 %collective-permute-start = (bf16[64,1024]{1,0:T(8,128)(2,1)S(1)}, bf16[64,1024]{1,0:T(8,128)(2,1)}, u32[]{:S(2)}, u32[]{:S(2)}) collective-permute-start(bf16[64,1024]{1,0:T(8,128)(2,1)S(1)} %get-tuple-element.59), channel_id=1, source_target_pairs={{0,14},{2,12},{4,10},{6,8},{8,6},{10,4},{12,2},{14,0},{1,15},{3,13... | collective-permute-start | bytes 393224 | tf_op jit(solution)/shard_map/ppermute | solution.py:303
  26.2 13.0 %collective-permute-done.6 = bf16[2,1024]{1,0:T(2,128)(2,1)S(1)} collective-permute-done((bf16[2,1024]{1,0:T(2,128)(2,1)S(1)}, bf16[2,1024]{1,0:T(2,128)(2,1)S(1)}, u32[]{:S(2)}, u32[]{:S(2)}) %collective-permute-start.6) | collective-permute-done | bytes 4128 | tf_op jit(solution)/shard_map/ppermute | solution.py:331
  41.8 7.8 %shard_map.59 = (f32[512,1024]{1,0:T(8,128)S(1)}, f32[8,512,1]{2,1,0:T(8,128)S(1)}, f32[8,512,1]{2,1,0:T(8,128)S(1)}) custom-call(bf16[512,1024]{1,0:T(8,128)(2,1)S(1)} %copy-done.1, bf16[512,1024]{1,0:T(8,128)(2,1)S(1)} %copy-done, bf16[512,1024]{1,0:T(8,128)(2,1)S(1)} %copy-done.8), custom_call_target="tpu_custom_call" | custom-call | flops 1073741824 | bytes 5242880 | tf_op jit(solution)/shard_map/pallas_call | solution.py:190
  53.6 3.1 %shard_map.60 = bf16[8,64,1024]{2,1,0:T(8,128)(2,1)} custom-call(s32[1]{0:T(128)} %bitcast.me_ref, s32[8,8]{1,0:T(8,128)} %bitcast.36, bf16[8,64,1024]{2,1,0:T(8,128)(2,1)} %all-to-all-done.held), custom_call_target="tpu_custom_call" | custom-call | bytes 2097152 | tf_op jit(solution)/shard_map/pallas_call | solution.py:157
  56.7 8.3 %all-to-all-start.1 = ((bf16[8,64,1024]{2,1,0:T(8,128)(2,1)}), bf16[8,64,1024]{2,1,0:T(8,128)(2,1)S(1)}, u32[]{:S(2)}, u32[]{:S(2)}) async-start(bf16[8,64,1024]{2,1,0:T(8,128)(2,1)} %shard_map.60), calls=%async_computation.1 | async-start | bytes 2097152 | tf_op jit(solution)/shard_map/all_to_all | solution.py:319
  65.0 3.8 %collective-permute-start.9 = (bf16[64,1024]{1,0:T(8,128)(2,1)S(1)}, bf16[64,1024]{1,0:T(8,128)(2,1)S(1)}, u32[]{:S(2)}, u32[]{:S(2)}) collective-permute-start(bf16[64,1024]{1,0:T(8,128)(2,1)S(1)} %get-tuple-element.56), channel_id=1, source_target_pairs={{0,12},{2,14},{4,8},{6,10},{8,4},{10,6},{12,0},{14,2},{1,13},{3,15... | collective-permute-start | bytes 393224 | tf_op jit(solution)/shard_map/ppermute | solution.py:303
  68.8 3.8 %collective-permute-start.13 = (bf16[64,1024]{1,0:T(8,128)(2,1)}, bf16[64,1024]{1,0:T(8,128)(2,1)}, u32[]{:S(2)}, u32[]{:S(2)}) collective-permute-start(bf16[64,1024]{1,0:T(8,128)(2,1)} %get-tuple-element.54), channel_id=1, source_target_pairs={{0,10},{2,8},{4,14},{6,12},{8,2},{10,0},{12,6},{14,4},{1,11},{3,9}... | collective-permute-start | bytes 393224 | tf_op jit(solution)/shard_map/ppermute | solution.py:303
  72.8 17.5 %collective-permute-done.9.refs_6_ = bf16[64,1024]{1,0:T(8,128)(2,1)S(1)} collective-permute-done((bf16[64,1024]{1,0:T(8,128)(2,1)S(1)}, bf16[64,1024]{1,0:T(8,128)(2,1)S(1)}, u32[]{:S(2)}, u32[]{:S(2)}) %collective-permute-start.9) | collective-permute-done | bytes 131104 | tf_op jit(solution)/shard_map/ppermute | solution.py:303
  92.4 13.3 %collective-permute-start.11 = (bf16[64,1024]{1,0:T(8,128)(2,1)S(1)}, bf16[64,1024]{1,0:T(8,128)(2,1)S(1)}, u32[]{:S(2)}, u32[]{:S(2)}) collective-permute-start(bf16[64,1024]{1,0:T(8,128)(2,1)S(1)} %constant_dynamic-slice_fusion.2), channel_id=1, source_target_pairs={{0,4},{2,6},{4,0},{6,2},{8,12},{10,14},{12,8},{14,10},{1,5},{3,7},... | collective-permute-start | bytes 393224 | tf_op jit(solution)/shard_map/ppermute | solution.py:303
  106.4 2.3 %collective-permute-done.13.refs_5_ = bf16[64,1024]{1,0:T(8,128)(2,1)} collective-permute-done((bf16[64,1024]{1,0:T(8,128)(2,1)}, bf16[64,1024]{1,0:T(8,128)(2,1)}, u32[]{:S(2)}, u32[]{:S(2)}) %collective-permute-start.13) | collective-permute-done | bytes 131104 | tf_op jit(solution)/shard_map/ppermute | solution.py:303
  108.6 1.7 %collective-permute-done.11.refs_2_ = bf16[64,1024]{1,0:T(8,128)(2,1)S(1)} collective-permute-done((bf16[64,1024]{1,0:T(8,128)(2,1)S(1)}, bf16[64,1024]{1,0:T(8,128)(2,1)S(1)}, u32[]{:S(2)}, u32[]{:S(2)}) %collective-permute-start.11) | collective-permute-done | bytes 131104 | tf_op jit(solution)/shard_map/ppermute | solution.py:303
  111.0 3.1 %shard_map.62 = (bf16[64,1024]{1,0:T(8,128)(2,1)}, bf16[64,1024]{1,0:T(8,128)(2,1)}, bf16[64,1024]{1,0:T(8,128)(2,1)}, bf16[64,1024]{1,0:T(8,128)(2,1)}, bf16[64...) custom-call(s32[1]{0:T(128)} %bitcast.me_ref, ...), custom_call_target="tpu_custom_call" | custom-call | bytes 2097152 | tf_op jit(solution)/shard_map/pallas_call | solution.py:130
  115.3 3.5 %collective-permute-start.16 = (bf16[64,1024]{1,0:T(8,128)(2,1)}, bf16[64,1024]{1,0:T(8,128)(2,1)S(1)}, u32[]{:S(2)}, u32[]{:S(2)}) collective-permute-start(bf16[64,1024]{1,0:T(8,128)(2,1)} %get-tuple-element.42), channel_id=1, source_target_pairs={{0,14},{2,12},{4,10},{6,8},{8,6},{10,4},{12,2},{14,0},{1,15},{3,13... | collective-permute-start | bytes 393224 | tf_op jit(solution)/shard_map/ppermute | solution.py:303
  118.9 1.7 %collective-permute-start.19 = (bf16[64,1024]{1,0:T(8,128)(2,1)}, bf16[64,1024]{1,0:T(8,128)(2,1)S(1)}, u32[]{:S(2)}, u32[]{:S(2)}) collective-permute-start(bf16[64,1024]{1,0:T(8,128)(2,1)} %get-tuple-element.47), channel_id=1, source_target_pairs={{0,8},{2,10},{4,12},{6,14},{8,0},{10,2},{12,4},{14,6},{1,9},{3,11}... | collective-permute-start | bytes 393224 | tf_op jit(solution)/shard_map/ppermute | solution.py:303
  124.1 2.2 %collective-permute-done.16.refs_7_ = bf16[64,1024]{1,0:T(8,128)(2,1)S(1)} collective-permute-done((bf16[64,1024]{1,0:T(8,128)(2,1)}, bf16[64,1024]{1,0:T(8,128)(2,1)S(1)}, u32[]{:S(2)}, u32[]{:S(2)}) %collective-permute-start.16) | collective-permute-done | bytes 131104 | tf_op jit(solution)/shard_map/ppermute | solution.py:303
  126.3 9.3 %collective-permute-start.17 = (bf16[64,1024]{1,0:T(8,128)(2,1)}, bf16[64,1024]{1,0:T(8,128)(2,1)S(1)}, u32[]{:S(2)}, u32[]{:S(2)}) collective-permute-start(bf16[64,1024]{1,0:T(8,128)(2,1)} %get-tuple-element.43), channel_id=1, source_target_pairs={{0,4},{2,6},{4,0},{6,2},{8,12},{10,14},{12,8},{14,10},{1,5},{3,7},... | collective-permute-start | bytes 393224 | tf_op jit(solution)/shard_map/ppermute | solution.py:303
  136.2 1.6 %copy-done.3 = f32[512,1024]{1,0:T(8,128)S(1)} copy-done((f32[512,1024]{1,0:T(8,128)S(1)}, f32[512,1024]{1,0:T(8,128)}, u32[]{:S(2)}) %copy-start.3) | copy-done | bytes 2097176
  137.8 1.6 %copy-done.5 = f32[8,512,1]{2,1,0:T(8,128)S(1)} copy-done((f32[8,512,1]{2,1,0:T(8,128)S(1)}, f32[8,512,1]{2,1,0:T(8,128)}, u32[]{:S(2)}) %copy-start.5) | copy-done | bytes 16408
  141.0 8.8 %shard_map.61 = (f32[512,1024]{1,0:T(8,128)S(1)}, bf16[8,512,512]{2,1,0:T(8,128)(2,1)S(1)}) custom-call(bf16[512,1024]{1,0:T(8,128)(2,1)S(1)} %copy-done.1, f32[512,1024]{1,0:T(8,128)S(1)} %copy-done.3, f32[8,512,1]{2,1,0:T(8,128)S(1)} %copy-done.5, f32[8,512,1]{2,1,0:T(8,128)S(1)} %copy-done.7, bf16[8,64,1024]{2,1,0:T(8,128)(2,1)S(1)} %all-to-all-done.1.far_k), custom_call_target="tpu_custom_call" | custom-call | flops 536870912 | bytes 10485760 | tf_op jit(solution)/shard_map/pallas_call | solution.py:227
  149.9 4.7 %shard_map.63 = bf16[512,1024]{1,0:T(8,128)(2,1)} custom-call(s32[1]{0:T(128)} %bitcast.me_ref, bf16[8,512,512]{2,1,0:T(8,128)(2,1)S(1)} %get-tuple-element.31.w_ref, f32[512,1024]{1,0:T(8,128)S(1)} %get-tuple-element.32.own_ref, bf16[64,1024]{1,0:T(8,128)(2,1)S(1)} %copy-done.9, bf16[64,1024]{1,0:T(8,128)(2,1)S(1)} %collective-permute-done.15.refs_1_, ...), custom_call_target="tpu_custom_call" | custom-call | flops 536870912 | bytes 8388608 | tf_op jit(solution)/shard_map/pallas_call | solution.py:263
  (75 shorter events, 24.6 us)
Async XLA Ops:
  2.8 38.9 %copy-start = (bf16[512,1024]{1,0:T(8,128)(2,1)S(1)}, bf16[512,1024]{1,0:T(8,128)(2,1)}, u32[]{:S(2)}) copy-start(bf16[512,1024]{1,0:T(8,128)(2,1)} %k_ref.1) | copy-start | bytes 3145732
  2.9 14.5 %collective-permute-start.1 = (bf16[2,1024]{1,0:T(2,128)(2,1)S(1)}, bf16[2,1024]{1,0:T(2,128)(2,1)S(1)}, u32[]{:S(2)}, u32[]{:S(2)}) collective-permute-start(bf16[2,1024]{1,0:T(2,128)(2,1)S(1)} %get-tuple-element.53), channel_id=1, source_target_pairs={{0,2},{2,0},{4,6},{6,4},{8,10},{10,8},{12,14},{14,12},{1,3},{3,1},... | collective-permute-start | bytes 12296 | tf_op jit(solution)/shard_map/ppermute | solution.py:331
  5.9 15.4 %collective-permute-start.2 = (bf16[2,1024]{1,0:T(2,128)(2,1)S(1)}, bf16[2,1024]{1,0:T(2,128)(2,1)S(1)}, u32[]{:S(2)}, u32[]{:S(2)}) collective-permute-start(bf16[2,1024]{1,0:T(2,128)(2,1)S(1)} %get-tuple-element.53), channel_id=1, source_target_pairs={{0,4},{2,6},{4,0},{6,2},{8,12},{10,14},{12,8},{14,10},{1,5},{3,7},... | collective-permute-start | bytes 12296 | tf_op jit(solution)/shard_map/ppermute | solution.py:331
  7.5 15.3 %collective-permute-start.3 = (bf16[2,1024]{1,0:T(2,128)(2,1)S(1)}, bf16[2,1024]{1,0:T(2,128)(2,1)S(1)}, u32[]{:S(2)}, u32[]{:S(2)}) collective-permute-start(bf16[2,1024]{1,0:T(2,128)(2,1)S(1)} %get-tuple-element.53), channel_id=1, source_target_pairs={{0,6},{2,4},{4,2},{6,0},{8,14},{10,12},{12,10},{14,8},{1,7},{3,5},... | collective-permute-start | bytes 12296 | tf_op jit(solution)/shard_map/ppermute | solution.py:331
  7.5 18.7 %collective-permute-start.4 = (bf16[2,1024]{1,0:T(2,128)(2,1)S(1)}, bf16[2,1024]{1,0:T(2,128)(2,1)S(1)}, u32[]{:S(2)}, u32[]{:S(2)}) collective-permute-start(bf16[2,1024]{1,0:T(2,128)(2,1)S(1)} %get-tuple-element.53), channel_id=1, source_target_pairs={{0,8},{2,10},{4,12},{6,14},{8,0},{10,2},{12,4},{14,6},{1,9},{3,11}... | collective-permute-start | bytes 12296 | tf_op jit(solution)/shard_map/ppermute | solution.py:331
  10.5 15.7 %collective-permute-start.5 = (bf16[2,1024]{1,0:T(2,128)(2,1)S(1)}, bf16[2,1024]{1,0:T(2,128)(2,1)S(1)}, u32[]{:S(2)}, u32[]{:S(2)}) collective-permute-start(bf16[2,1024]{1,0:T(2,128)(2,1)S(1)} %get-tuple-element.53), channel_id=1, source_target_pairs={{0,10},{2,8},{4,14},{6,12},{8,2},{10,0},{12,6},{14,4},{1,11},{3,9}... | collective-permute-start | bytes 12296 | tf_op jit(solution)/shard_map/ppermute | solution.py:331
  11.7 41.9 %all-to-all-start = ((bf16[8,64,1024]{2,1,0:T(8,128)(2,1)}), bf16[8,64,1024]{2,1,0:T(8,128)(2,1)}, u32[]{:S(2)}, u32[]{:S(2)}) async-start(bf16[8,64,1024]{2,1,0:T(8,128)(2,1)} %bitcast.35), calls=%async_computation | async-start | bytes 2097152 | tf_op jit(solution)/shard_map/all_to_all | solution.py:319
  17.4 21.8 %collective-permute-start.6 = (bf16[2,1024]{1,0:T(2,128)(2,1)S(1)}, bf16[2,1024]{1,0:T(2,128)(2,1)S(1)}, u32[]{:S(2)}, u32[]{:S(2)}) collective-permute-start(bf16[2,1024]{1,0:T(2,128)(2,1)S(1)} %get-tuple-element.53), channel_id=1, source_target_pairs={{0,12},{2,14},{4,8},{6,10},{8,4},{10,6},{12,0},{14,2},{1,13},{3,15... | collective-permute-start | bytes 12296 | tf_op jit(solution)/shard_map/ppermute | solution.py:331
  21.2 19.0 %collective-permute-start.7 = (bf16[2,1024]{1,0:T(2,128)(2,1)S(1)}, bf16[2,1024]{1,0:T(2,128)(2,1)S(1)}, u32[]{:S(2)}, u32[]{:S(2)}) collective-permute-start(bf16[2,1024]{1,0:T(2,128)(2,1)S(1)} %get-tuple-element.53), channel_id=1, source_target_pairs={{0,14},{2,12},{4,10},{6,8},{8,6},{10,4},{12,2},{14,0},{1,15},{3,13... | collective-permute-start | bytes 12296 | tf_op jit(solution)/shard_map/ppermute | solution.py:331
  22.8 19.0 %collective-permute-start = (bf16[64,1024]{1,0:T(8,128)(2,1)S(1)}, bf16[64,1024]{1,0:T(8,128)(2,1)}, u32[]{:S(2)}, u32[]{:S(2)}) collective-permute-start(bf16[64,1024]{1,0:T(8,128)(2,1)S(1)} %get-tuple-element.59), channel_id=1, source_target_pairs={{0,14},{2,12},{4,10},{6,8},{8,6},{10,4},{12,2},{14,0},{1,15},{3,13... | collective-permute-start | bytes 393224 | tf_op jit(solution)/shard_map/ppermute | solution.py:303
  26.1 27.5 %collective-permute-start.8 = (bf16[64,1024]{1,0:T(8,128)(2,1)S(1)}, bf16[64,1024]{1,0:T(8,128)(2,1)}, u32[]{:S(2)}, u32[]{:S(2)}) collective-permute-start(bf16[64,1024]{1,0:T(8,128)(2,1)S(1)} %get-tuple-element.58), channel_id=1, source_target_pairs={{0,6},{2,4},{4,2},{6,0},{8,14},{10,12},{12,10},{14,8},{1,7},{3,5},... | collective-permute-start | bytes 393224 | tf_op jit(solution)/shard_map/ppermute | solution.py:303
  56.7 79.5 %all-to-all-start.1 = ((bf16[8,64,1024]{2,1,0:T(8,128)(2,1)}), bf16[8,64,1024]{2,1,0:T(8,128)(2,1)S(1)}, u32[]{:S(2)}, u32[]{:S(2)}) async-start(bf16[8,64,1024]{2,1,0:T(8,128)(2,1)} %shard_map.60), calls=%async_computation.1 | async-start | bytes 2097152 | tf_op jit(solution)/shard_map/all_to_all | solution.py:319
  65.0 25.3 %collective-permute-start.9 = (bf16[64,1024]{1,0:T(8,128)(2,1)S(1)}, bf16[64,1024]{1,0:T(8,128)(2,1)S(1)}, u32[]{:S(2)}, u32[]{:S(2)}) collective-permute-start(bf16[64,1024]{1,0:T(8,128)(2,1)S(1)} %get-tuple-element.56), channel_id=1, source_target_pairs={{0,12},{2,14},{4,8},{6,10},{8,4},{10,6},{12,0},{14,2},{1,13},{3,15... | collective-permute-start | bytes 393224 | tf_op jit(solution)/shard_map/ppermute | solution.py:303
  68.8 37.6 %collective-permute-start.12 = (bf16[64,1024]{1,0:T(8,128)(2,1)}, bf16[64,1024]{1,0:T(8,128)(2,1)}, u32[]{:S(2)}, u32[]{:S(2)}) collective-permute-start(bf16[64,1024]{1,0:T(8,128)(2,1)} %get-tuple-element.55), channel_id=1, source_target_pairs={{0,8},{2,10},{4,12},{6,14},{8,0},{10,2},{12,4},{14,6},{1,9},{3,11}... | collective-permute-start | bytes 393224 | tf_op jit(solution)/shard_map/ppermute | solution.py:303
  68.8 39.8 %collective-permute-start.13 = (bf16[64,1024]{1,0:T(8,128)(2,1)}, bf16[64,1024]{1,0:T(8,128)(2,1)}, u32[]{:S(2)}, u32[]{:S(2)}) collective-permute-start(bf16[64,1024]{1,0:T(8,128)(2,1)} %get-tuple-element.54), channel_id=1, source_target_pairs={{0,10},{2,8},{4,14},{6,12},{8,2},{10,0},{12,6},{14,4},{1,11},{3,9}... | collective-permute-start | bytes 393224 | tf_op jit(solution)/shard_map/ppermute | solution.py:303
  90.9 17.7 %collective-permute-start.10 = (bf16[64,1024]{1,0:T(8,128)(2,1)S(1)}, bf16[64,1024]{1,0:T(8,128)(2,1)}, u32[]{:S(2)}, u32[]{:S(2)}) collective-permute-start(bf16[64,1024]{1,0:T(8,128)(2,1)S(1)} %constant_dynamic-slice_fusion.3), channel_id=1, source_target_pairs={{0,2},{2,0},{4,6},{6,4},{8,10},{10,8},{12,14},{14,12},{1,3},{3,1},... | collective-permute-start | bytes 393224 | tf_op jit(solution)/shard_map/ppermute | solution.py:303
  92.4 18.0 %collective-permute-start.11 = (bf16[64,1024]{1,0:T(8,128)(2,1)S(1)}, bf16[64,1024]{1,0:T(8,128)(2,1)S(1)}, u32[]{:S(2)}, u32[]{:S(2)}) collective-permute-start(bf16[64,1024]{1,0:T(8,128)(2,1)S(1)} %constant_dynamic-slice_fusion.2), channel_id=1, source_target_pairs={{0,4},{2,6},{4,0},{6,2},{8,12},{10,14},{12,8},{14,10},{1,5},{3,7},... | collective-permute-start | bytes 393224 | tf_op jit(solution)/shard_map/ppermute | solution.py:303
  114.2 8.4 %collective-permute-start.14 = (bf16[64,1024]{1,0:T(8,128)(2,1)}, bf16[64,1024]{1,0:T(8,128)(2,1)S(1)}, u32[]{:S(2)}, u32[]{:S(2)}) collective-permute-start(bf16[64,1024]{1,0:T(8,128)(2,1)} %get-tuple-element.38), channel_id=1, source_target_pairs={{0,12},{2,14},{4,8},{6,10},{8,4},{10,6},{12,0},{14,2},{1,13},{3,15... | collective-permute-start | bytes 393224 | tf_op jit(solution)/shard_map/ppermute | solution.py:303
  115.3 11.0 %collective-permute-start.16 = (bf16[64,1024]{1,0:T(8,128)(2,1)}, bf16[64,1024]{1,0:T(8,128)(2,1)S(1)}, u32[]{:S(2)}, u32[]{:S(2)}) collective-permute-start(bf16[64,1024]{1,0:T(8,128)(2,1)} %get-tuple-element.42), channel_id=1, source_target_pairs={{0,14},{2,12},{4,10},{6,8},{8,6},{10,4},{12,2},{14,0},{1,15},{3,13... | collective-permute-start | bytes 393224 | tf_op jit(solution)/shard_map/ppermute | solution.py:303
  118.9 30.9 %collective-permute-start.18 = (bf16[64,1024]{1,0:T(8,128)(2,1)}, bf16[64,1024]{1,0:T(8,128)(2,1)S(1)}, u32[]{:S(2)}, u32[]{:S(2)}) collective-permute-start(bf16[64,1024]{1,0:T(8,128)(2,1)} %get-tuple-element.45), channel_id=1, source_target_pairs={{0,6},{2,4},{4,2},{6,0},{8,14},{10,12},{12,10},{14,8},{1,7},{3,5},... | collective-permute-start | bytes 393224 | tf_op jit(solution)/shard_map/ppermute | solution.py:303
  118.9 30.9 %collective-permute-start.19 = (bf16[64,1024]{1,0:T(8,128)(2,1)}, bf16[64,1024]{1,0:T(8,128)(2,1)S(1)}, u32[]{:S(2)}, u32[]{:S(2)}) collective-permute-start(bf16[64,1024]{1,0:T(8,128)(2,1)} %get-tuple-element.47), channel_id=1, source_target_pairs={{0,8},{2,10},{4,12},{6,14},{8,0},{10,2},{12,4},{14,6},{1,9},{3,11}... | collective-permute-start | bytes 393224 | tf_op jit(solution)/shard_map/ppermute | solution.py:303
  120.7 29.2 %collective-permute-start.20 = (bf16[64,1024]{1,0:T(8,128)(2,1)}, bf16[64,1024]{1,0:T(8,128)(2,1)S(1)}, u32[]{:S(2)}, u32[]{:S(2)}) collective-permute-start(bf16[64,1024]{1,0:T(8,128)(2,1)} %get-tuple-element.49), channel_id=1, source_target_pairs={{0,10},{2,8},{4,14},{6,12},{8,2},{10,0},{12,6},{14,4},{1,11},{3,9}... | collective-permute-start | bytes 393224 | tf_op jit(solution)/shard_map/ppermute | solution.py:303
  122.6 27.3 %collective-permute-start.15 = (bf16[64,1024]{1,0:T(8,128)(2,1)}, bf16[64,1024]{1,0:T(8,128)(2,1)S(1)}, u32[]{:S(2)}, u32[]{:S(2)}) collective-permute-start(bf16[64,1024]{1,0:T(8,128)(2,1)} %get-tuple-element.39), channel_id=1, source_target_pairs={{0,2},{2,0},{4,6},{6,4},{8,10},{10,8},{12,14},{14,12},{1,3},{3,1},... | collective-permute-start | bytes 393224 | tf_op jit(solution)/shard_map/ppermute | solution.py:303
  126.3 23.6 %collective-permute-start.17 = (bf16[64,1024]{1,0:T(8,128)(2,1)}, bf16[64,1024]{1,0:T(8,128)(2,1)S(1)}, u32[]{:S(2)}, u32[]{:S(2)}) collective-permute-start(bf16[64,1024]{1,0:T(8,128)(2,1)} %get-tuple-element.43), channel_id=1, source_target_pairs={{0,4},{2,6},{4,0},{6,2},{8,12},{10,14},{12,8},{14,10},{1,5},{3,7},... | collective-permute-start | bytes 393224 | tf_op jit(solution)/shard_map/ppermute | solution.py:303
  (11 other events, 74.0 us)

commit v4 on v0

--- a/solution.py
+++ b/solution.py
@@ -1,12 +1,17 @@
+import functools
 import math
 
 import jax
 import jax.numpy as jnp
 from jax import lax
+from jax.experimental import pallas as pl
+from jax.experimental.pallas import tpu as pltpu
 from jax.sharding import PartitionSpec as P
 
 DH = 128
 BS = 512
+BF16 = jnp.bfloat16
+F32 = jnp.float32
 
 
 def block_partial(query_block, key_block, value_block):
@@ -32,7 +37,7 @@
     return merged.astype(jnp.bfloat16)
 
 
-def per_device(query_rows, key_rows, value_rows, selection):
+def any_size(query_rows, key_rows, value_rows, selection):
     members = lax.axis_size("context")
     tok_rows, width = query_rows.shape
     blocks = tok_rows // BS
@@ -107,7 +112,182 @@
     return (attended, sort_logits)
 
 
+SCALE = math.log2(math.e) / math.sqrt(DH)
+EXTRA = 16
+
+
+def pack_kernel(heads, k_ref, chosen_ref, out_ref):
+    sums = jnp.sum(k_ref[...].astype(F32), axis=0, keepdims=True) / math.sqrt(BS)
+    pooled = sums.astype(BF16)
+    rows = jnp.concatenate([pooled[:, h * DH : (h + 1) * DH] for h in range(heads)], axis=0)
+    for h in range(heads):
+        out_ref[h, pl.ds(0, BS), :] = k_ref[:, pl.ds(h * DH, DH)]
+        out_ref[h, pl.ds(BS, EXTRA), :] = jnp.concatenate(
+            [rows, jnp.broadcast_to(chosen_ref[pl.ds(h, 1), :], (EXTRA - heads, DH))], axis=0
+        )
+
+
+def pack_keys(k, chosen):
+    tok, width = k.shape
+    heads = width // DH
+    return pl.pallas_call(
+        functools.partial(pack_kernel, heads),
+        out_shape=jax.ShapeDtypeStruct((heads, BS + EXTRA, DH), BF16),
+        compiler_params=pltpu.CompilerParams(vmem_limit_bytes=16 << 20),
+        cost_estimate=pl.CostEstimate(
+            flops=tok * width, transcendentals=0, bytes_accessed=4 * tok * width
+        ),
+    )(k, chosen)
+
+
+def split_kernel(heads, v_ref, out_ref):
+    for h in range(heads):
+        out_ref[h] = v_ref[:, pl.ds(h * DH, DH)]
+
+
+def split_heads(v):
+    tok, width = v.shape
+    heads = width // DH
+    return pl.pallas_call(
+        functools.partial(split_kernel, heads),
+        out_shape=jax.ShapeDtypeStruct((heads, tok, DH), BF16),
+        compiler_params=pltpu.CompilerParams(vmem_limit_bytes=16 << 20),
+        cost_estimate=pl.CostEstimate(
+            flops=0, transcendentals=0, bytes_accessed=4 * tok * width
+        ),
+    )(v)
+
+
+def attend_kernel(me_ref, chosen, q_ref, ko_ref, kf_ref, vo_ref, vf_ref, out_ref):
+    q = q_ref[...]
+
+    def part(keys, values):
+        s = lax.dot_general(q, keys, (((1,), (1,)), ((), ())), preferred_element_type=F32)
+        top = jnp.max(s, axis=1, keepdims=True) * SCALE
+        w = jnp.exp2(s * SCALE - top).astype(BF16)
+        total = jnp.sum(w.astype(F32), axis=1, keepdims=True)
+        return top, total, jnp.dot(w, values, preferred_element_type=F32)
+
+    own_max, own_total, own_sum = part(ko_ref[0], vo_ref[0])
+    far_max, far_total, far_sum = part(kf_ref[0], vf_ref[0])
+    joint = jnp.maximum(own_max, far_max)
+    own_e = jnp.exp2(own_max - joint)
+    far_e = jnp.exp2(far_max - joint)
+    inverse = 1.0 / (own_e * own_total + far_e * far_total)
+    out_ref[...] = ((own_e * inverse) * own_sum + (far_e * inverse) * far_sum).astype(BF16)
+
+
+def attend(me, chosen, d, q, keys, values):
+    own = pl.BlockSpec((1, BS, DH), lambda i, m, t: (m[0] ^ d, 0, 0))
+    far = pl.BlockSpec((1, BS, DH), lambda i, m, t: (t[m[0] ^ d], 0, 0))
+    rows = pl.BlockSpec((BS, DH), lambda i, m, t: (0, 0))
+    return pl.pallas_call(
+        attend_kernel,
+        grid_spec=pltpu.PrefetchScalarGridSpec(
+            num_scalar_prefetch=2,
+            grid=(1,),
+            in_specs=[rows, own, far, own, far],
+            out_specs=rows,
+        ),
+        out_shape=jax.ShapeDtypeStruct((BS, DH), BF16),
+        compiler_params=pltpu.CompilerParams(vmem_limit_bytes=16 << 20),
+        cost_estimate=pl.CostEstimate(
+            flops=8 * BS * BS * DH, transcendentals=2 * BS * BS, bytes_accessed=12 * BS * DH
+        ),
+    )(me, chosen, q, keys, keys, values, values)
+
+
+def join_kernel(members, me_ref, *refs):
+    pieces, out_ref = refs[:members], refs[members]
+    for d in range(members):
+        first = pl.multiple_of((me_ref[0] ^ d) * DH, DH)
+        out_ref[:, pl.ds(first, DH)] = pieces[d][...]
+
+
+def join_heads(me, pieces):
+    members = len(pieces)
+    tok = pieces[0].shape[0]
+    piece = pl.BlockSpec((tok, DH), lambda i, m: (0, 0))
+    return pl.pallas_call(
+        functools.partial(join_kernel, members),
+        grid_spec=pltpu.PrefetchScalarGridSpec(
+            num_scalar_prefetch=1,
+            grid=(1,),
+            in_specs=[piece] * members,
+            out_specs=pl.BlockSpec((tok, members * DH), lambda i, m: (0, 0)),
+        ),
+        out_shape=jax.ShapeDtypeStruct((tok, members * DH), BF16),
+        compiler_params=pltpu.CompilerParams(vmem_limit_bytes=16 << 20),
+        cost_estimate=pl.CostEstimate(
+            flops=0, transcendentals=0, bytes_accessed=4 * members * tok * DH
+        ),
+    )(me, *pieces)
+
+
+def after(x, *earlier):
+    return lax.optimization_barrier((x, *earlier))[0]
+
+
+IN_FLIGHT = 5
+BEFORE_VALUES = 5
+
+
+def by_heads(query_rows, key_rows, value_rows, selection):
+    members = lax.axis_size("context")
+    me = lax.axis_index("context")
+    tok, width = query_rows.shape
+    heads = width // DH
+    order = sorted(range(1, members), reverse=True)
+
+    def send(x, d):
+        return lax.ppermute(x, "context", [(i, i ^ d) for i in range(members)])
+
+    def swap(array):
+        return lax.all_to_all(array, "context", 0, 0, tiled=True)
+
+    def columns(array, d):
+        return lax.dynamic_slice_in_dim(array, (me ^ d) * DH, DH, axis=1)
+
+    chosen = jnp.broadcast_to(selection.astype(BF16), (heads, DH))
+    keys = swap(pack_keys(key_rows, chosen))
+    queries = [None] * members
+    arrived = []
+    for n, d in enumerate(order):
+        earlier = arrived[n - IN_FLIGHT : n - IN_FLIGHT + 1] if n >= IN_FLIGHT else []
+        queries[d] = send(columns(after(query_rows, *earlier), d), d)
+        arrived.append(queries[d])
+    queries[0] = columns(query_rows, 0)
+    values = swap(after(split_heads(value_rows), keys, *arrived[:BEFORE_VALUES]))
+
+    chosen = keys[:, BS + heads, 0].astype(jnp.int32)
+    here = me.astype(jnp.int32)[None]
+    outputs = [None] * members
+    for d in order + [0]:
+        outputs[d] = attend(here, chosen, d, queries[d], keys, values)
+        if d:
+            outputs[d] = send(outputs[d], d)
+    attended = join_heads(here, outputs)
+
+    pooled_q = (jnp.sum(query_rows, axis=0, dtype=F32) / math.sqrt(BS)).astype(BF16)
+    sort_logits = jnp.einsum(
+        "hd,chd->hc",
+        pooled_q.reshape(heads, DH),
+        keys[:, BS : BS + heads],
+        preferred_element_type=F32,
+    ) / math.sqrt(DH)
+    return attended, sort_logits.reshape(heads, 1, members)
+
+
 def solution(mesh):
+    members = mesh.shape["context"]
+
+    def per_device(query_rows, key_rows, value_rows, selection):
+        tok, width = query_rows.shape
+        fits = tok == BS and width == members * DH and members & (members - 1) == 0
+        if fits and members < EXTRA:
+            return by_heads(query_rows, key_rows, value_rows, selection)
+        return any_size(query_rows, key_rows, value_rows, selection)
+
     placed = (
         P(("groups", "context"), "tensor"),
         P(("groups", "context"), "tensor"),

time: 237 us -> 122 us (0.51)
  blocking collectives: 100 us -> 0 us
  local copies, waits for them, and re-layouts: 69.2 us -> 4.23 us
  waiting for transfers between devices: 0.01 us -> 59.7 us
  matrix products: 30.8 us -> 0.12 us
  starting transfers between devices: 15.9 us -> 36.3 us
  Pallas kernels: 0 us -> 17.3 us
  loops' own time: 15.1 us -> 0 us
    all_gather x2 -> x0, blocking collectives: 67.3 us -> none  [the longest x1 36.3 us: per_device(): lax.all_gather(pooled_k, 'context', axis=1, tiled=True)]
    gather x2 -> x0, local copies, waits for them, and re-layouts: 50.5 us -> none  [pick_rows(): grid[source_blk, source_dev, row_ids, head_ids]]
    ppermute x0 -> x14, waiting for transfers between devices: none -> 41.8 us  [send(): return lax.ppermute(x, 'context', [(i, i ^ d) for i in range(members)])]
    all_to_all x1 -> x0, blocking collectives: 33 us -> none  [per_device(): lax.all_to_all(spread_k, 'context', split_axis=1, concat_axis=1, tiled=True)]
    dot_general x33 -> x1, matrix products: 30.8 us -> 0.12 us  [by_heads(): jnp.einsum('hd,chd->hc', pooled_q.reshape(heads, DH), keys[:, BS:BS + hea...]
    ppermute x0 -> x14, starting transfers between devices: none -> 25.2 us  [send(): return lax.ppermute(x, 'context', [(i, i ^ d) for i in range(members)])]
    all_to_all x3 -> x2, waiting for transfers between devices: 0.01 us -> 17.9 us  [swap(): return lax.all_to_all(array, 'context', 0, 0, tiled=True)]
    pallas_call x0 -> x11, Pallas kernels: none -> 17.3 us  [the longest x8 13.5 us: attend(): pl.pallas_call(attend_kernel, grid_spec=pltpu.PrefetchScalarGridSpec(num_...]
  transfers between devices with their start and end apart: 3 -> 16, of which waited for: 0 -> 8; matrix products, arithmetic and copies ran while one was open for 25% -> 4% of each run, Pallas kernels for 0% -> 12%
where the time goes in v4:
time: 122 us; the launch traced here: 121 us
  waiting for transfers between devices  59.7 us (49%)
  starting transfers between devices  36.3 us (30%)
  Pallas kernels  17.3 us (14%)
  local copies, waits for them, and re-layouts  4.23 us (3%)
  other arithmetic  2.9 us (2%)
    ppermute x14, waiting for transfers between devices, send(): return lax.ppermute(x, 'context', [(i, i ^ d) for i in range(members)])  41.8 us
    ppermute x14, starting transfers between devices, send(): return lax.ppermute(x, 'context', [(i, i ^ d) for i in range(members)])  25.2 us
    all_to_all x2, waiting for transfers between devices, swap(): return lax.all_to_all(array, 'context', 0, 0, tiled=True)  17.9 us
    pallas_call x8, Pallas kernels, attend(): pl.pallas_call(attend_kernel, grid_spec=pltpu.PrefetchScalarGridSpec(num_...  13.5 us
    all_to_all x2, starting transfers between devices, swap(): return lax.all_to_all(array, 'context', 0, 0, tiled=True)  11.1 us
    dynamic_slice x4, local copies, waits for them, and re-layouts, columns(): return lax.dynamic_slice_in_dim(array, (me ^ d) * DH, DH, axis=1)  2.93 us
  transfers between devices with their start and end apart: 16, of which 8 were waited for; matrix products, arithmetic and copies ran while one was open for 4% of the time, Pallas kernels for 12%

profile of v4, /device:TPU:0, one launch (start us, length us, event | category | flops | bytes accessed | tf_op | source)
XLA Modules:
  0.0 121.4 jit_solution(4967465116812738922)
XLA Ops:
  3.9 7.4 %all-to-all-start = ((bf16[8,528,128]{2,1,0:T(8,128)(2,1)}), bf16[8,528,128]{2,1,0:T(8,128)(2,1)S(1)}, u32[]{:S(2)}, u32[]{:S(2)}) async-start(bf16[8,528,128]{2,1,0:T(8,128)(2,1)} %shard_map.59), calls=%async_computation | async-start | bytes 2162688 | tf_op jit(solution)/shard_map/all_to_all | solution.py:246
  11.6 4.7 %collective-permute-start = (bf16[512,128]{1,0:T(8,128)(2,1)S(1)}, bf16[512,128]{1,0:T(8,128)(2,1)S(1)}, u32[]{:S(2)}, u32[]{:S(2)}) collective-permute-start(bf16[512,128]{1,0:T(8,128)(2,1)S(1)} %get-tuple-element.16), channel_id=1, source_target_pairs={{0,14},{2,12},{4,10},{6,8},{8,6},{10,4},{12,2},{14,0},{1,15},{3,13... | collective-permute-start | bytes 393224 | tf_op jit(solution)/shard_map/ppermute | solution.py:243
  17.4 1.9 %collective-permute-start.3 = (bf16[512,128]{1,0:T(8,128)(2,1)S(1)}, bf16[512,128]{1,0:T(8,128)(2,1)S(1)}, u32[]{:S(2)}, u32[]{:S(2)}) collective-permute-start(bf16[512,128]{1,0:T(8,128)(2,1)S(1)} %get-tuple-element.13), channel_id=1, source_target_pairs={{0,8},{2,10},{4,12},{6,14},{8,0},{10,2},{12,4},{14,6},{1,9},{3,11}... | collective-permute-start | bytes 393224 | tf_op jit(solution)/shard_map/ppermute | solution.py:243
  19.3 2.3 %collective-permute-start.4 = (bf16[512,128]{1,0:T(8,128)(2,1)S(1)}, bf16[512,128]{1,0:T(8,128)(2,1)S(1)}, u32[]{:S(2)}, u32[]{:S(2)}) collective-permute-start(bf16[512,128]{1,0:T(8,128)(2,1)S(1)} %get-tuple-element.12), channel_id=1, source_target_pairs={{0,6},{2,4},{4,2},{6,0},{8,14},{10,12},{12,10},{14,8},{1,7},{3,5},... | collective-permute-start | bytes 393224 | tf_op jit(solution)/shard_map/ppermute | solution.py:243
  22.7 15.3 %collective-permute-done.q_ref = bf16[512,128]{1,0:T(8,128)(2,1)S(1)} collective-permute-done((bf16[512,128]{1,0:T(8,128)(2,1)S(1)}, bf16[512,128]{1,0:T(8,128)(2,1)S(1)}, u32[]{:S(2)}, u32[]{:S(2)}) %collective-permute-start) | collective-permute-done | bytes 131104 | tf_op jit(solution)/shard_map/ppermute | solution.py:243
  38.0 1.9 %collective-permute-done.1.q_ref = bf16[512,128]{1,0:T(8,128)(2,1)S(1)} collective-permute-done((bf16[512,128]{1,0:T(8,128)(2,1)S(1)}, bf16[512,128]{1,0:T(8,128)(2,1)S(1)}, u32[]{:S(2)}, u32[]{:S(2)}) %collective-permute-start.1) | collective-permute-done | bytes 131104 | tf_op jit(solution)/shard_map/ppermute | solution.py:243
  39.9 19.4 %collective-permute-done.2.q_ref = bf16[512,128]{1,0:T(8,128)(2,1)S(1)} collective-permute-done((bf16[512,128]{1,0:T(8,128)(2,1)S(1)}, bf16[512,128]{1,0:T(8,128)(2,1)S(1)}, u32[]{:S(2)}, u32[]{:S(2)}) %collective-permute-start.2) | collective-permute-done | bytes 131104 | tf_op jit(solution)/shard_map/ppermute | solution.py:243
  60.3 3.7 %all-to-all-start.1 = ((bf16[8,512,128]{2,1,0:T(8,128)(2,1)}), bf16[8,512,128]{2,1,0:T(8,128)(2,1)S(1)}, u32[]{:S(2)}, u32[]{:S(2)}) async-start(bf16[8,512,128]{2,1,0:T(8,128)(2,1)} %shard_map.60), calls=%async_computation.1 | async-start | bytes 2097152 | tf_op jit(solution)/shard_map/all_to_all | solution.py:246
  67.3 2.1 %collective-permute-start.7 = (bf16[512,128]{1,0:T(8,128)(2,1)S(1)}, bf16[512,128]{1,0:T(8,128)(2,1)S(1)}, u32[]{:S(2)}, u32[]{:S(2)}) collective-permute-start(bf16[512,128]{1,0:T(8,128)(2,1)S(1)} %constant_dynamic-slice_fusion), channel_id=1, source_target_pairs={{0,4},{2,6},{4,0},{6,2},{8,12},{10,14},{12,8},{14,10},{1,5},{3,7},... | collective-permute-start | bytes 393224 | tf_op jit(solution)/shard_map/ppermute | solution.py:243
  72.0 17.9 %all-to-all-done.1.vo_ref.vf_ref = bf16[8,512,128]{2,1,0:T(8,128)(2,1)S(1)} async-done(((bf16[8,512,128]{2,1,0:T(8,128)(2,1)}), bf16[8,512,128]{2,1,0:T(8,128)(2,1)S(1)}, u32[]{:S(2)}, u32[]{:S(2)}) %all-to-all-start.1) | async-done | bytes 1048608 | tf_op jit(solution)/shard_map/all_to_all | solution.py:246
  90.0 1.7 %shard_map.68 = bf16[512,128]{1,0:T(8,128)(2,1)S(1)} custom-call(s32[1]{0:T(128)} %bitcast.me_ref, s32[8]{0:T(128)S(1)} %fusion.2.chosen, bf16[512,128]{1,0:T(8,128)(2,1)S(1)} %collective-permute-done.q_ref, bf16[8,528,128]{2,1,0:T(8,128)(2,1)S(1)} %all-to-all-done.ko_ref.kf_ref, bf16[8,528,128]{2,1,0:T(8,128)(2,1)S(1)} %all-to-all-done.ko_ref.kf_ref, ...), custom_call_target="tpu_custom_call" | custom-call | flops 268435456 | bytes 786432 | tf_op jit(solution)/shard_map/pallas_call | solution.py:184
  91.6 2.5 %collective-permute-start.13 = (bf16[512,128]{1,0:T(8,128)(2,1)S(1)}, bf16[512,128]{1,0:T(8,128)(2,1)S(1)}, u32[]{:S(2)}, u32[]{:S(2)}) collective-permute-start(bf16[512,128]{1,0:T(8,128)(2,1)S(1)} %shard_map.68), channel_id=1, source_target_pairs={{0,14},{2,12},{4,10},{6,8},{8,6},{10,4},{12,2},{14,0},{1,15},{3,13... | collective-permute-start | bytes 393224 | tf_op jit(solution)/shard_map/ppermute | solution.py:243
  94.1 1.7 %shard_map.67 = bf16[512,128]{1,0:T(8,128)(2,1)S(1)} custom-call(s32[1]{0:T(128)} %bitcast.me_ref, s32[8]{0:T(128)S(1)} %fusion.2.chosen, bf16[512,128]{1,0:T(8,128)(2,1)S(1)} %collective-permute-done.1.q_ref, bf16[8,528,128]{2,1,0:T(8,128)(2,1)S(1)} %all-to-all-done.ko_ref.kf_ref, bf16[8,528,128]{2,1,0:T(8,128)(2,1)S(1)} %all-to-all-done.ko_ref.kf_ref, ...), custom_call_target="tpu_custom_call" | custom-call | flops 268435456 | bytes 786432 | tf_op jit(solution)/shard_map/pallas_call | solution.py:184
  95.8 2.3 %collective-permute-start.12 = (bf16[512,128]{1,0:T(8,128)(2,1)S(1)}, bf16[512,128]{1,0:T(8,128)(2,1)S(1)}, u32[]{:S(2)}, u32[]{:S(2)}) collective-permute-start(bf16[512,128]{1,0:T(8,128)(2,1)S(1)} %shard_map.67), channel_id=1, source_target_pairs={{0,12},{2,14},{4,8},{6,10},{8,4},{10,6},{12,0},{14,2},{1,13},{3,15... | collective-permute-start | bytes 393224 | tf_op jit(solution)/shard_map/ppermute | solution.py:243
  98.3 1.7 %shard_map.66 = bf16[512,128]{1,0:T(8,128)(2,1)S(1)} custom-call(s32[1]{0:T(128)} %bitcast.me_ref, s32[8]{0:T(128)S(1)} %fusion.2.chosen, bf16[512,128]{1,0:T(8,128)(2,1)S(1)} %collective-permute-done.2.q_ref, bf16[8,528,128]{2,1,0:T(8,128)(2,1)S(1)} %all-to-all-done.ko_ref.kf_ref, bf16[8,528,128]{2,1,0:T(8,128)(2,1)S(1)} %all-to-all-done.ko_ref.kf_ref, ...), custom_call_target="tpu_custom_call" | custom-call | flops 268435456 | bytes 786432 | tf_op jit(solution)/shard_map/pallas_call | solution.py:184
  100.0 1.7 %shard_map.65 = bf16[512,128]{1,0:T(8,128)(2,1)S(1)} custom-call(s32[1]{0:T(128)} %bitcast.me_ref, s32[8]{0:T(128)S(1)} %fusion.2.chosen, bf16[512,128]{1,0:T(8,128)(2,1)S(1)} %collective-permute-done.3.q_ref, bf16[8,528,128]{2,1,0:T(8,128)(2,1)S(1)} %all-to-all-done.ko_ref.kf_ref, bf16[8,528,128]{2,1,0:T(8,128)(2,1)S(1)} %all-to-all-done.ko_ref.kf_ref, ...), custom_call_target="tpu_custom_call" | custom-call | flops 268435456 | bytes 786432 | tf_op jit(solution)/shard_map/pallas_call | solution.py:184
  101.7 1.7 %shard_map.64 = bf16[512,128]{1,0:T(8,128)(2,1)S(1)} custom-call(s32[1]{0:T(128)} %bitcast.me_ref, s32[8]{0:T(128)S(1)} %fusion.2.chosen, bf16[512,128]{1,0:T(8,128)(2,1)S(1)} %collective-permute-done.4.q_ref, bf16[8,528,128]{2,1,0:T(8,128)(2,1)S(1)} %all-to-all-done.ko_ref.kf_ref, bf16[8,528,128]{2,1,0:T(8,128)(2,1)S(1)} %all-to-all-done.ko_ref.kf_ref, ...), custom_call_target="tpu_custom_call" | custom-call | flops 268435456 | bytes 786432 | tf_op jit(solution)/shard_map/pallas_call | solution.py:184
  103.4 3.0 %collective-permute-start.10 = (bf16[512,128]{1,0:T(8,128)(2,1)S(1)}, bf16[512,128]{1,0:T(8,128)(2,1)S(1)}, u32[]{:S(2)}, u32[]{:S(2)}) collective-permute-start(bf16[512,128]{1,0:T(8,128)(2,1)S(1)} %shard_map.65), channel_id=1, source_target_pairs={{0,8},{2,10},{4,12},{6,14},{8,0},{10,2},{12,4},{14,6},{1,9},{3,11}... | collective-permute-start | bytes 393224 | tf_op jit(solution)/shard_map/ppermute | solution.py:243
  106.5 1.7 %shard_map.63 = bf16[512,128]{1,0:T(8,128)(2,1)S(1)} custom-call(s32[1]{0:T(128)} %bitcast.me_ref, s32[8]{0:T(128)S(1)} %fusion.2.chosen, bf16[512,128]{1,0:T(8,128)(2,1)S(1)} %collective-permute-done.7.q_ref, bf16[8,528,128]{2,1,0:T(8,128)(2,1)S(1)} %all-to-all-done.ko_ref.kf_ref, bf16[8,528,128]{2,1,0:T(8,128)(2,1)S(1)} %all-to-all-done.ko_ref.kf_ref, ...), custom_call_target="tpu_custom_call" | custom-call | flops 268435456 | bytes 786432 | tf_op jit(solution)/shard_map/pallas_call | solution.py:184
  108.3 1.7 %shard_map.62 = bf16[512,128]{1,0:T(8,128)(2,1)S(1)} custom-call(s32[1]{0:T(128)} %bitcast.me_ref, s32[8]{0:T(128)S(1)} %fusion.2.chosen, bf16[512,128]{1,0:T(8,128)(2,1)S(1)} %collective-permute-done.5.q_ref, bf16[8,528,128]{2,1,0:T(8,128)(2,1)S(1)} %all-to-all-done.ko_ref.kf_ref, bf16[8,528,128]{2,1,0:T(8,128)(2,1)S(1)} %all-to-all-done.ko_ref.kf_ref, ...), custom_call_target="tpu_custom_call" | custom-call | flops 268435456 | bytes 786432 | tf_op jit(solution)/shard_map/pallas_call | solution.py:184
  110.0 2.9 %collective-permute-start.8 = (bf16[512,128]{1,0:T(8,128)(2,1)S(1)}, bf16[512,128]{1,0:T(8,128)(2,1)S(1)}, u32[]{:S(2)}, u32[]{:S(2)}) collective-permute-start(bf16[512,128]{1,0:T(8,128)(2,1)S(1)} %shard_map.63), channel_id=1, source_target_pairs={{0,4},{2,6},{4,0},{6,2},{8,12},{10,14},{12,8},{14,10},{1,5},{3,7},... | collective-permute-start | bytes 393224 | tf_op jit(solution)/shard_map/ppermute | solution.py:243
  114.1 1.7 %shard_map.61.refs_0_ = bf16[512,128]{1,0:T(8,128)(2,1)S(1)} custom-call(s32[1]{0:T(128)} %bitcast.me_ref, s32[8]{0:T(128)S(1)} %fusion.2.chosen, bf16[512,128]{1,0:T(8,128)(2,1)S(1)} %constant_dynamic-slice_fusion.7.q_ref, bf16[8,528,128]{2,1,0:T(8,128)(2,1)S(1)} %all-to-all-done.ko_ref.kf_ref, bf16[8,528,128]{2,1,0:T(8,128)(2,1)S(1)} %all-to-all-done.ko_ref.kf_ref, ...), custom_call_target="tpu_custom_call" | custom-call | flops 268435456 | bytes 786432 | tf_op jit(solution)/shard_map/pallas_call | solution.py:184
  116.0 2.4 %collective-permute-done.9.refs_3_ = bf16[512,128]{1,0:T(8,128)(2,1)S(1)} collective-permute-done((bf16[512,128]{1,0:T(8,128)(2,1)S(1)}, bf16[512,128]{1,0:T(8,128)(2,1)S(1)}, u32[]{:S(2)}, u32[]{:S(2)}) %collective-permute-start.9) | collective-permute-done | bytes 131104 | tf_op jit(solution)/shard_map/ppermute | solution.py:243
  118.4 1.7 %collective-permute-done.8.refs_2_ = bf16[512,128]{1,0:T(8,128)(2,1)S(1)} collective-permute-done((bf16[512,128]{1,0:T(8,128)(2,1)S(1)}, bf16[512,128]{1,0:T(8,128)(2,1)S(1)}, u32[]{:S(2)}, u32[]{:S(2)}) %collective-permute-start.8) | collective-permute-done | bytes 131104 | tf_op jit(solution)/shard_map/ppermute | solution.py:243
  (37 shorter events, 15.6 us)
Async XLA Ops:
  1.4 1.2 %copy-start = (bf16[512,1024]{1,0:T(8,128)(2,1)S(1)}, bf16[512,1024]{1,0:T(8,128)(2,1)}, u32[]{:S(2)}) copy-start(bf16[512,1024]{1,0:T(8,128)(2,1)} %k_ref.1) | copy-start | bytes 3145732
  3.9 7.4 %copy-start.2 = (bf16[512,1024]{1,0:T(8,128)(2,1)S(1)}, bf16[512,1024]{1,0:T(8,128)(2,1)}, u32[]{:S(2)}) copy-start(bf16[512,1024]{1,0:T(8,128)(2,1)} %param.4) | copy-start | bytes 3145732
  3.9 56.3 %all-to-all-start = ((bf16[8,528,128]{2,1,0:T(8,128)(2,1)}), bf16[8,528,128]{2,1,0:T(8,128)(2,1)S(1)}, u32[]{:S(2)}, u32[]{:S(2)}) async-start(bf16[8,528,128]{2,1,0:T(8,128)(2,1)} %shard_map.59), calls=%async_computation | async-start | bytes 2162688 | tf_op jit(solution)/shard_map/all_to_all | solution.py:246
  11.3 10.3 %copy-start.1 = (bf16[512,1024]{1,0:T(8,128)(2,1)S(1)}, bf16[512,1024]{1,0:T(8,128)(2,1)}, u32[]{:S(2)}) copy-start(bf16[512,1024]{1,0:T(8,128)(2,1)} %v_ref.1) | copy-start | bytes 3145732
  11.6 26.5 %collective-permute-start = (bf16[512,128]{1,0:T(8,128)(2,1)S(1)}, bf16[512,128]{1,0:T(8,128)(2,1)S(1)}, u32[]{:S(2)}, u32[]{:S(2)}) collective-permute-start(bf16[512,128]{1,0:T(8,128)(2,1)S(1)} %get-tuple-element.16), channel_id=1, source_target_pairs={{0,14},{2,12},{4,10},{6,8},{8,6},{10,4},{12,2},{14,0},{1,15},{3,13... | collective-permute-start | bytes 393224 | tf_op jit(solution)/shard_map/ppermute | solution.py:243
  16.3 23.6 %collective-permute-start.1 = (bf16[512,128]{1,0:T(8,128)(2,1)S(1)}, bf16[512,128]{1,0:T(8,128)(2,1)S(1)}, u32[]{:S(2)}, u32[]{:S(2)}) collective-permute-start(bf16[512,128]{1,0:T(8,128)(2,1)S(1)} %get-tuple-element.15), channel_id=1, source_target_pairs={{0,12},{2,14},{4,8},{6,10},{8,4},{10,6},{12,0},{14,2},{1,13},{3,15... | collective-permute-start | bytes 393224 | tf_op jit(solution)/shard_map/ppermute | solution.py:243
  16.9 42.5 %collective-permute-start.2 = (bf16[512,128]{1,0:T(8,128)(2,1)S(1)}, bf16[512,128]{1,0:T(8,128)(2,1)S(1)}, u32[]{:S(2)}, u32[]{:S(2)}) collective-permute-start(bf16[512,128]{1,0:T(8,128)(2,1)S(1)} %get-tuple-element.14), channel_id=1, source_target_pairs={{0,10},{2,8},{4,14},{6,12},{8,2},{10,0},{12,6},{14,4},{1,11},{3,9}... | collective-permute-start | bytes 393224 | tf_op jit(solution)/shard_map/ppermute | solution.py:243
  17.4 42.8 %collective-permute-start.3 = (bf16[512,128]{1,0:T(8,128)(2,1)S(1)}, bf16[512,128]{1,0:T(8,128)(2,1)S(1)}, u32[]{:S(2)}, u32[]{:S(2)}) collective-permute-start(bf16[512,128]{1,0:T(8,128)(2,1)S(1)} %get-tuple-element.13), channel_id=1, source_target_pairs={{0,8},{2,10},{4,12},{6,14},{8,0},{10,2},{12,4},{14,6},{1,9},{3,11}... | collective-permute-start | bytes 393224 | tf_op jit(solution)/shard_map/ppermute | solution.py:243
  19.3 41.0 %collective-permute-start.4 = (bf16[512,128]{1,0:T(8,128)(2,1)S(1)}, bf16[512,128]{1,0:T(8,128)(2,1)S(1)}, u32[]{:S(2)}, u32[]{:S(2)}) collective-permute-start(bf16[512,128]{1,0:T(8,128)(2,1)S(1)} %get-tuple-element.12), channel_id=1, source_target_pairs={{0,6},{2,4},{4,2},{6,0},{8,14},{10,12},{12,10},{14,8},{1,7},{3,5},... | collective-permute-start | bytes 393224 | tf_op jit(solution)/shard_map/ppermute | solution.py:243
  60.3 29.7 %all-to-all-start.1 = ((bf16[8,512,128]{2,1,0:T(8,128)(2,1)}), bf16[8,512,128]{2,1,0:T(8,128)(2,1)S(1)}, u32[]{:S(2)}, u32[]{:S(2)}) async-start(bf16[8,512,128]{2,1,0:T(8,128)(2,1)} %shard_map.60), calls=%async_computation.1 | async-start | bytes 2097152 | tf_op jit(solution)/shard_map/all_to_all | solution.py:246
  67.3 36.2 %collective-permute-start.7 = (bf16[512,128]{1,0:T(8,128)(2,1)S(1)}, bf16[512,128]{1,0:T(8,128)(2,1)S(1)}, u32[]{:S(2)}, u32[]{:S(2)}) collective-permute-start(bf16[512,128]{1,0:T(8,128)(2,1)S(1)} %constant_dynamic-slice_fusion), channel_id=1, source_target_pairs={{0,4},{2,6},{4,0},{6,2},{8,12},{10,14},{12,8},{14,10},{1,5},{3,7},... | collective-permute-start | bytes 393224 | tf_op jit(solution)/shard_map/ppermute | solution.py:243
  70.3 37.9 %collective-permute-start.5 = (bf16[512,128]{1,0:T(8,128)(2,1)S(1)}, bf16[512,128]{1,0:T(8,128)(2,1)S(1)}, u32[]{:S(2)}, u32[]{:S(2)}) collective-permute-start(bf16[512,128]{1,0:T(8,128)(2,1)S(1)} %constant_dynamic-slice_fusion.1), channel_id=1, source_target_pairs={{0,2},{2,0},{4,6},{6,4},{8,10},{10,8},{12,14},{14,12},{1,3},{3,1},... | collective-permute-start | bytes 393224 | tf_op jit(solution)/shard_map/ppermute | solution.py:243
  91.6 18.3 %collective-permute-start.13 = (bf16[512,128]{1,0:T(8,128)(2,1)S(1)}, bf16[512,128]{1,0:T(8,128)(2,1)S(1)}, u32[]{:S(2)}, u32[]{:S(2)}) collective-permute-start(bf16[512,128]{1,0:T(8,128)(2,1)S(1)} %shard_map.68), channel_id=1, source_target_pairs={{0,14},{2,12},{4,10},{6,8},{8,6},{10,4},{12,2},{14,0},{1,15},{3,13... | collective-permute-start | bytes 393224 | tf_op jit(solution)/shard_map/ppermute | solution.py:243
  95.8 17.1 %collective-permute-start.12 = (bf16[512,128]{1,0:T(8,128)(2,1)S(1)}, bf16[512,128]{1,0:T(8,128)(2,1)S(1)}, u32[]{:S(2)}, u32[]{:S(2)}) collective-permute-start(bf16[512,128]{1,0:T(8,128)(2,1)S(1)} %shard_map.67), channel_id=1, source_target_pairs={{0,12},{2,14},{4,8},{6,10},{8,4},{10,6},{12,0},{14,2},{1,13},{3,15... | collective-permute-start | bytes 393224 | tf_op jit(solution)/shard_map/ppermute | solution.py:243
  100.0 15.8 %collective-permute-start.11 = (bf16[512,128]{1,0:T(8,128)(2,1)S(1)}, bf16[512,128]{1,0:T(8,128)(2,1)S(1)}, u32[]{:S(2)}, u32[]{:S(2)}) collective-permute-start(bf16[512,128]{1,0:T(8,128)(2,1)S(1)} %shard_map.66), channel_id=1, source_target_pairs={{0,10},{2,8},{4,14},{6,12},{8,2},{10,0},{12,6},{14,4},{1,11},{3,9}... | collective-permute-start | bytes 393224 | tf_op jit(solution)/shard_map/ppermute | solution.py:243
  103.4 12.6 %collective-permute-start.10 = (bf16[512,128]{1,0:T(8,128)(2,1)S(1)}, bf16[512,128]{1,0:T(8,128)(2,1)S(1)}, u32[]{:S(2)}, u32[]{:S(2)}) collective-permute-start(bf16[512,128]{1,0:T(8,128)(2,1)S(1)} %shard_map.65), channel_id=1, source_target_pairs={{0,8},{2,10},{4,12},{6,14},{8,0},{10,2},{12,4},{14,6},{1,9},{3,11}... | collective-permute-start | bytes 393224 | tf_op jit(solution)/shard_map/ppermute | solution.py:243
  108.2 10.3 %collective-permute-start.9 = (bf16[512,128]{1,0:T(8,128)(2,1)S(1)}, bf16[512,128]{1,0:T(8,128)(2,1)S(1)}, u32[]{:S(2)}, u32[]{:S(2)}) collective-permute-start(bf16[512,128]{1,0:T(8,128)(2,1)S(1)} %shard_map.64), channel_id=1, source_target_pairs={{0,6},{2,4},{4,2},{6,0},{8,14},{10,12},{12,10},{14,8},{1,7},{3,5},... | collective-permute-start | bytes 393224 | tf_op jit(solution)/shard_map/ppermute | solution.py:243
  110.0 10.1 %collective-permute-start.8 = (bf16[512,128]{1,0:T(8,128)(2,1)S(1)}, bf16[512,128]{1,0:T(8,128)(2,1)S(1)}, u32[]{:S(2)}, u32[]{:S(2)}) collective-permute-start(bf16[512,128]{1,0:T(8,128)(2,1)S(1)} %shard_map.63), channel_id=1, source_target_pairs={{0,4},{2,6},{4,0},{6,2},{8,12},{10,14},{12,8},{14,10},{1,5},{3,7},... | collective-permute-start | bytes 393224 | tf_op jit(solution)/shard_map/ppermute | solution.py:243
  112.9 7.2 %collective-permute-start.6 = (bf16[512,128]{1,0:T(8,128)(2,1)S(1)}, bf16[512,128]{1,0:T(8,128)(2,1)S(1)}, u32[]{:S(2)}, u32[]{:S(2)}) collective-permute-start(bf16[512,128]{1,0:T(8,128)(2,1)S(1)} %shard_map.62), channel_id=1, source_target_pairs={{0,2},{2,0},{4,6},{6,4},{8,10},{10,8},{12,14},{14,12},{1,3},{3,1},... | collective-permute-start | bytes 393224 | tf_op jit(solution)/shard_map/ppermute | solution.py:243

commit v5 on v4

--- a/solution.py
+++ b/solution.py
@@ -113,52 +113,103 @@
 
 
 SCALE = math.log2(math.e) / math.sqrt(DH)
-EXTRA = 16
-
-
-def pack_kernel(heads, k_ref, chosen_ref, out_ref):
-    sums = jnp.sum(k_ref[...].astype(F32), axis=0, keepdims=True) / math.sqrt(BS)
-    pooled = sums.astype(BF16)
-    rows = jnp.concatenate([pooled[:, h * DH : (h + 1) * DH] for h in range(heads)], axis=0)
-    for h in range(heads):
-        out_ref[h, pl.ds(0, BS), :] = k_ref[:, pl.ds(h * DH, DH)]
-        out_ref[h, pl.ds(BS, EXTRA), :] = jnp.concatenate(
-            [rows, jnp.broadcast_to(chosen_ref[pl.ds(h, 1), :], (EXTRA - heads, DH))], axis=0
-        )
-
-
-def pack_keys(k, chosen):
-    tok, width = k.shape
+TILE = 8
+
+
+def pack_kernel(me_ref, k_ref, v_ref, out_ref):
+    out_ref[pl.ds(0, BS), :] = k_ref[...]
+    out_ref[pl.ds(BS, BS), :] = v_ref[...]
+
+
+def pack_head(me, d, k, v):
+    rows = 2 * BS
+    part = pl.BlockSpec((BS, DH), lambda i, m: (0, m[0] ^ d))
+    return pl.pallas_call(
+        pack_kernel,
+        grid_spec=pltpu.PrefetchScalarGridSpec(
+            num_scalar_prefetch=1,
+            grid=(1,),
+            in_specs=[part, part],
+            out_specs=pl.BlockSpec((rows, DH), lambda i, m: (0, 0)),
+        ),
+        out_shape=jax.ShapeDtypeStruct((rows, DH), BF16),
+        cost_estimate=pl.CostEstimate(
+            flops=0, transcendentals=0, bytes_accessed=4 * rows * DH
+        ),
+    )(me, k, v)
+
+
+def pooled(array):
+    return (jnp.sum(array.astype(F32), axis=0, keepdims=True) / math.sqrt(BS)).astype(BF16)
+
+
+def cut_kernel(heads, me_ref, q_ref, k_ref, chosen_ref, pooled_ref, *pieces):
+    def by_head(row):
+        return jnp.concatenate([row[:, h * DH : (h + 1) * DH] for h in range(heads)], axis=0)
+
+    pooled_ref[...] = by_head(pooled(q_ref[...]))
+    pooled_keys = by_head(pooled(k_ref[...]))
+    for d in range(heads):
+        first = pl.multiple_of((me_ref[0] ^ d) * DH, DH)
+        pieces[d][pl.ds(0, BS), :] = q_ref[:, pl.ds(first, DH)]
+        pieces[d][pl.ds(BS, heads), :] = pooled_keys
+        pieces[d][pl.ds(BS + heads, TILE), :] = chosen_ref[me_ref[0] ^ d]
+
+
+def cut_queries(me, q, k, chosen):
+    tok, width = q.shape
     heads = width // DH
-    return pl.pallas_call(
-        functools.partial(pack_kernel, heads),
-        out_shape=jax.ShapeDtypeStruct((heads, BS + EXTRA, DH), BF16),
-        compiler_params=pltpu.CompilerParams(vmem_limit_bytes=16 << 20),
+    whole = pl.BlockSpec((tok, width), lambda i, m: (0, 0))
+    piece = pl.BlockSpec((tok + heads + TILE, DH), lambda i, m: (0, 0))
+    return pl.pallas_call(
+        functools.partial(cut_kernel, heads),
+        grid_spec=pltpu.PrefetchScalarGridSpec(
+            num_scalar_prefetch=1,
+            grid=(1,),
+            in_specs=[whole, whole, pl.BlockSpec((heads, TILE, DH), lambda i, m: (0, 0, 0))],
+            out_specs=[pl.BlockSpec((heads, DH), lambda i, m: (0, 0))] + [piece] * heads,
+        ),
+        out_shape=[jax.ShapeDtypeStruct((heads, DH), BF16)]
+        + [jax.ShapeDtypeStruct((tok + heads + TILE, DH), BF16)] * heads,
+        compiler_params=pltpu.CompilerParams(vmem_limit_bytes=24 << 20),
         cost_estimate=pl.CostEstimate(
-            flops=tok * width, transcendentals=0, bytes_accessed=4 * tok * width
-        ),
-    )(k, chosen)
-
-
-def split_kernel(heads, v_ref, out_ref):
-    for h in range(heads):
-        out_ref[h] = v_ref[:, pl.ds(h * DH, DH)]
-
-
-def split_heads(v):
-    tok, width = v.shape
-    heads = width // DH
-    return pl.pallas_call(
-        functools.partial(split_kernel, heads),
-        out_shape=jax.ShapeDtypeStruct((heads, tok, DH), BF16),
-        compiler_params=pltpu.CompilerParams(vmem_limit_bytes=16 << 20),
-        cost_estimate=pl.CostEstimate(
-            flops=0, transcendentals=0, bytes_accessed=4 * tok * width
-        ),
-    )(v)
-
-
-def attend_kernel(me_ref, chosen, q_ref, ko_ref, kf_ref, vo_ref, vf_ref, out_ref):
+            flops=2 * tok * width, transcendentals=0, bytes_accessed=6 * tok * width
+        ),
+    )(me, q, k, chosen)
+
+
+def logits_kernel(heads, me_ref, pooled_ref, *refs):
+    pieces, out_ref = refs[:heads], refs[heads]
+    q = pooled_ref[...].astype(F32)
+    lane = lax.broadcasted_iota(jnp.int32, (heads, heads), 1)
+    logits = jnp.zeros((heads, heads), F32)
+    for d in range(heads):
+        one = jnp.sum(q * pieces[d][...].astype(F32), axis=1, keepdims=True)
+        logits = jnp.where(lane == (me_ref[0] ^ d), one / math.sqrt(DH), logits)
+    out_ref[...] = logits
+
+
+def logits_of(me, pooled_q, pieces):
+    heads = len(pieces)
+    rows = pl.BlockSpec((heads, DH), lambda i, m: (BS // heads, 0))
+    return pl.pallas_call(
+        functools.partial(logits_kernel, heads),
+        grid_spec=pltpu.PrefetchScalarGridSpec(
+            num_scalar_prefetch=1,
+            grid=(1,),
+            in_specs=[pl.BlockSpec((heads, DH), lambda i, m: (0, 0))] + [rows] * heads,
+            out_specs=pl.BlockSpec((heads, heads), lambda i, m: (0, 0)),
+        ),
+        out_shape=jax.ShapeDtypeStruct((heads, heads), F32),
+    )(me, pooled_q, *pieces)
+
+
+def attend_kernel(me_ref, q_ref, tile_ref, k_ref, v_ref, *refs):
+    packed, (out_ref, far_ref, sem) = refs[:-3], refs[-3:]
+    source = me_ref[0] ^ jnp.max(tile_ref[...].astype(F32)).astype(jnp.int32)
+    copies = [pltpu.make_async_copy(one, far_ref, sem) for one in packed]
+    for n, copy in enumerate(copies):
+        pl.when(source == n)(copy.start)
     q = q_ref[...]
 
     def part(keys, values):
@@ -168,8 +219,9 @@
         total = jnp.sum(w.astype(F32), axis=1, keepdims=True)
         return top, total, jnp.dot(w, values, preferred_element_type=F32)
 
-    own_max, own_total, own_sum = part(ko_ref[0], vo_ref[0])
-    far_max, far_total, far_sum = part(kf_ref[0], vf_ref[0])
+    own_max, own_total, own_sum = part(k_ref[...], v_ref[...])
+    copies[0].wait()
+    far_max, far_total, far_sum = part(far_ref[pl.ds(0, BS), :], far_ref[pl.ds(BS, BS), :])
     joint = jnp.maximum(own_max, far_max)
     own_e = jnp.exp2(own_max - joint)
     far_e = jnp.exp2(far_max - joint)
@@ -177,24 +229,31 @@
     out_ref[...] = ((own_e * inverse) * own_sum + (far_e * inverse) * far_sum).astype(BF16)
 
 
-def attend(me, chosen, d, q, keys, values):
-    own = pl.BlockSpec((1, BS, DH), lambda i, m, t: (m[0] ^ d, 0, 0))
-    far = pl.BlockSpec((1, BS, DH), lambda i, m, t: (t[m[0] ^ d], 0, 0))
-    rows = pl.BlockSpec((BS, DH), lambda i, m, t: (0, 0))
+def attend(me, d, q, packed):
+    def rows(n):
+        return pl.BlockSpec((BS, DH), lambda i, m: (n, 0))
+
     return pl.pallas_call(
         attend_kernel,
         grid_spec=pltpu.PrefetchScalarGridSpec(
-            num_scalar_prefetch=2,
-            grid=(1,),
-            in_specs=[rows, own, far, own, far],
-            out_specs=rows,
+            num_scalar_prefetch=1,
+            grid=(1,),
+            in_specs=[
+                rows(0),
+                pl.BlockSpec((TILE, DH), lambda i, m: (q.shape[0] // TILE - 1, 0)),
+                rows(0),
+                rows(1),
+            ]
+            + [pl.BlockSpec(memory_space=pl.ANY)] * len(packed),
+            out_specs=rows(0),
+            scratch_shapes=[pltpu.VMEM((2 * BS, DH), BF16), pltpu.SemaphoreType.DMA],
         ),
         out_shape=jax.ShapeDtypeStruct((BS, DH), BF16),
         compiler_params=pltpu.CompilerParams(vmem_limit_bytes=16 << 20),
         cost_estimate=pl.CostEstimate(
             flops=8 * BS * BS * DH, transcendentals=2 * BS * BS, bytes_accessed=12 * BS * DH
         ),
-    )(me, chosen, q, keys, keys, values, values)
+    )(me, q, q, packed[d], packed[d], *packed)
 
 
 def join_kernel(members, me_ref, *refs):
@@ -229,7 +288,6 @@
 
 
 IN_FLIGHT = 5
-BEFORE_VALUES = 5
 
 
 def by_heads(query_rows, key_rows, value_rows, selection):
@@ -237,44 +295,36 @@
     me = lax.axis_index("context")
     tok, width = query_rows.shape
     heads = width // DH
-    order = sorted(range(1, members), reverse=True)
-
-    def send(x, d):
-        return lax.ppermute(x, "context", [(i, i ^ d) for i in range(members)])
-
-    def swap(array):
-        return lax.all_to_all(array, "context", 0, 0, tiled=True)
-
-    def columns(array, d):
-        return lax.dynamic_slice_in_dim(array, (me ^ d) * DH, DH, axis=1)
-
-    chosen = jnp.broadcast_to(selection.astype(BF16), (heads, DH))
-    keys = swap(pack_keys(key_rows, chosen))
-    queries = [None] * members
+    here = me.astype(jnp.int32)[None]
+    near = list(range(1, members // 2))
+    far = list(range(members // 2, members))
     arrived = []
-    for n, d in enumerate(order):
-        earlier = arrived[n - IN_FLIGHT : n - IN_FLIGHT + 1] if n >= IN_FLIGHT else []
-        queries[d] = send(columns(after(query_rows, *earlier), d), d)
-        arrived.append(queries[d])
-    queries[0] = columns(query_rows, 0)
-    values = swap(after(split_heads(value_rows), keys, *arrived[:BEFORE_VALUES]))
-
-    chosen = keys[:, BS + heads, 0].astype(jnp.int32)
-    here = me.astype(jnp.int32)[None]
+
+    def exchange(pieces, order):
+        got = list(pieces)
+        for d in order:
+            earlier = arrived[-IN_FLIGHT:][:1] if len(arrived) >= IN_FLIGHT else []
+            got[d] = lax.ppermute(
+                after(pieces[d], *earlier), "context", [(i, i ^ d) for i in range(members)]
+            )
+            arrived.append(got[d])
+        return got
+
+    packed = [pack_head(here, d, key_rows, value_rows) for d in range(members)]
+    packed = exchange(packed, far[::-1] + near)
+    chosen = jnp.broadcast_to(selection.astype(BF16)[:, :, None], (heads, TILE, DH))
+    pooled_q, *pieces = cut_queries(here, after(query_rows, arrived[0]), key_rows, chosen)
+    queries = exchange(pieces, far[::-1] + near)
+    sort_logits = logits_of(here, pooled_q, queries)
+
     outputs = [None] * members
-    for d in order + [0]:
-        outputs[d] = attend(here, chosen, d, queries[d], keys, values)
+    for d in far[::-1] + near + [0]:
+        outputs[d] = attend(here, d, queries[d], packed)
         if d:
-            outputs[d] = send(outputs[d], d)
+            outputs[d] = lax.ppermute(
+                outputs[d], "context", [(i, i ^ d) for i in range(members)]
+            )
     attended = join_heads(here, outputs)
-
-    pooled_q = (jnp.sum(query_rows, axis=0, dtype=F32) / math.sqrt(BS)).astype(BF16)
-    sort_logits = jnp.einsum(
-        "hd,chd->hc",
-        pooled_q.reshape(heads, DH),
-        keys[:, BS : BS + heads],
-        preferred_element_type=F32,
-    ) / math.sqrt(DH)
     return attended, sort_logits.reshape(heads, 1, members)
 
 
@@ -284,7 +334,7 @@
     def per_device(query_rows, key_rows, value_rows, selection):
         tok, width = query_rows.shape
         fits = tok == BS and width == members * DH and members & (members - 1) == 0
-        if fits and members < EXTRA:
+        if fits and members == TILE:
             return by_heads(query_rows, key_rows, value_rows, selection)
         return any_size(query_rows, key_rows, value_rows, selection)
 

time: 122 us -> 107 us (0.88)
  waiting for transfers between devices: 59.7 us -> 10.3 us
  starting transfers between devices: 36.3 us -> 58.4 us
  Pallas kernels: 17.3 us -> 34 us
  other arithmetic: 2.9 us -> 0.01 us
  local copies, waits for them, and re-layouts: 4.23 us -> 2.89 us
    ppermute x14 -> x21, starting transfers between devices: 25.2 us -> 58.4 us  [the longest x14 47 us: exchange(): lax.ppermute(after(pieces[d], *earlier), 'context', [(i, i ^ d) for i in...]
    ppermute x14 -> x21, waiting for transfers between devices: 41.8 us -> 10.3 us  [the longest x14 9.66 us: exchange(): lax.ppermute(after(pieces[d], *earlier), 'context', [(i, i ^ d) for i in...]
    all_to_all x2 -> x0, waiting for transfers between devices: 17.9 us -> none  [swap(): return lax.all_to_all(array, 'context', 0, 0, tiled=True)]
    pallas_call x2 -> x10, Pallas kernels: 2.5 us -> 16.3 us  [the longest x8 13.6 us: pack_head(): pl.pallas_call(pack_kernel, grid_spec=pltpu.PrefetchScalarGridSpec(num_sc...]
    all_to_all x2 -> x0, starting transfers between devices: 11.1 us -> none  [swap(): return lax.all_to_all(array, 'context', 0, 0, tiled=True)]
    dynamic_slice x4 -> x0, local copies, waits for them, and re-layouts: 2.93 us -> none  [columns(): return lax.dynamic_slice_in_dim(array, (me ^ d) * DH, DH, axis=1)]
    pallas_call x8, Pallas kernels: 13.5 us -> 16.4 us  [attend(): pl.pallas_call(attend_kernel, grid_spec=pltpu.PrefetchScalarGridSpec(num_...]
    unnamed x6 -> x28, local copies, waits for them, and re-layouts: 1.23 us -> 2.81 us
  transfers between devices with their start and end apart: 16 -> 21, of which waited for: 8 -> 4; matrix products, arithmetic and copies ran while one was open for 4% -> 0% of each run, Pallas kernels for 12% -> 29%
where the time goes in v5:
time: 107 us
  starting transfers between devices  58.4 us (55%)
  Pallas kernels  34 us (32%)
  waiting for transfers between devices  10.3 us (10%)
  local copies, waits for them, and re-layouts  2.89 us (3%)
    ppermute x14, starting transfers between devices, exchange(): lax.ppermute(after(pieces[d], *earlier), 'context', [(i, i ^ d) for i in...  47 us
    pallas_call x8, Pallas kernels, attend(): pl.pallas_call(attend_kernel, grid_spec=pltpu.PrefetchScalarGridSpec(num_...  16.4 us
    pallas_call x8, Pallas kernels, pack_head(): pl.pallas_call(pack_kernel, grid_spec=pltpu.PrefetchScalarGridSpec(num_sc...  13.6 us
    ppermute x7, starting transfers between devices, by_heads(): lax.ppermute(outputs[d], 'context', [(i, i ^ d) for i in range(members)])  11.5 us
    ppermute x14, waiting for transfers between devices, exchange(): lax.ppermute(after(pieces[d], *earlier), 'context', [(i, i ^ d) for i in...  9.66 us
    unnamed x28, local copies, waits for them, and re-layouts  2.81 us
  transfers between devices with their start and end apart: 21, of which 4 were waited for; matrix products, arithmetic and copies ran while one was open for 0% of the time, Pallas kernels for 29%

profile of v5, /device:TPU:0, one launch (start us, length us, event | category | flops | bytes accessed | tf_op | source)
XLA Modules:
  0.0 106.5 jit_solution(17996318013599929121)
XLA Ops:
  2.3 6.0 %collective-permute-start = (bf16[1024,128]{1,0:T(8,128)(2,1)}, bf16[1024,128]{1,0:T(8,128)(2,1)S(1)}, u32[]{:S(2)}, u32[]{:S(2)}) collective-permute-start(bf16[1024,128]{1,0:T(8,128)(2,1)} %shard_map.59), channel_id=1, source_target_pairs={{0,14},{2,12},{4,10},{6,8},{8,6},{10,4},{12,2},{14,0},{1,15},{3,13... | collective-permute-start | bytes 786440 | tf_op jit(solution)/shard_map/ppermute | solution.py:307
  12.7 1.7 %shard_map.67 = bf16[1024,128]{1,0:T(8,128)(2,1)} custom-call(s32[1]{0:T(128)} %bitcast.me_ref, bf16[512,1024]{1,0:T(8,128)(2,1)} %k_ref.17, bf16[512,1024]{1,0:T(8,128)(2,1)} %v_ref.15), custom_call_target="tpu_custom_call" | custom-call | bytes 524288 | tf_op jit(solution)/shard_map/pallas_call | solution.py:127
  14.4 1.9 %collective-permute-start.6 = (bf16[1024,128]{1,0:T(8,128)(2,1)}, bf16[1024,128]{1,0:T(8,128)(2,1)S(1)}, u32[]{:S(2)}, u32[]{:S(2)}) collective-permute-start(bf16[1024,128]{1,0:T(8,128)(2,1)} %shard_map.67), channel_id=1, source_target_pairs={{0,10},{2,8},{4,14},{6,12},{8,2},{10,0},{12,6},{14,4},{1,11},{3,9}... | collective-permute-start | bytes 786440 | tf_op jit(solution)/shard_map/ppermute | solution.py:307
  21.4 1.8 %shard_map.64 = bf16[1024,128]{1,0:T(8,128)(2,1)} custom-call(s32[1]{0:T(128)} %bitcast.me_ref, bf16[512,1024]{1,0:T(8,128)(2,1)} %k_ref.17, bf16[512,1024]{1,0:T(8,128)(2,1)} %v_ref.15), custom_call_target="tpu_custom_call" | custom-call | bytes 524288 | tf_op jit(solution)/shard_map/pallas_call | solution.py:127
  23.2 14.9 %collective-permute-start.2 = (bf16[1024,128]{1,0:T(8,128)(2,1)}, bf16[1024,128]{1,0:T(8,128)(2,1)S(1)}, u32[]{:S(2)}, u32[]{:S(2)}) collective-permute-start(bf16[1024,128]{1,0:T(8,128)(2,1)} %shard_map.63), channel_id=1, source_target_pairs={{0,4},{2,6},{4,0},{6,2},{8,12},{10,14},{12,8},{14,10},{1,5},{3,7},... | collective-permute-start | bytes 786440 | tf_op jit(solution)/shard_map/ppermute | solution.py:307
  38.0 5.6 %collective-permute-start.4 = (bf16[1024,128]{1,0:T(8,128)(2,1)}, bf16[1024,128]{1,0:T(8,128)(2,1)S(1)}, u32[]{:S(2)}, u32[]{:S(2)}) collective-permute-start(bf16[1024,128]{1,0:T(8,128)(2,1)} %shard_map.64), channel_id=1, source_target_pairs={{0,6},{2,4},{4,2},{6,0},{8,14},{10,12},{12,10},{14,8},{1,7},{3,5},... | collective-permute-start | bytes 786440 | tf_op jit(solution)/shard_map/ppermute | solution.py:307
  46.8 1.9 %collective-permute-done.5.refs_4_.k_ref.v_ref = bf16[1024,128]{1,0:T(8,128)(2,1)S(1)} collective-permute-done((bf16[1024,128]{1,0:T(8,128)(2,1)}, bf16[1024,128]{1,0:T(8,128)(2,1)S(1)}, u32[]{:S(2)}, u32[]{:S(2)}) %collective-permute-start.5) | collective-permute-done | bytes 262176 | tf_op jit(solution)/shard_map/ppermute | solution.py:307
  48.7 2.7 %collective-permute-start.12 = (bf16[528,128]{1,0:T(8,128)(2,1)S(1)}, bf16[528,128]{1,0:T(8,128)(2,1)S(1)}, u32[]{:S(2)}, u32[]{:S(2)}) collective-permute-start(bf16[528,128]{1,0:T(8,128)(2,1)S(1)} %get-tuple-element.33), channel_id=1, source_target_pairs={{0,12},{2,14},{4,8},{6,10},{8,4},{10,6},{12,0},{14,2},{1,13},{3,15... | collective-permute-start | bytes 405512 | tf_op jit(solution)/shard_map/ppermute | solution.py:307
  51.4 5.8 %collective-permute-done.6.refs_5_.k_ref.v_ref = bf16[1024,128]{1,0:T(8,128)(2,1)S(1)} collective-permute-done((bf16[1024,128]{1,0:T(8,128)(2,1)}, bf16[1024,128]{1,0:T(8,128)(2,1)S(1)}, u32[]{:S(2)}, u32[]{:S(2)}) %collective-permute-start.6) | collective-permute-done | bytes 262176 | tf_op jit(solution)/shard_map/ppermute | solution.py:307
  57.2 3.5 %collective-permute-start.9 = (bf16[528,128]{1,0:T(8,128)(2,1)S(1)}, bf16[528,128]{1,0:T(8,128)(2,1)S(1)}, u32[]{:S(2)}, u32[]{:S(2)}) collective-permute-start(bf16[528,128]{1,0:T(8,128)(2,1)S(1)} %get-tuple-element.29), channel_id=1, source_target_pairs={{0,14},{2,12},{4,10},{6,8},{8,6},{10,4},{12,2},{14,0},{1,15},{3,13... | collective-permute-start | bytes 405512 | tf_op jit(solution)/shard_map/ppermute | solution.py:307
  60.8 2.8 %collective-permute-start.13 = (bf16[528,128]{1,0:T(8,128)(2,1)S(1)}, bf16[528,128]{1,0:T(8,128)(2,1)S(1)}, u32[]{:S(2)}, u32[]{:S(2)}) collective-permute-start(bf16[528,128]{1,0:T(8,128)(2,1)S(1)} %get-tuple-element.34), channel_id=1, source_target_pairs={{0,6},{2,4},{4,2},{6,0},{8,14},{10,12},{12,10},{14,8},{1,7},{3,5},... | collective-permute-start | bytes 405512 | tf_op jit(solution)/shard_map/ppermute | solution.py:307
  63.6 1.9 %collective-permute-done.9.q_ref.tile_ref.refs_7_ = bf16[528,128]{1,0:T(8,128)(2,1)S(1)} collective-permute-done((bf16[528,128]{1,0:T(8,128)(2,1)S(1)}, bf16[528,128]{1,0:T(8,128)(2,1)S(1)}, u32[]{:S(2)}, u32[]{:S(2)}) %collective-permute-start.9) | collective-permute-done | bytes 135200 | tf_op jit(solution)/shard_map/ppermute | solution.py:307
  65.5 4.5 %collective-permute-start.10 = (bf16[528,128]{1,0:T(8,128)(2,1)S(1)}, bf16[528,128]{1,0:T(8,128)(2,1)S(1)}, u32[]{:S(2)}, u32[]{:S(2)}) collective-permute-start(bf16[528,128]{1,0:T(8,128)(2,1)S(1)} %get-tuple-element.30), channel_id=1, source_target_pairs={{0,4},{2,6},{4,0},{6,2},{8,12},{10,14},{12,8},{14,10},{1,5},{3,7},... | collective-permute-start | bytes 405512 | tf_op jit(solution)/shard_map/ppermute | solution.py:307
  75.1 1.9 %shard_map.74 = bf16[512,128]{1,0:T(8,128)(2,1)S(1)} custom-call(s32[1]{0:T(128)} %bitcast.me_ref, bf16[528,128]{1,0:T(8,128)(2,1)S(1)} %collective-permute-done.12.q_ref.tile_ref.refs_6_, bf16[528,128]{1,0:T(8,128)(2,1)S(1)} %collective-permute-done.12.q_ref.tile_ref.refs_6_, bf16[1024,128]{1,0:T(8,128)(2,1)S(1)} %collective-permute-done.3.refs_6_.k_ref.v_ref, ...), custom_call_target="tpu_custom_call" | custom-call | flops 268435456 | bytes 786432 | tf_op jit(solution)/shard_map/pallas_call | solution.py:236
  76.9 1.9 %shard_map.75 = bf16[512,128]{1,0:T(8,128)(2,1)S(1)} custom-call(s32[1]{0:T(128)} %bitcast.me_ref, bf16[528,128]{1,0:T(8,128)(2,1)S(1)} %collective-permute-done.9.q_ref.tile_ref.refs_7_, bf16[528,128]{1,0:T(8,128)(2,1)S(1)} %collective-permute-done.9.q_ref.tile_ref.refs_7_, bf16[1024,128]{1,0:T(8,128)(2,1)S(1)} %collective-permute-done.refs_7_.k_ref.v_ref, ...), custom_call_target="tpu_custom_call" | custom-call | flops 268435456 | bytes 786432 | tf_op jit(solution)/shard_map/pallas_call | solution.py:236
  80.3 2.7 %collective-permute-start.20 = (bf16[512,128]{1,0:T(8,128)(2,1)S(1)}, bf16[512,128]{1,0:T(8,128)(2,1)S(1)}, u32[]{:S(2)}, u32[]{:S(2)}) collective-permute-start(bf16[512,128]{1,0:T(8,128)(2,1)S(1)} %shard_map.75), channel_id=1, source_target_pairs={{0,14},{2,12},{4,10},{6,8},{8,6},{10,4},{12,2},{14,0},{1,15},{3,13... | collective-permute-start | bytes 393224 | tf_op jit(solution)/shard_map/ppermute | solution.py:324
  83.0 1.9 %shard_map.73 = bf16[512,128]{1,0:T(8,128)(2,1)S(1)} custom-call(s32[1]{0:T(128)} %bitcast.me_ref, bf16[528,128]{1,0:T(8,128)(2,1)S(1)} %collective-permute-done.17.q_ref.tile_ref.refs_5_, bf16[528,128]{1,0:T(8,128)(2,1)S(1)} %collective-permute-done.17.q_ref.tile_ref.refs_5_, bf16[1024,128]{1,0:T(8,128)(2,1)S(1)} %collective-permute-done.6.refs_5_.k_ref.v_ref, ...), custom_call_target="tpu_custom_call" | custom-call | flops 268435456 | bytes 786432 | tf_op jit(solution)/shard_map/pallas_call | solution.py:236
  84.9 1.9 %shard_map.71 = bf16[512,128]{1,0:T(8,128)(2,1)S(1)} custom-call(s32[1]{0:T(128)} %bitcast.me_ref, bf16[528,128]{1,0:T(8,128)(2,1)S(1)} %collective-permute-done.13.q_ref.tile_ref.refs_3_, bf16[528,128]{1,0:T(8,128)(2,1)S(1)} %collective-permute-done.13.q_ref.tile_ref.refs_3_, bf16[1024,128]{1,0:T(8,128)(2,1)S(1)} %collective-permute-done.4.refs_3_.k_ref.v_ref, ...), custom_call_target="tpu_custom_call" | custom-call | flops 268435456 | bytes 786432 | tf_op jit(solution)/shard_map/pallas_call | solution.py:236
  87.4 1.9 %shard_map.70 = bf16[512,128]{1,0:T(8,128)(2,1)S(1)} custom-call(s32[1]{0:T(128)} %bitcast.me_ref, bf16[528,128]{1,0:T(8,128)(2,1)S(1)} %collective-permute-done.10.q_ref.tile_ref.refs_2_, bf16[528,128]{1,0:T(8,128)(2,1)S(1)} %collective-permute-done.10.q_ref.tile_ref.refs_2_, bf16[1024,128]{1,0:T(8,128)(2,1)S(1)} %collective-permute-done.2.refs_2_.k_ref.v_ref, ...), custom_call_target="tpu_custom_call" | custom-call | flops 268435456 | bytes 786432 | tf_op jit(solution)/shard_map/pallas_call | solution.py:236
  89.3 2.3 %collective-permute-start.14 = (bf16[512,128]{1,0:T(8,128)(2,1)S(1)}, bf16[512,128]{1,0:T(8,128)(2,1)S(1)}, u32[]{:S(2)}, u32[]{:S(2)}) collective-permute-start(bf16[512,128]{1,0:T(8,128)(2,1)S(1)} %shard_map.71), channel_id=1, source_target_pairs={{0,6},{2,4},{4,2},{6,0},{8,14},{10,12},{12,10},{14,8},{1,7},{3,5},... | collective-permute-start | bytes 393224 | tf_op jit(solution)/shard_map/ppermute | solution.py:324
  91.7 2.5 %shard_map.72 = bf16[512,128]{1,0:T(8,128)(2,1)} custom-call(s32[1]{0:T(128)} %bitcast.me_ref, bf16[528,128]{1,0:T(8,128)(2,1)S(1)} %collective-permute-done.15.q_ref.tile_ref.refs_4_, bf16[528,128]{1,0:T(8,128)(2,1)S(1)} %collective-permute-done.15.q_ref.tile_ref.refs_4_, bf16[1024,128]{1,0:T(8,128)(2,1)S(1)} %collective-permute-done.5.refs_4_.k_ref.v_ref, ...), custom_call_target="tpu_custom_call" | custom-call | flops 268435456 | bytes 786432 | tf_op jit(solution)/shard_map/pallas_call | solution.py:236
  94.3 2.7 %shard_map.69 = bf16[512,128]{1,0:T(8,128)(2,1)} custom-call(s32[1]{0:T(128)} %bitcast.me_ref, bf16[528,128]{1,0:T(8,128)(2,1)S(1)} %collective-permute-done.7.q_ref.tile_ref.refs_1_, bf16[528,128]{1,0:T(8,128)(2,1)S(1)} %collective-permute-done.7.q_ref.tile_ref.refs_1_, bf16[1024,128]{1,0:T(8,128)(2,1)S(1)} %collective-permute-done.1.refs_1_.k_ref.v_ref, ...), custom_call_target="tpu_custom_call" | custom-call | flops 268435456 | bytes 786432 | tf_op jit(solution)/shard_map/pallas_call | solution.py:236
  97.0 3.0 %collective-permute-start.16 = (bf16[512,128]{1,0:T(8,128)(2,1)}, bf16[512,128]{1,0:T(8,128)(2,1)S(1)}, u32[]{:S(2)}, u32[]{:S(2)}) collective-permute-start(bf16[512,128]{1,0:T(8,128)(2,1)} %shard_map.72), channel_id=1, source_target_pairs={{0,8},{2,10},{4,12},{6,14},{8,0},{10,2},{12,4},{14,6},{1,9},{3,11}... | collective-permute-start | bytes 393224 | tf_op jit(solution)/shard_map/ppermute | solution.py:324
  101.3 1.9 %shard_map.68.refs_0_ = bf16[512,128]{1,0:T(8,128)(2,1)S(1)} custom-call(s32[1]{0:T(128)} %bitcast.me_ref, bf16[528,128]{1,0:T(8,128)(2,1)S(1)} %get-tuple-element.22.q_ref.tile_ref.refs_0_, bf16[528,128]{1,0:T(8,128)(2,1)S(1)} %get-tuple-element.22.q_ref.tile_ref.refs_0_, bf16[1024,128]{1,0:T(8,128)(2,1)S(1)} %copy-done.2, bf16[1024,128]{1,0:T(8,128)(2,1)S(1)} %copy-done.2, ...), custom_call_target="tpu_custom_call" | custom-call | flops 268435456 | bytes 786432 | tf_op jit(solution)/shard_map/pallas_call | solution.py:236
  (67 shorter events, 26.2 us)
Async XLA Ops:
  2.3 20.8 %collective-permute-start = (bf16[1024,128]{1,0:T(8,128)(2,1)}, bf16[1024,128]{1,0:T(8,128)(2,1)S(1)}, u32[]{:S(2)}, u32[]{:S(2)}) collective-permute-start(bf16[1024,128]{1,0:T(8,128)(2,1)} %shard_map.59), channel_id=1, source_target_pairs={{0,14},{2,12},{4,10},{6,8},{8,6},{10,4},{12,2},{14,0},{1,15},{3,13... | collective-permute-start | bytes 786440 | tf_op jit(solution)/shard_map/ppermute | solution.py:307
  10.0 28.0 %collective-permute-start.3 = (bf16[1024,128]{1,0:T(8,128)(2,1)}, bf16[1024,128]{1,0:T(8,128)(2,1)S(1)}, u32[]{:S(2)}, u32[]{:S(2)}) collective-permute-start(bf16[1024,128]{1,0:T(8,128)(2,1)} %shard_map.65), channel_id=1, source_target_pairs={{0,12},{2,14},{4,8},{6,10},{8,4},{10,6},{12,0},{14,2},{1,13},{3,15... | collective-permute-start | bytes 786440 | tf_op jit(solution)/shard_map/ppermute | solution.py:307
  11.9 36.8 %collective-permute-start.5 = (bf16[1024,128]{1,0:T(8,128)(2,1)}, bf16[1024,128]{1,0:T(8,128)(2,1)S(1)}, u32[]{:S(2)}, u32[]{:S(2)}) collective-permute-start(bf16[1024,128]{1,0:T(8,128)(2,1)} %shard_map.66), channel_id=1, source_target_pairs={{0,8},{2,10},{4,12},{6,14},{8,0},{10,2},{12,4},{14,6},{1,9},{3,11}... | collective-permute-start | bytes 786440 | tf_op jit(solution)/shard_map/ppermute | solution.py:307
  14.4 42.8 %collective-permute-start.6 = (bf16[1024,128]{1,0:T(8,128)(2,1)}, bf16[1024,128]{1,0:T(8,128)(2,1)S(1)}, u32[]{:S(2)}, u32[]{:S(2)}) collective-permute-start(bf16[1024,128]{1,0:T(8,128)(2,1)} %shard_map.67), channel_id=1, source_target_pairs={{0,10},{2,8},{4,14},{6,12},{8,2},{10,0},{12,6},{14,4},{1,11},{3,9}... | collective-permute-start | bytes 786440 | tf_op jit(solution)/shard_map/ppermute | solution.py:307
  18.0 42.7 %collective-permute-start.1 = (bf16[1024,128]{1,0:T(8,128)(2,1)}, bf16[1024,128]{1,0:T(8,128)(2,1)S(1)}, u32[]{:S(2)}, u32[]{:S(2)}) collective-permute-start(bf16[1024,128]{1,0:T(8,128)(2,1)} %shard_map.62), channel_id=1, source_target_pairs={{0,2},{2,0},{4,6},{6,4},{8,10},{10,8},{12,14},{14,12},{1,3},{3,1},... | collective-permute-start | bytes 786440 | tf_op jit(solution)/shard_map/ppermute | solution.py:307
  21.4 22.3 %copy-start.13 = (s32[8,1]{0,1:T(1,128)S(1)}, s32[8,1]{0,1:T(1,128)}, u32[]{:S(2)}) copy-start(s32[8,1]{0,1:T(1,128)} %param.7) | copy-start | bytes 100
  21.4 22.3 %copy-start = (bf16[512,1024]{1,0:T(8,128)(2,1)S(1)}, bf16[512,1024]{1,0:T(8,128)(2,1)}, u32[]{:S(2)}) copy-start(bf16[512,1024]{1,0:T(8,128)(2,1)} %k_ref.17) | copy-start | bytes 3145732
  23.2 46.8 %collective-permute-start.2 = (bf16[1024,128]{1,0:T(8,128)(2,1)}, bf16[1024,128]{1,0:T(8,128)(2,1)S(1)}, u32[]{:S(2)}, u32[]{:S(2)}) collective-permute-start(bf16[1024,128]{1,0:T(8,128)(2,1)} %shard_map.63), channel_id=1, source_target_pairs={{0,4},{2,6},{4,0},{6,2},{8,12},{10,14},{12,8},{14,10},{1,5},{3,7},... | collective-permute-start | bytes 786440 | tf_op jit(solution)/shard_map/ppermute | solution.py:307
  38.0 34.9 %collective-permute-start.4 = (bf16[1024,128]{1,0:T(8,128)(2,1)}, bf16[1024,128]{1,0:T(8,128)(2,1)S(1)}, u32[]{:S(2)}, u32[]{:S(2)}) collective-permute-start(bf16[1024,128]{1,0:T(8,128)(2,1)} %shard_map.64), channel_id=1, source_target_pairs={{0,6},{2,4},{4,2},{6,0},{8,14},{10,12},{12,10},{14,8},{1,7},{3,5},... | collective-permute-start | bytes 786440 | tf_op jit(solution)/shard_map/ppermute | solution.py:307
  46.8 54.5 %copy-start.3 = (bf16[528,128]{1,0:T(8,128)(2,1)}, bf16[528,128]{1,0:T(8,128)(2,1)S(1)}, u32[]{:S(2)}) copy-start(bf16[528,128]{1,0:T(8,128)(2,1)S(1)} %get-tuple-element.22.q_ref.tile_ref.refs_0_) | copy-start | bytes 405508
  48.7 12.0 %collective-permute-start.12 = (bf16[528,128]{1,0:T(8,128)(2,1)S(1)}, bf16[528,128]{1,0:T(8,128)(2,1)S(1)}, u32[]{:S(2)}, u32[]{:S(2)}) collective-permute-start(bf16[528,128]{1,0:T(8,128)(2,1)S(1)} %get-tuple-element.33), channel_id=1, source_target_pairs={{0,12},{2,14},{4,8},{6,10},{8,4},{10,6},{12,0},{14,2},{1,13},{3,15... | collective-permute-start | bytes 405512 | tf_op jit(solution)/shard_map/ppermute | solution.py:307
  57.2 8.3 %collective-permute-start.9 = (bf16[528,128]{1,0:T(8,128)(2,1)S(1)}, bf16[528,128]{1,0:T(8,128)(2,1)S(1)}, u32[]{:S(2)}, u32[]{:S(2)}) collective-permute-start(bf16[528,128]{1,0:T(8,128)(2,1)S(1)} %get-tuple-element.29), channel_id=1, source_target_pairs={{0,14},{2,12},{4,10},{6,8},{8,6},{10,4},{12,2},{14,0},{1,15},{3,13... | collective-permute-start | bytes 405512 | tf_op jit(solution)/shard_map/ppermute | solution.py:307
  60.8 18.0 %collective-permute-start.17 = (bf16[528,128]{1,0:T(8,128)(2,1)S(1)}, bf16[528,128]{1,0:T(8,128)(2,1)S(1)}, u32[]{:S(2)}, u32[]{:S(2)}) collective-permute-start(bf16[528,128]{1,0:T(8,128)(2,1)S(1)} %get-tuple-element.38), channel_id=1, source_target_pairs={{0,10},{2,8},{4,14},{6,12},{8,2},{10,0},{12,6},{14,4},{1,11},{3,9}... | collective-permute-start | bytes 405512 | tf_op jit(solution)/shard_map/ppermute | solution.py:307
  60.8 19.5 %collective-permute-start.13 = (bf16[528,128]{1,0:T(8,128)(2,1)S(1)}, bf16[528,128]{1,0:T(8,128)(2,1)S(1)}, u32[]{:S(2)}, u32[]{:S(2)}) collective-permute-start(bf16[528,128]{1,0:T(8,128)(2,1)S(1)} %get-tuple-element.34), channel_id=1, source_target_pairs={{0,6},{2,4},{4,2},{6,0},{8,14},{10,12},{12,10},{14,8},{1,7},{3,5},... | collective-permute-start | bytes 405512 | tf_op jit(solution)/shard_map/ppermute | solution.py:307
  65.5 21.2 %collective-permute-start.10 = (bf16[528,128]{1,0:T(8,128)(2,1)S(1)}, bf16[528,128]{1,0:T(8,128)(2,1)S(1)}, u32[]{:S(2)}, u32[]{:S(2)}) collective-permute-start(bf16[528,128]{1,0:T(8,128)(2,1)S(1)} %get-tuple-element.30), channel_id=1, source_target_pairs={{0,4},{2,6},{4,0},{6,2},{8,12},{10,14},{12,8},{14,10},{1,5},{3,7},... | collective-permute-start | bytes 405512 | tf_op jit(solution)/shard_map/ppermute | solution.py:307
  70.0 19.3 %collective-permute-start.15 = (bf16[528,128]{1,0:T(8,128)(2,1)}, bf16[528,128]{1,0:T(8,128)(2,1)S(1)}, u32[]{:S(2)}, u32[]{:S(2)}) collective-permute-start(bf16[528,128]{1,0:T(8,128)(2,1)} %get-tuple-element.36), channel_id=1, source_target_pairs={{0,8},{2,10},{4,12},{6,14},{8,0},{10,2},{12,4},{14,6},{1,9},{3,11}... | collective-permute-start | bytes 405512 | tf_op jit(solution)/shard_map/ppermute | solution.py:307
  72.9 21.3 %collective-permute-start.7 = (bf16[528,128]{1,0:T(8,128)(2,1)}, bf16[528,128]{1,0:T(8,128)(2,1)S(1)}, u32[]{:S(2)}, u32[]{:S(2)}) collective-permute-start(bf16[528,128]{1,0:T(8,128)(2,1)} %get-tuple-element.26), channel_id=1, source_target_pairs={{0,2},{2,0},{4,6},{6,4},{8,10},{10,8},{12,14},{14,12},{1,3},{3,1},... | collective-permute-start | bytes 405512 | tf_op jit(solution)/shard_map/ppermute | solution.py:307
  78.8 18.2 %collective-permute-start.19 = (bf16[512,128]{1,0:T(8,128)(2,1)S(1)}, bf16[512,128]{1,0:T(8,128)(2,1)S(1)}, u32[]{:S(2)}, u32[]{:S(2)}) collective-permute-start(bf16[512,128]{1,0:T(8,128)(2,1)S(1)} %shard_map.74), channel_id=1, source_target_pairs={{0,12},{2,14},{4,8},{6,10},{8,4},{10,6},{12,0},{14,2},{1,13},{3,15... | collective-permute-start | bytes 393224 | tf_op jit(solution)/shard_map/ppermute | solution.py:324
  80.3 19.8 %collective-permute-start.20 = (bf16[512,128]{1,0:T(8,128)(2,1)S(1)}, bf16[512,128]{1,0:T(8,128)(2,1)S(1)}, u32[]{:S(2)}, u32[]{:S(2)}) collective-permute-start(bf16[512,128]{1,0:T(8,128)(2,1)S(1)} %shard_map.75), channel_id=1, source_target_pairs={{0,14},{2,12},{4,10},{6,8},{8,6},{10,4},{12,2},{14,0},{1,15},{3,13... | collective-permute-start | bytes 393224 | tf_op jit(solution)/shard_map/ppermute | solution.py:324
  86.8 17.8 %collective-permute-start.18 = (bf16[512,128]{1,0:T(8,128)(2,1)S(1)}, bf16[512,128]{1,0:T(8,128)(2,1)S(1)}, u32[]{:S(2)}, u32[]{:S(2)}) collective-permute-start(bf16[512,128]{1,0:T(8,128)(2,1)S(1)} %shard_map.73), channel_id=1, source_target_pairs={{0,10},{2,8},{4,14},{6,12},{8,2},{10,0},{12,6},{14,4},{1,11},{3,9}... | collective-permute-start | bytes 393224 | tf_op jit(solution)/shard_map/ppermute | solution.py:324
  89.3 15.2 %collective-permute-start.14 = (bf16[512,128]{1,0:T(8,128)(2,1)S(1)}, bf16[512,128]{1,0:T(8,128)(2,1)S(1)}, u32[]{:S(2)}, u32[]{:S(2)}) collective-permute-start(bf16[512,128]{1,0:T(8,128)(2,1)S(1)} %shard_map.71), channel_id=1, source_target_pairs={{0,6},{2,4},{4,2},{6,0},{8,14},{10,12},{12,10},{14,8},{1,7},{3,5},... | collective-permute-start | bytes 393224 | tf_op jit(solution)/shard_map/ppermute | solution.py:324
  94.2 10.4 %collective-permute-start.11 = (bf16[512,128]{1,0:T(8,128)(2,1)S(1)}, bf16[512,128]{1,0:T(8,128)(2,1)S(1)}, u32[]{:S(2)}, u32[]{:S(2)}) collective-permute-start(bf16[512,128]{1,0:T(8,128)(2,1)S(1)} %shard_map.70), channel_id=1, source_target_pairs={{0,4},{2,6},{4,0},{6,2},{8,12},{10,14},{12,8},{14,10},{1,5},{3,7},... | collective-permute-start | bytes 393224 | tf_op jit(solution)/shard_map/ppermute | solution.py:324
  97.0 7.6 %collective-permute-start.16 = (bf16[512,128]{1,0:T(8,128)(2,1)}, bf16[512,128]{1,0:T(8,128)(2,1)S(1)}, u32[]{:S(2)}, u32[]{:S(2)}) collective-permute-start(bf16[512,128]{1,0:T(8,128)(2,1)} %shard_map.72), channel_id=1, source_target_pairs={{0,8},{2,10},{4,12},{6,14},{8,0},{10,2},{12,4},{14,6},{1,9},{3,11}... | collective-permute-start | bytes 393224 | tf_op jit(solution)/shard_map/ppermute | solution.py:324
  100.1 5.2 %collective-permute-start.8 = (bf16[512,128]{1,0:T(8,128)(2,1)}, bf16[512,128]{1,0:T(8,128)(2,1)S(1)}, u32[]{:S(2)}, u32[]{:S(2)}) collective-permute-start(bf16[512,128]{1,0:T(8,128)(2,1)} %shard_map.69), channel_id=1, source_target_pairs={{0,2},{2,0},{4,6},{6,4},{8,10},{10,8},{12,14},{14,12},{1,3},{3,1},... | collective-permute-start | bytes 393224 | tf_op jit(solution)/shard_map/ppermute | solution.py:324
  (11 other events, 55.4 us)

commit v6 on v5

--- a/solution.py
+++ b/solution.py
@@ -287,9 +287,6 @@
     return lax.optimization_barrier((x, *earlier))[0]
 
 
-IN_FLIGHT = 5
-
-
 def by_heads(query_rows, key_rows, value_rows, selection):
     members = lax.axis_size("context")
     me = lax.axis_index("context")
@@ -297,33 +294,38 @@
     heads = width // DH
     here = me.astype(jnp.int32)[None]
     near = list(range(1, members // 2))
-    far = list(range(members // 2, members))
-    arrived = []
-
-    def exchange(pieces, order):
-        got = list(pieces)
-        for d in order:
-            earlier = arrived[-IN_FLIGHT:][:1] if len(arrived) >= IN_FLIGHT else []
-            got[d] = lax.ppermute(
-                after(pieces[d], *earlier), "context", [(i, i ^ d) for i in range(members)]
-            )
-            arrived.append(got[d])
-        return got
+    far = list(range(members // 2, members))[::-1]
+
+    def send(x, d):
+        return lax.ppermute(x, "context", [(i, i ^ d) for i in range(members)])
 
     packed = [pack_head(here, d, key_rows, value_rows) for d in range(members)]
-    packed = exchange(packed, far[::-1] + near)
+    got = {}
+
+    def exchange(pieces, kind, ds, window, done):
+        for d in ds:
+            earlier = [got[done[-window]]] if len(done) >= window else []
+            got[kind, d] = send(after(pieces[d], *earlier), d)
+            done.append((kind, d))
+
+    far_done, near_done = [], []
+    exchange(packed, 0, far[::-1], 3, far_done)
+    exchange(packed, 0, near, 2, near_done)
     chosen = jnp.broadcast_to(selection.astype(BF16)[:, :, None], (heads, TILE, DH))
-    pooled_q, *pieces = cut_queries(here, after(query_rows, arrived[0]), key_rows, chosen)
-    queries = exchange(pieces, far[::-1] + near)
+    pooled_q, *pieces = cut_queries(
+        here, after(query_rows, got[0, members // 2]), key_rows, chosen
+    )
+    exchange(pieces, 1, near, 2, near_done)
+    exchange(pieces, 1, far[::-1], 3, far_done)
+    packed = packed[:1] + [got[0, d] for d in range(1, members)]
+    queries = pieces[:1] + [got[1, d] for d in range(1, members)]
     sort_logits = logits_of(here, pooled_q, queries)
 
     outputs = [None] * members
     for d in far[::-1] + near + [0]:
         outputs[d] = attend(here, d, queries[d], packed)
         if d:
-            outputs[d] = lax.ppermute(
-                outputs[d], "context", [(i, i ^ d) for i in range(members)]
-            )
+            outputs[d] = send(outputs[d], d)
     attended = join_heads(here, outputs)
     return attended, sort_logits.reshape(heads, 1, members)
 

time: 107 us -> 103 us (0.963)
  starting transfers between devices: 58.4 us -> 41.1 us
  waiting for transfers between devices: 10.3 us -> 24.1 us
    ppermute x21, starting transfers between devices: 58.4 us -> 41.1 us  [send(): return lax.ppermute(x, 'context', [(i, i ^ d) for i in range(members)])]
    ppermute x21, waiting for transfers between devices: 10.3 us -> 24.1 us  [send(): return lax.ppermute(x, 'context', [(i, i ^ d) for i in range(members)])]
  transfers between devices with their start and end apart: 21 -> 21, of which waited for: 4 -> 5; matrix products, arithmetic and copies ran while one was open for 0% -> 0% of each run, Pallas kernels for 29% -> 30%
where the time goes in v6:
time: 103 us
  starting transfers between devices  41.1 us (40%)
  Pallas kernels  34 us (33%)
  waiting for transfers between devices  24.1 us (23%)
  local copies, waits for them, and re-layouts  2.87 us (3%)
    ppermute x21, starting transfers between devices, send(): return lax.ppermute(x, 'context', [(i, i ^ d) for i in range(members)])  41.1 us
    ppermute x21, waiting for transfers between devices, send(): return lax.ppermute(x, 'context', [(i, i ^ d) for i in range(members)])  24.1 us
    pallas_call x8, Pallas kernels, attend(): pl.pallas_call(attend_kernel, grid_spec=pltpu.PrefetchScalarGridSpec(num_...  16.4 us
    pallas_call x8, Pallas kernels, pack_head(): pl.pallas_call(pack_kernel, grid_spec=pltpu.PrefetchScalarGridSpec(num_sc...  13.6 us
    unnamed x28, local copies, waits for them, and re-layouts  2.8 us
  transfers between devices with their start and end apart: 21, of which 5 were waited for; matrix products, arithmetic and copies ran while one was open for 0% of the time, Pallas kernels for 30%

profile of v6, /device:TPU:0, one launch (start us, length us, event | category | flops | bytes accessed | tf_op | source)
XLA Modules:
  0.0 102.9 jit_solution(3796025617985115555)
XLA Ops:
  0.6 1.7 %shard_map.59 = bf16[1024,128]{1,0:T(8,128)(2,1)} custom-call(s32[1]{0:T(128)} %bitcast.me_ref, bf16[512,1024]{1,0:T(8,128)(2,1)} %k_ref.17, bf16[512,1024]{1,0:T(8,128)(2,1)} %v_ref.15), custom_call_target="tpu_custom_call" | custom-call | bytes 524288 | tf_op jit(solution)/shard_map/pallas_call | solution.py:127
  2.3 4.0 %collective-permute-start = (bf16[1024,128]{1,0:T(8,128)(2,1)}, bf16[1024,128]{1,0:T(8,128)(2,1)S(1)}, u32[]{:S(2)}, u32[]{:S(2)}) collective-permute-start(bf16[1024,128]{1,0:T(8,128)(2,1)} %shard_map.59), channel_id=1, source_target_pairs={{0,8},{2,10},{4,12},{6,14},{8,0},{10,2},{12,4},{14,6},{1,9},{3,11}... | collective-permute-start | bytes 786440 | tf_op jit(solution)/shard_map/ppermute | solution.py:300
  9.6 1.7 %shard_map.65 = bf16[1024,128]{1,0:T(8,128)(2,1)} custom-call(s32[1]{0:T(128)} %bitcast.me_ref, bf16[512,1024]{1,0:T(8,128)(2,1)} %k_ref.17, bf16[512,1024]{1,0:T(8,128)(2,1)} %v_ref.15), custom_call_target="tpu_custom_call" | custom-call | bytes 524288 | tf_op jit(solution)/shard_map/pallas_call | solution.py:127
  13.0 1.9 %collective-permute-start.2 = (bf16[1024,128]{1,0:T(8,128)(2,1)}, bf16[1024,128]{1,0:T(8,128)(2,1)S(1)}, u32[]{:S(2)}, u32[]{:S(2)}) collective-permute-start(bf16[1024,128]{1,0:T(8,128)(2,1)} %shard_map.63), channel_id=1, source_target_pairs={{0,4},{2,6},{4,0},{6,2},{8,12},{10,14},{12,8},{14,10},{1,5},{3,7},... | collective-permute-start | bytes 786440 | tf_op jit(solution)/shard_map/ppermute | solution.py:300
  16.5 2.5 %collective-permute-start.5 = (bf16[1024,128]{1,0:T(8,128)(2,1)}, bf16[1024,128]{1,0:T(8,128)(2,1)S(1)}, u32[]{:S(2)}, u32[]{:S(2)}) collective-permute-start(bf16[1024,128]{1,0:T(8,128)(2,1)} %shard_map.66), channel_id=1, source_target_pairs={{0,12},{2,14},{4,8},{6,10},{8,4},{10,6},{12,0},{14,2},{1,13},{3,15... | collective-permute-start | bytes 786440 | tf_op jit(solution)/shard_map/ppermute | solution.py:300
  20.7 1.8 %shard_map.64 = bf16[1024,128]{1,0:T(8,128)(2,1)} custom-call(s32[1]{0:T(128)} %bitcast.me_ref, bf16[512,1024]{1,0:T(8,128)(2,1)} %k_ref.17, bf16[512,1024]{1,0:T(8,128)(2,1)} %v_ref.15), custom_call_target="tpu_custom_call" | custom-call | bytes 524288 | tf_op jit(solution)/shard_map/pallas_call | solution.py:127
  22.5 2.6 %collective-permute-done.refs_4_.k_ref.v_ref = bf16[1024,128]{1,0:T(8,128)(2,1)S(1)} collective-permute-done((bf16[1024,128]{1,0:T(8,128)(2,1)}, bf16[1024,128]{1,0:T(8,128)(2,1)S(1)}, u32[]{:S(2)}, u32[]{:S(2)}) %collective-permute-start) | collective-permute-done | bytes 262176 | tf_op jit(solution)/shard_map/ppermute | solution.py:300
  25.1 4.6 %collective-permute-start.6 = (bf16[1024,128]{1,0:T(8,128)(2,1)}, bf16[1024,128]{1,0:T(8,128)(2,1)S(1)}, u32[]{:S(2)}, u32[]{:S(2)}) collective-permute-start(bf16[1024,128]{1,0:T(8,128)(2,1)} %shard_map.67), channel_id=1, source_target_pairs={{0,14},{2,12},{4,10},{6,8},{8,6},{10,4},{12,2},{14,0},{1,15},{3,13... | collective-permute-start | bytes 786440 | tf_op jit(solution)/shard_map/ppermute | solution.py:300
  32.9 10.2 %collective-permute-done.4.refs_5_.k_ref.v_ref = bf16[1024,128]{1,0:T(8,128)(2,1)S(1)} collective-permute-done((bf16[1024,128]{1,0:T(8,128)(2,1)}, bf16[1024,128]{1,0:T(8,128)(2,1)S(1)}, u32[]{:S(2)}, u32[]{:S(2)}) %collective-permute-start.4) | collective-permute-done | bytes 262176 | tf_op jit(solution)/shard_map/ppermute | solution.py:300
  43.3 9.9 %collective-permute-start.15 = (bf16[528,128]{1,0:T(8,128)(2,1)}, bf16[528,128]{1,0:T(8,128)(2,1)S(1)}, u32[]{:S(2)}, u32[]{:S(2)}) collective-permute-start(bf16[528,128]{1,0:T(8,128)(2,1)} %get-tuple-element.34), channel_id=1, source_target_pairs={{0,10},{2,8},{4,14},{6,12},{8,2},{10,0},{12,6},{14,4},{1,11},{3,9}... | collective-permute-start | bytes 405512 | tf_op jit(solution)/shard_map/ppermute | solution.py:300
  53.2 8.6 %collective-permute-done.13.q_ref.tile_ref.refs_4_ = bf16[528,128]{1,0:T(8,128)(2,1)S(1)} collective-permute-done((bf16[528,128]{1,0:T(8,128)(2,1)S(1)}, bf16[528,128]{1,0:T(8,128)(2,1)S(1)}, u32[]{:S(2)}, u32[]{:S(2)}) %collective-permute-start.13) | collective-permute-done | bytes 135200 | tf_op jit(solution)/shard_map/ppermute | solution.py:300
  61.8 3.7 %collective-permute-start.19 = (bf16[528,128]{1,0:T(8,128)(2,1)S(1)}, bf16[528,128]{1,0:T(8,128)(2,1)S(1)}, u32[]{:S(2)}, u32[]{:S(2)}) collective-permute-start(bf16[528,128]{1,0:T(8,128)(2,1)S(1)} %get-tuple-element.38), channel_id=1, source_target_pairs={{0,14},{2,12},{4,10},{6,8},{8,6},{10,4},{12,2},{14,0},{1,15},{3,13... | collective-permute-start | bytes 405512 | tf_op jit(solution)/shard_map/ppermute | solution.py:300
  70.3 1.9 %shard_map.73 = bf16[512,128]{1,0:T(8,128)(2,1)S(1)} custom-call(s32[1]{0:T(128)} %bitcast.me_ref, bf16[528,128]{1,0:T(8,128)(2,1)S(1)} %collective-permute-done.15.q_ref.tile_ref.refs_5_, bf16[528,128]{1,0:T(8,128)(2,1)S(1)} %collective-permute-done.15.q_ref.tile_ref.refs_5_, bf16[1024,128]{1,0:T(8,128)(2,1)S(1)} %collective-permute-done.4.refs_5_.k_ref.v_ref, ...), custom_call_target="tpu_custom_call" | custom-call | flops 268435456 | bytes 786432 | tf_op jit(solution)/shard_map/pallas_call | solution.py:236
  72.2 2.4 %collective-permute-start.16 = (bf16[512,128]{1,0:T(8,128)(2,1)S(1)}, bf16[512,128]{1,0:T(8,128)(2,1)S(1)}, u32[]{:S(2)}, u32[]{:S(2)}) collective-permute-start(bf16[512,128]{1,0:T(8,128)(2,1)S(1)} %shard_map.73), channel_id=1, source_target_pairs={{0,10},{2,8},{4,14},{6,12},{8,2},{10,0},{12,6},{14,4},{1,11},{3,9}... | collective-permute-start | bytes 393224 | tf_op jit(solution)/shard_map/ppermute | solution.py:300
  74.5 1.9 %shard_map.72 = bf16[512,128]{1,0:T(8,128)(2,1)S(1)} custom-call(s32[1]{0:T(128)} %bitcast.me_ref, bf16[528,128]{1,0:T(8,128)(2,1)S(1)} %collective-permute-done.13.q_ref.tile_ref.refs_4_, bf16[528,128]{1,0:T(8,128)(2,1)S(1)} %collective-permute-done.13.q_ref.tile_ref.refs_4_, bf16[1024,128]{1,0:T(8,128)(2,1)S(1)} %collective-permute-done.refs_4_.k_ref.v_ref, ...), custom_call_target="tpu_custom_call" | custom-call | flops 268435456 | bytes 786432 | tf_op jit(solution)/shard_map/pallas_call | solution.py:236
  76.4 2.0 %collective-permute-start.14 = (bf16[512,128]{1,0:T(8,128)(2,1)S(1)}, bf16[512,128]{1,0:T(8,128)(2,1)S(1)}, u32[]{:S(2)}, u32[]{:S(2)}) collective-permute-start(bf16[512,128]{1,0:T(8,128)(2,1)S(1)} %shard_map.72), channel_id=1, source_target_pairs={{0,8},{2,10},{4,12},{6,14},{8,0},{10,2},{12,4},{14,6},{1,9},{3,11}... | collective-permute-start | bytes 393224 | tf_op jit(solution)/shard_map/ppermute | solution.py:300
  78.4 1.9 %shard_map.69 = bf16[512,128]{1,0:T(8,128)(2,1)S(1)} custom-call(s32[1]{0:T(128)} %bitcast.me_ref, bf16[528,128]{1,0:T(8,128)(2,1)S(1)} %collective-permute-done.7.q_ref.tile_ref.refs_1_, bf16[528,128]{1,0:T(8,128)(2,1)S(1)} %collective-permute-done.7.q_ref.tile_ref.refs_1_, bf16[1024,128]{1,0:T(8,128)(2,1)S(1)} %collective-permute-done.1.refs_1_.k_ref.v_ref, ...), custom_call_target="tpu_custom_call" | custom-call | flops 268435456 | bytes 786432 | tf_op jit(solution)/shard_map/pallas_call | solution.py:236
  80.3 1.9 %shard_map.75 = bf16[512,128]{1,0:T(8,128)(2,1)S(1)} custom-call(s32[1]{0:T(128)} %bitcast.me_ref, bf16[528,128]{1,0:T(8,128)(2,1)S(1)} %collective-permute-done.19.q_ref.tile_ref.refs_7_, bf16[528,128]{1,0:T(8,128)(2,1)S(1)} %collective-permute-done.19.q_ref.tile_ref.refs_7_, bf16[1024,128]{1,0:T(8,128)(2,1)S(1)} %collective-permute-done.6.refs_7_.k_ref.v_ref, ...), custom_call_target="tpu_custom_call" | custom-call | flops 268435456 | bytes 786432 | tf_op jit(solution)/shard_map/pallas_call | solution.py:236
  82.4 1.9 %shard_map.71 = bf16[512,128]{1,0:T(8,128)(2,1)S(1)} custom-call(s32[1]{0:T(128)} %bitcast.me_ref, bf16[528,128]{1,0:T(8,128)(2,1)S(1)} %collective-permute-done.11.q_ref.tile_ref.refs_3_, bf16[528,128]{1,0:T(8,128)(2,1)S(1)} %collective-permute-done.11.q_ref.tile_ref.refs_3_, bf16[1024,128]{1,0:T(8,128)(2,1)S(1)} %collective-permute-done.3.refs_3_.k_ref.v_ref, ...), custom_call_target="tpu_custom_call" | custom-call | flops 268435456 | bytes 786432 | tf_op jit(solution)/shard_map/pallas_call | solution.py:236
  84.3 3.8 %collective-permute-start.20 = (bf16[512,128]{1,0:T(8,128)(2,1)S(1)}, bf16[512,128]{1,0:T(8,128)(2,1)S(1)}, u32[]{:S(2)}, u32[]{:S(2)}) collective-permute-start(bf16[512,128]{1,0:T(8,128)(2,1)S(1)} %shard_map.75), channel_id=1, source_target_pairs={{0,14},{2,12},{4,10},{6,8},{8,6},{10,4},{12,2},{14,0},{1,15},{3,13... | collective-permute-start | bytes 393224 | tf_op jit(solution)/shard_map/ppermute | solution.py:300
  88.1 2.5 %shard_map.74 = bf16[512,128]{1,0:T(8,128)(2,1)} custom-call(s32[1]{0:T(128)} %bitcast.me_ref, bf16[528,128]{1,0:T(8,128)(2,1)S(1)} %collective-permute-done.17.q_ref.tile_ref.refs_6_, bf16[528,128]{1,0:T(8,128)(2,1)S(1)} %collective-permute-done.17.q_ref.tile_ref.refs_6_, bf16[1024,128]{1,0:T(8,128)(2,1)S(1)} %collective-permute-done.5.refs_6_.k_ref.v_ref, ...), custom_call_target="tpu_custom_call" | custom-call | flops 268435456 | bytes 786432 | tf_op jit(solution)/shard_map/pallas_call | solution.py:236
  90.8 2.7 %shard_map.70 = bf16[512,128]{1,0:T(8,128)(2,1)} custom-call(s32[1]{0:T(128)} %bitcast.me_ref, bf16[528,128]{1,0:T(8,128)(2,1)S(1)} %collective-permute-done.9.q_ref.tile_ref.refs_2_, bf16[528,128]{1,0:T(8,128)(2,1)S(1)} %collective-permute-done.9.q_ref.tile_ref.refs_2_, bf16[1024,128]{1,0:T(8,128)(2,1)S(1)} %collective-permute-done.2.refs_2_.k_ref.v_ref, ...), custom_call_target="tpu_custom_call" | custom-call | flops 268435456 | bytes 786432 | tf_op jit(solution)/shard_map/pallas_call | solution.py:236
  95.7 1.9 %shard_map.68.refs_0_ = bf16[512,128]{1,0:T(8,128)(2,1)S(1)} custom-call(s32[1]{0:T(128)} %bitcast.me_ref, bf16[528,128]{1,0:T(8,128)(2,1)S(1)} %get-tuple-element.22.q_ref.tile_ref.refs_0_, bf16[528,128]{1,0:T(8,128)(2,1)S(1)} %get-tuple-element.22.q_ref.tile_ref.refs_0_, bf16[1024,128]{1,0:T(8,128)(2,1)S(1)} %copy-done.2, bf16[1024,128]{1,0:T(8,128)(2,1)S(1)} %copy-done.2, ...), custom_call_target="tpu_custom_call" | custom-call | flops 268435456 | bytes 786432 | tf_op jit(solution)/shard_map/pallas_call | solution.py:236
  99.0 1.8 %collective-permute-done.12.refs_3_ = bf16[512,128]{1,0:T(8,128)(2,1)S(1)} collective-permute-done((bf16[512,128]{1,0:T(8,128)(2,1)S(1)}, bf16[512,128]{1,0:T(8,128)(2,1)S(1)}, u32[]{:S(2)}, u32[]{:S(2)}) %collective-permute-start.12) | collective-permute-done | bytes 131104 | tf_op jit(solution)/shard_map/ppermute | solution.py:300
  (67 shorter events, 22.4 us)
Async XLA Ops:
  2.3 22.8 %collective-permute-start = (bf16[1024,128]{1,0:T(8,128)(2,1)}, bf16[1024,128]{1,0:T(8,128)(2,1)S(1)}, u32[]{:S(2)}, u32[]{:S(2)}) collective-permute-start(bf16[1024,128]{1,0:T(8,128)(2,1)} %shard_map.59), channel_id=1, source_target_pairs={{0,8},{2,10},{4,12},{6,14},{8,0},{10,2},{12,4},{14,6},{1,9},{3,11}... | collective-permute-start | bytes 786440 | tf_op jit(solution)/shard_map/ppermute | solution.py:300
  8.1 21.7 %collective-permute-start.1 = (bf16[1024,128]{1,0:T(8,128)(2,1)}, bf16[1024,128]{1,0:T(8,128)(2,1)S(1)}, u32[]{:S(2)}, u32[]{:S(2)}) collective-permute-start(bf16[1024,128]{1,0:T(8,128)(2,1)} %shard_map.62), channel_id=1, source_target_pairs={{0,2},{2,0},{4,6},{6,4},{8,10},{10,8},{12,14},{14,12},{1,3},{3,1},... | collective-permute-start | bytes 786440 | tf_op jit(solution)/shard_map/ppermute | solution.py:300
  11.3 31.9 %collective-permute-start.4 = (bf16[1024,128]{1,0:T(8,128)(2,1)}, bf16[1024,128]{1,0:T(8,128)(2,1)S(1)}, u32[]{:S(2)}, u32[]{:S(2)}) collective-permute-start(bf16[1024,128]{1,0:T(8,128)(2,1)} %shard_map.65), channel_id=1, source_target_pairs={{0,10},{2,8},{4,14},{6,12},{8,2},{10,0},{12,6},{14,4},{1,11},{3,9}... | collective-permute-start | bytes 786440 | tf_op jit(solution)/shard_map/ppermute | solution.py:300
  13.0 30.2 %collective-permute-start.2 = (bf16[1024,128]{1,0:T(8,128)(2,1)}, bf16[1024,128]{1,0:T(8,128)(2,1)S(1)}, u32[]{:S(2)}, u32[]{:S(2)}) collective-permute-start(bf16[1024,128]{1,0:T(8,128)(2,1)} %shard_map.63), channel_id=1, source_target_pairs={{0,4},{2,6},{4,0},{6,2},{8,12},{10,14},{12,8},{14,10},{1,5},{3,7},... | collective-permute-start | bytes 786440 | tf_op jit(solution)/shard_map/ppermute | solution.py:300
  16.5 26.8 %collective-permute-start.5 = (bf16[1024,128]{1,0:T(8,128)(2,1)}, bf16[1024,128]{1,0:T(8,128)(2,1)S(1)}, u32[]{:S(2)}, u32[]{:S(2)}) collective-permute-start(bf16[1024,128]{1,0:T(8,128)(2,1)} %shard_map.66), channel_id=1, source_target_pairs={{0,12},{2,14},{4,8},{6,10},{8,4},{10,6},{12,0},{14,2},{1,13},{3,15... | collective-permute-start | bytes 786440 | tf_op jit(solution)/shard_map/ppermute | solution.py:300
  25.1 40.4 %collective-permute-start.6 = (bf16[1024,128]{1,0:T(8,128)(2,1)}, bf16[1024,128]{1,0:T(8,128)(2,1)S(1)}, u32[]{:S(2)}, u32[]{:S(2)}) collective-permute-start(bf16[1024,128]{1,0:T(8,128)(2,1)} %shard_map.67), channel_id=1, source_target_pairs={{0,14},{2,12},{4,10},{6,8},{8,6},{10,4},{12,2},{14,0},{1,15},{3,13... | collective-permute-start | bytes 786440 | tf_op jit(solution)/shard_map/ppermute | solution.py:300
  29.7 38.9 %collective-permute-start.3 = (bf16[1024,128]{1,0:T(8,128)(2,1)}, bf16[1024,128]{1,0:T(8,128)(2,1)S(1)}, u32[]{:S(2)}, u32[]{:S(2)}) collective-permute-start(bf16[1024,128]{1,0:T(8,128)(2,1)} %shard_map.64), channel_id=1, source_target_pairs={{0,6},{2,4},{4,2},{6,0},{8,14},{10,12},{12,10},{14,8},{1,7},{3,5},... | collective-permute-start | bytes 786440 | tf_op jit(solution)/shard_map/ppermute | solution.py:300
  32.9 62.7 %copy-start.3 = (bf16[528,128]{1,0:T(8,128)(2,1)}, bf16[528,128]{1,0:T(8,128)(2,1)S(1)}, u32[]{:S(2)}) copy-start(bf16[528,128]{1,0:T(8,128)(2,1)S(1)} %get-tuple-element.22.q_ref.tile_ref.refs_0_) | copy-start | bytes 405508
  43.1 18.6 %collective-permute-start.13 = (bf16[528,128]{1,0:T(8,128)(2,1)S(1)}, bf16[528,128]{1,0:T(8,128)(2,1)S(1)}, u32[]{:S(2)}, u32[]{:S(2)}) collective-permute-start(bf16[528,128]{1,0:T(8,128)(2,1)S(1)} %get-tuple-element.32), channel_id=1, source_target_pairs={{0,8},{2,10},{4,12},{6,14},{8,0},{10,2},{12,4},{14,6},{1,9},{3,11}... | collective-permute-start | bytes 405512 | tf_op jit(solution)/shard_map/ppermute | solution.py:300
  43.1 22.4 %collective-permute-start.7 = (bf16[528,128]{1,0:T(8,128)(2,1)S(1)}, bf16[528,128]{1,0:T(8,128)(2,1)S(1)}, u32[]{:S(2)}, u32[]{:S(2)}) collective-permute-start(bf16[528,128]{1,0:T(8,128)(2,1)S(1)} %get-tuple-element.26), channel_id=1, source_target_pairs={{0,2},{2,0},{4,6},{6,4},{8,10},{10,8},{12,14},{14,12},{1,3},{3,1},... | collective-permute-start | bytes 405512 | tf_op jit(solution)/shard_map/ppermute | solution.py:300
  43.3 26.0 %collective-permute-start.15 = (bf16[528,128]{1,0:T(8,128)(2,1)}, bf16[528,128]{1,0:T(8,128)(2,1)S(1)}, u32[]{:S(2)}, u32[]{:S(2)}) collective-permute-start(bf16[528,128]{1,0:T(8,128)(2,1)} %get-tuple-element.34), channel_id=1, source_target_pairs={{0,10},{2,8},{4,14},{6,12},{8,2},{10,0},{12,6},{14,4},{1,11},{3,9}... | collective-permute-start | bytes 405512 | tf_op jit(solution)/shard_map/ppermute | solution.py:300
  61.8 12.8 %copy-start.4 = (bf16[528,128]{1,0:T(8,128)(2,1)}, bf16[528,128]{1,0:T(8,128)(2,1)S(1)}, u32[]{:S(2)}) copy-start(bf16[528,128]{1,0:T(8,128)(2,1)S(1)} %collective-permute-done.13.q_ref.tile_ref.refs_4_) | copy-start | bytes 405508
  61.8 14.7 %collective-permute-start.19 = (bf16[528,128]{1,0:T(8,128)(2,1)S(1)}, bf16[528,128]{1,0:T(8,128)(2,1)S(1)}, u32[]{:S(2)}, u32[]{:S(2)}) collective-permute-start(bf16[528,128]{1,0:T(8,128)(2,1)S(1)} %get-tuple-element.38), channel_id=1, source_target_pairs={{0,14},{2,12},{4,10},{6,8},{8,6},{10,4},{12,2},{14,0},{1,15},{3,13... | collective-permute-start | bytes 405512 | tf_op jit(solution)/shard_map/ppermute | solution.py:300
  65.5 12.9 %copy-start.5 = (bf16[528,128]{1,0:T(8,128)(2,1)}, bf16[528,128]{1,0:T(8,128)(2,1)S(1)}, u32[]{:S(2)}) copy-start(bf16[528,128]{1,0:T(8,128)(2,1)S(1)} %collective-permute-done.7.q_ref.tile_ref.refs_1_) | copy-start | bytes 405508
  65.5 16.7 %collective-permute-start.11 = (bf16[528,128]{1,0:T(8,128)(2,1)S(1)}, bf16[528,128]{1,0:T(8,128)(2,1)S(1)}, u32[]{:S(2)}, u32[]{:S(2)}) collective-permute-start(bf16[528,128]{1,0:T(8,128)(2,1)S(1)} %get-tuple-element.30), channel_id=1, source_target_pairs={{0,6},{2,4},{4,2},{6,0},{8,14},{10,12},{12,10},{14,8},{1,7},{3,5},... | collective-permute-start | bytes 405512 | tf_op jit(solution)/shard_map/ppermute | solution.py:300
  65.5 18.8 %collective-permute-start.17 = (bf16[528,128]{1,0:T(8,128)(2,1)}, bf16[528,128]{1,0:T(8,128)(2,1)S(1)}, u32[]{:S(2)}, u32[]{:S(2)}) collective-permute-start(bf16[528,128]{1,0:T(8,128)(2,1)} %get-tuple-element.36), channel_id=1, source_target_pairs={{0,12},{2,14},{4,8},{6,10},{8,4},{10,6},{12,0},{14,2},{1,13},{3,15... | collective-permute-start | bytes 405512 | tf_op jit(solution)/shard_map/ppermute | solution.py:300
  68.7 22.0 %collective-permute-start.9 = (bf16[528,128]{1,0:T(8,128)(2,1)}, bf16[528,128]{1,0:T(8,128)(2,1)S(1)}, u32[]{:S(2)}, u32[]{:S(2)}) collective-permute-start(bf16[528,128]{1,0:T(8,128)(2,1)} %get-tuple-element.28), channel_id=1, source_target_pairs={{0,4},{2,6},{4,0},{6,2},{8,12},{10,14},{12,8},{14,10},{1,5},{3,7},... | collective-permute-start | bytes 405512 | tf_op jit(solution)/shard_map/ppermute | solution.py:300
  72.2 21.4 %collective-permute-start.16 = (bf16[512,128]{1,0:T(8,128)(2,1)S(1)}, bf16[512,128]{1,0:T(8,128)(2,1)S(1)}, u32[]{:S(2)}, u32[]{:S(2)}) collective-permute-start(bf16[512,128]{1,0:T(8,128)(2,1)S(1)} %shard_map.73), channel_id=1, source_target_pairs={{0,10},{2,8},{4,14},{6,12},{8,2},{10,0},{12,6},{14,4},{1,11},{3,9}... | collective-permute-start | bytes 393224 | tf_op jit(solution)/shard_map/ppermute | solution.py:300
  76.4 18.6 %collective-permute-start.14 = (bf16[512,128]{1,0:T(8,128)(2,1)S(1)}, bf16[512,128]{1,0:T(8,128)(2,1)S(1)}, u32[]{:S(2)}, u32[]{:S(2)}) collective-permute-start(bf16[512,128]{1,0:T(8,128)(2,1)S(1)} %shard_map.72), channel_id=1, source_target_pairs={{0,8},{2,10},{4,12},{6,14},{8,0},{10,2},{12,4},{14,6},{1,9},{3,11}... | collective-permute-start | bytes 393224 | tf_op jit(solution)/shard_map/ppermute | solution.py:300
  82.2 16.7 %collective-permute-start.8 = (bf16[512,128]{1,0:T(8,128)(2,1)S(1)}, bf16[512,128]{1,0:T(8,128)(2,1)S(1)}, u32[]{:S(2)}, u32[]{:S(2)}) collective-permute-start(bf16[512,128]{1,0:T(8,128)(2,1)S(1)} %shard_map.69), channel_id=1, source_target_pairs={{0,2},{2,0},{4,6},{6,4},{8,10},{10,8},{12,14},{14,12},{1,3},{3,1},... | collective-permute-start | bytes 393224 | tf_op jit(solution)/shard_map/ppermute | solution.py:300
  84.3 14.6 %collective-permute-start.20 = (bf16[512,128]{1,0:T(8,128)(2,1)S(1)}, bf16[512,128]{1,0:T(8,128)(2,1)S(1)}, u32[]{:S(2)}, u32[]{:S(2)}) collective-permute-start(bf16[512,128]{1,0:T(8,128)(2,1)S(1)} %shard_map.75), channel_id=1, source_target_pairs={{0,14},{2,12},{4,10},{6,8},{8,6},{10,4},{12,2},{14,0},{1,15},{3,13... | collective-permute-start | bytes 393224 | tf_op jit(solution)/shard_map/ppermute | solution.py:300
  90.7 10.1 %collective-permute-start.12 = (bf16[512,128]{1,0:T(8,128)(2,1)S(1)}, bf16[512,128]{1,0:T(8,128)(2,1)S(1)}, u32[]{:S(2)}, u32[]{:S(2)}) collective-permute-start(bf16[512,128]{1,0:T(8,128)(2,1)S(1)} %shard_map.71), channel_id=1, source_target_pairs={{0,6},{2,4},{4,2},{6,0},{8,14},{10,12},{12,10},{14,8},{1,7},{3,5},... | collective-permute-start | bytes 393224 | tf_op jit(solution)/shard_map/ppermute | solution.py:300
  93.6 7.2 %collective-permute-start.18 = (bf16[512,128]{1,0:T(8,128)(2,1)}, bf16[512,128]{1,0:T(8,128)(2,1)S(1)}, u32[]{:S(2)}, u32[]{:S(2)}) collective-permute-start(bf16[512,128]{1,0:T(8,128)(2,1)} %shard_map.74), channel_id=1, source_target_pairs={{0,12},{2,14},{4,8},{6,10},{8,4},{10,6},{12,0},{14,2},{1,13},{3,15... | collective-permute-start | bytes 393224 | tf_op jit(solution)/shard_map/ppermute | solution.py:300
  95.0 6.6 %collective-permute-start.10 = (bf16[512,128]{1,0:T(8,128)(2,1)}, bf16[512,128]{1,0:T(8,128)(2,1)S(1)}, u32[]{:S(2)}, u32[]{:S(2)}) collective-permute-start(bf16[512,128]{1,0:T(8,128)(2,1)} %shard_map.70), channel_id=1, source_target_pairs={{0,4},{2,6},{4,0},{6,2},{8,12},{10,14},{12,8},{14,10},{1,5},{3,7},... | collective-permute-start | bytes 393224 | tf_op jit(solution)/shard_map/ppermute | solution.py:300
  (11 other events, 43.1 us)

commit v7 on v6

--- a/solution.py
+++ b/solution.py
@@ -313,7 +313,7 @@
     exchange(packed, 0, near, 2, near_done)
     chosen = jnp.broadcast_to(selection.astype(BF16)[:, :, None], (heads, TILE, DH))
     pooled_q, *pieces = cut_queries(
-        here, after(query_rows, got[0, members // 2]), key_rows, chosen
+        here, after(query_rows, got[0, members // 2], packed[0]), key_rows, chosen
     )
     exchange(pieces, 1, near, 2, near_done)
     exchange(pieces, 1, far[::-1], 3, far_done)

time: 103 us -> 101 us (0.981)
  waiting for transfers between devices: 24.1 us -> 23 us
    ppermute x21, waiting for transfers between devices: 24.1 us -> 23 us  [send(): return lax.ppermute(x, 'context', [(i, i ^ d) for i in range(members)])]
where the time goes in v7:
time: 101 us; the launch traced here: 100 us
  starting transfers between devices  41.1 us (41%)
  Pallas kernels  33.4 us (33%)
  waiting for transfers between devices  23 us (23%)
  local copies, waits for them, and re-layouts  1.92 us (2%)
    ppermute x21, starting transfers between devices, send(): return lax.ppermute(x, 'context', [(i, i ^ d) for i in range(members)])  41.1 us
    ppermute x21, waiting for transfers between devices, send(): return lax.ppermute(x, 'context', [(i, i ^ d) for i in range(members)])  23 us
    pallas_call x8, Pallas kernels, attend(): pl.pallas_call(attend_kernel, grid_spec=pltpu.PrefetchScalarGridSpec(num_...  16.4 us
    pallas_call x8, Pallas kernels, pack_head(): pl.pallas_call(pack_kernel, grid_spec=pltpu.PrefetchScalarGridSpec(num_sc...  13.7 us
  transfers between devices with their start and end apart: 21, of which 5 were waited for; matrix products, arithmetic and copies ran while one was open for 0% of the time, Pallas kernels for 30%

profile of v7, /device:TPU:0, one launch (start us, length us, event | category | flops | bytes accessed | tf_op | source)
XLA Modules:
  0.0 100.3 jit_solution(14272929157187739431)
XLA Ops:
  2.3 4.0 %collective-permute-start = (bf16[1024,128]{1,0:T(8,128)(2,1)}, bf16[1024,128]{1,0:T(8,128)(2,1)S(1)}, u32[]{:S(2)}, u32[]{:S(2)}) collective-permute-start(bf16[1024,128]{1,0:T(8,128)(2,1)} %shard_map.59), channel_id=1, source_target_pairs={{0,8},{2,10},{4,12},{6,14},{8,0},{10,2},{12,4},{14,6},{1,9},{3,11}... | collective-permute-start | bytes 786440 | tf_op jit(solution)/shard_map/ppermute | solution.py:300
  12.9 1.9 %collective-permute-start.2 = (bf16[1024,128]{1,0:T(8,128)(2,1)}, bf16[1024,128]{1,0:T(8,128)(2,1)S(1)}, u32[]{:S(2)}, u32[]{:S(2)}) collective-permute-start(bf16[1024,128]{1,0:T(8,128)(2,1)} %shard_map.63), channel_id=1, source_target_pairs={{0,4},{2,6},{4,0},{6,2},{8,12},{10,14},{12,8},{14,10},{1,5},{3,7},... | collective-permute-start | bytes 786440 | tf_op jit(solution)/shard_map/ppermute | solution.py:300
  14.8 1.7 %shard_map.66 = bf16[1024,128]{1,0:T(8,128)(2,1)} custom-call(s32[1]{0:T(128)} %bitcast.me_ref, bf16[512,1024]{1,0:T(8,128)(2,1)} %k_ref.17, bf16[512,1024]{1,0:T(8,128)(2,1)} %v_ref.15), custom_call_target="tpu_custom_call" | custom-call | bytes 524288 | tf_op jit(solution)/shard_map/pallas_call | solution.py:127
  16.5 2.5 %collective-permute-start.5 = (bf16[1024,128]{1,0:T(8,128)(2,1)}, bf16[1024,128]{1,0:T(8,128)(2,1)S(1)}, u32[]{:S(2)}, u32[]{:S(2)}) collective-permute-start(bf16[1024,128]{1,0:T(8,128)(2,1)} %shard_map.66), channel_id=1, source_target_pairs={{0,12},{2,14},{4,8},{6,10},{8,4},{10,6},{12,0},{14,2},{1,13},{3,15... | collective-permute-start | bytes 786440 | tf_op jit(solution)/shard_map/ppermute | solution.py:300
  20.7 1.7 %shard_map.64 = bf16[1024,128]{1,0:T(8,128)(2,1)} custom-call(s32[1]{0:T(128)} %bitcast.me_ref, bf16[512,1024]{1,0:T(8,128)(2,1)} %k_ref.17, bf16[512,1024]{1,0:T(8,128)(2,1)} %v_ref.15), custom_call_target="tpu_custom_call" | custom-call | bytes 524288 | tf_op jit(solution)/shard_map/pallas_call | solution.py:127
  22.4 2.7 %collective-permute-done.refs_4_.k_ref.v_ref = bf16[1024,128]{1,0:T(8,128)(2,1)S(1)} collective-permute-done((bf16[1024,128]{1,0:T(8,128)(2,1)}, bf16[1024,128]{1,0:T(8,128)(2,1)S(1)}, u32[]{:S(2)}, u32[]{:S(2)}) %collective-permute-start) | collective-permute-done | bytes 262176 | tf_op jit(solution)/shard_map/ppermute | solution.py:300
  25.1 4.6 %collective-permute-start.6 = (bf16[1024,128]{1,0:T(8,128)(2,1)S(1)}, bf16[1024,128]{1,0:T(8,128)(2,1)S(1)}, u32[]{:S(2)}, u32[]{:S(2)}) collective-permute-start(bf16[1024,128]{1,0:T(8,128)(2,1)S(1)} %copy-done.12), channel_id=1, source_target_pairs={{0,14},{2,12},{4,10},{6,8},{8,6},{10,4},{12,2},{14,0},{1,15},{3,13... | collective-permute-start | bytes 786440 | tf_op jit(solution)/shard_map/ppermute | solution.py:300
  29.8 1.8 %shard_map.60.k_ref.v_ref.refs_0_ = bf16[1024,128]{1,0:T(8,128)(2,1)} custom-call(s32[1]{0:T(128)} %bitcast.me_ref, bf16[512,1024]{1,0:T(8,128)(2,1)} %k_ref.17, bf16[512,1024]{1,0:T(8,128)(2,1)} %v_ref.15), custom_call_target="tpu_custom_call" | custom-call | bytes 524288 | tf_op jit(solution)/shard_map/pallas_call | solution.py:127
  34.1 9.0 %collective-permute-done.4.refs_5_.k_ref.v_ref = bf16[1024,128]{1,0:T(8,128)(2,1)S(1)} collective-permute-done((bf16[1024,128]{1,0:T(8,128)(2,1)}, bf16[1024,128]{1,0:T(8,128)(2,1)S(1)}, u32[]{:S(2)}, u32[]{:S(2)}) %collective-permute-start.4) | collective-permute-done | bytes 262176 | tf_op jit(solution)/shard_map/ppermute | solution.py:300
  43.3 9.9 %collective-permute-start.15 = (bf16[528,128]{1,0:T(8,128)(2,1)S(1)}, bf16[528,128]{1,0:T(8,128)(2,1)S(1)}, u32[]{:S(2)}, u32[]{:S(2)}) collective-permute-start(bf16[528,128]{1,0:T(8,128)(2,1)S(1)} %get-tuple-element.34), channel_id=1, source_target_pairs={{0,10},{2,8},{4,14},{6,12},{8,2},{10,0},{12,6},{14,4},{1,11},{3,9}... | collective-permute-start | bytes 405512 | tf_op jit(solution)/shard_map/ppermute | solution.py:300
  53.2 8.6 %collective-permute-done.13.q_ref.tile_ref.refs_4_ = bf16[528,128]{1,0:T(8,128)(2,1)S(1)} collective-permute-done((bf16[528,128]{1,0:T(8,128)(2,1)S(1)}, bf16[528,128]{1,0:T(8,128)(2,1)S(1)}, u32[]{:S(2)}, u32[]{:S(2)}) %collective-permute-start.13) | collective-permute-done | bytes 135200 | tf_op jit(solution)/shard_map/ppermute | solution.py:300
  61.8 3.7 %collective-permute-start.19 = (bf16[528,128]{1,0:T(8,128)(2,1)S(1)}, bf16[528,128]{1,0:T(8,128)(2,1)S(1)}, u32[]{:S(2)}, u32[]{:S(2)}) collective-permute-start(bf16[528,128]{1,0:T(8,128)(2,1)S(1)} %get-tuple-element.38), channel_id=1, source_target_pairs={{0,14},{2,12},{4,10},{6,8},{8,6},{10,4},{12,2},{14,0},{1,15},{3,13... | collective-permute-start | bytes 405512 | tf_op jit(solution)/shard_map/ppermute | solution.py:300
  67.6 1.9 %shard_map.73 = bf16[512,128]{1,0:T(8,128)(2,1)S(1)} custom-call(s32[1]{0:T(128)} %bitcast.me_ref, bf16[528,128]{1,0:T(8,128)(2,1)S(1)} %collective-permute-done.15.q_ref.tile_ref.refs_5_, bf16[528,128]{1,0:T(8,128)(2,1)S(1)} %collective-permute-done.15.q_ref.tile_ref.refs_5_, bf16[1024,128]{1,0:T(8,128)(2,1)S(1)} %collective-permute-done.4.refs_5_.k_ref.v_ref, ...), custom_call_target="tpu_custom_call" | custom-call | flops 268435456 | bytes 786432 | tf_op jit(solution)/shard_map/pallas_call | solution.py:236
  69.5 2.4 %collective-permute-start.16 = (bf16[512,128]{1,0:T(8,128)(2,1)S(1)}, bf16[512,128]{1,0:T(8,128)(2,1)S(1)}, u32[]{:S(2)}, u32[]{:S(2)}) collective-permute-start(bf16[512,128]{1,0:T(8,128)(2,1)S(1)} %shard_map.73), channel_id=1, source_target_pairs={{0,10},{2,8},{4,14},{6,12},{8,2},{10,0},{12,6},{14,4},{1,11},{3,9}... | collective-permute-start | bytes 393224 | tf_op jit(solution)/shard_map/ppermute | solution.py:300
  71.9 1.9 %shard_map.72 = bf16[512,128]{1,0:T(8,128)(2,1)S(1)} custom-call(s32[1]{0:T(128)} %bitcast.me_ref, bf16[528,128]{1,0:T(8,128)(2,1)S(1)} %collective-permute-done.13.q_ref.tile_ref.refs_4_, bf16[528,128]{1,0:T(8,128)(2,1)S(1)} %collective-permute-done.13.q_ref.tile_ref.refs_4_, bf16[1024,128]{1,0:T(8,128)(2,1)S(1)} %collective-permute-done.refs_4_.k_ref.v_ref, ...), custom_call_target="tpu_custom_call" | custom-call | flops 268435456 | bytes 786432 | tf_op jit(solution)/shard_map/pallas_call | solution.py:236
  73.8 2.0 %collective-permute-start.14 = (bf16[512,128]{1,0:T(8,128)(2,1)S(1)}, bf16[512,128]{1,0:T(8,128)(2,1)S(1)}, u32[]{:S(2)}, u32[]{:S(2)}) collective-permute-start(bf16[512,128]{1,0:T(8,128)(2,1)S(1)} %shard_map.72), channel_id=1, source_target_pairs={{0,8},{2,10},{4,12},{6,14},{8,0},{10,2},{12,4},{14,6},{1,9},{3,11}... | collective-permute-start | bytes 393224 | tf_op jit(solution)/shard_map/ppermute | solution.py:300
  75.8 1.9 %shard_map.69 = bf16[512,128]{1,0:T(8,128)(2,1)S(1)} custom-call(s32[1]{0:T(128)} %bitcast.me_ref, bf16[528,128]{1,0:T(8,128)(2,1)S(1)} %collective-permute-done.7.q_ref.tile_ref.refs_1_, bf16[528,128]{1,0:T(8,128)(2,1)S(1)} %collective-permute-done.7.q_ref.tile_ref.refs_1_, bf16[1024,128]{1,0:T(8,128)(2,1)S(1)} %collective-permute-done.1.refs_1_.k_ref.v_ref, ...), custom_call_target="tpu_custom_call" | custom-call | flops 268435456 | bytes 786432 | tf_op jit(solution)/shard_map/pallas_call | solution.py:236
  77.7 1.9 %shard_map.75 = bf16[512,128]{1,0:T(8,128)(2,1)S(1)} custom-call(s32[1]{0:T(128)} %bitcast.me_ref, bf16[528,128]{1,0:T(8,128)(2,1)S(1)} %collective-permute-done.19.q_ref.tile_ref.refs_7_, bf16[528,128]{1,0:T(8,128)(2,1)S(1)} %collective-permute-done.19.q_ref.tile_ref.refs_7_, bf16[1024,128]{1,0:T(8,128)(2,1)S(1)} %collective-permute-done.6.refs_7_.k_ref.v_ref, ...), custom_call_target="tpu_custom_call" | custom-call | flops 268435456 | bytes 786432 | tf_op jit(solution)/shard_map/pallas_call | solution.py:236
  79.8 1.9 %shard_map.71 = bf16[512,128]{1,0:T(8,128)(2,1)S(1)} custom-call(s32[1]{0:T(128)} %bitcast.me_ref, bf16[528,128]{1,0:T(8,128)(2,1)S(1)} %collective-permute-done.11.q_ref.tile_ref.refs_3_, bf16[528,128]{1,0:T(8,128)(2,1)S(1)} %collective-permute-done.11.q_ref.tile_ref.refs_3_, bf16[1024,128]{1,0:T(8,128)(2,1)S(1)} %collective-permute-done.3.refs_3_.k_ref.v_ref, ...), custom_call_target="tpu_custom_call" | custom-call | flops 268435456 | bytes 786432 | tf_op jit(solution)/shard_map/pallas_call | solution.py:236
  81.7 3.8 %collective-permute-start.20 = (bf16[512,128]{1,0:T(8,128)(2,1)S(1)}, bf16[512,128]{1,0:T(8,128)(2,1)S(1)}, u32[]{:S(2)}, u32[]{:S(2)}) collective-permute-start(bf16[512,128]{1,0:T(8,128)(2,1)S(1)} %shard_map.75), channel_id=1, source_target_pairs={{0,14},{2,12},{4,10},{6,8},{8,6},{10,4},{12,2},{14,0},{1,15},{3,13... | collective-permute-start | bytes 393224 | tf_op jit(solution)/shard_map/ppermute | solution.py:300
  85.5 2.5 %shard_map.74 = bf16[512,128]{1,0:T(8,128)(2,1)} custom-call(s32[1]{0:T(128)} %bitcast.me_ref, bf16[528,128]{1,0:T(8,128)(2,1)S(1)} %collective-permute-done.17.q_ref.tile_ref.refs_6_, bf16[528,128]{1,0:T(8,128)(2,1)S(1)} %collective-permute-done.17.q_ref.tile_ref.refs_6_, bf16[1024,128]{1,0:T(8,128)(2,1)S(1)} %collective-permute-done.5.refs_6_.k_ref.v_ref, ...), custom_call_target="tpu_custom_call" | custom-call | flops 268435456 | bytes 786432 | tf_op jit(solution)/shard_map/pallas_call | solution.py:236
  88.2 2.7 %shard_map.70 = bf16[512,128]{1,0:T(8,128)(2,1)} custom-call(s32[1]{0:T(128)} %bitcast.me_ref, bf16[528,128]{1,0:T(8,128)(2,1)S(1)} %collective-permute-done.9.q_ref.tile_ref.refs_2_, bf16[528,128]{1,0:T(8,128)(2,1)S(1)} %collective-permute-done.9.q_ref.tile_ref.refs_2_, bf16[1024,128]{1,0:T(8,128)(2,1)S(1)} %collective-permute-done.2.refs_2_.k_ref.v_ref, ...), custom_call_target="tpu_custom_call" | custom-call | flops 268435456 | bytes 786432 | tf_op jit(solution)/shard_map/pallas_call | solution.py:236
  93.0 1.9 %shard_map.68.refs_0_ = bf16[512,128]{1,0:T(8,128)(2,1)S(1)} custom-call(s32[1]{0:T(128)} %bitcast.me_ref, bf16[528,128]{1,0:T(8,128)(2,1)S(1)} %get-tuple-element.22.q_ref.tile_ref.refs_0_, bf16[528,128]{1,0:T(8,128)(2,1)S(1)} %get-tuple-element.22.q_ref.tile_ref.refs_0_, bf16[1024,128]{1,0:T(8,128)(2,1)S(1)} %copy-done.1, bf16[1024,128]{1,0:T(8,128)(2,1)S(1)} %copy-done.1, ...), custom_call_target="tpu_custom_call" | custom-call | flops 268435456 | bytes 786432 | tf_op jit(solution)/shard_map/pallas_call | solution.py:236
  96.3 1.8 %collective-permute-done.12.refs_3_ = bf16[512,128]{1,0:T(8,128)(2,1)S(1)} collective-permute-done((bf16[512,128]{1,0:T(8,128)(2,1)S(1)}, bf16[512,128]{1,0:T(8,128)(2,1)S(1)}, u32[]{:S(2)}, u32[]{:S(2)}) %collective-permute-start.12) | collective-permute-done | bytes 131104 | tf_op jit(solution)/shard_map/ppermute | solution.py:300
  (67 shorter events, 20.9 us)
Async XLA Ops:
  2.3 22.8 %collective-permute-start = (bf16[1024,128]{1,0:T(8,128)(2,1)}, bf16[1024,128]{1,0:T(8,128)(2,1)S(1)}, u32[]{:S(2)}, u32[]{:S(2)}) collective-permute-start(bf16[1024,128]{1,0:T(8,128)(2,1)} %shard_map.59), channel_id=1, source_target_pairs={{0,8},{2,10},{4,12},{6,14},{8,0},{10,2},{12,4},{14,6},{1,9},{3,11}... | collective-permute-start | bytes 786440 | tf_op jit(solution)/shard_map/ppermute | solution.py:300
  8.1 21.7 %collective-permute-start.1 = (bf16[1024,128]{1,0:T(8,128)(2,1)}, bf16[1024,128]{1,0:T(8,128)(2,1)S(1)}, u32[]{:S(2)}, u32[]{:S(2)}) collective-permute-start(bf16[1024,128]{1,0:T(8,128)(2,1)} %shard_map.62), channel_id=1, source_target_pairs={{0,2},{2,0},{4,6},{6,4},{8,10},{10,8},{12,14},{14,12},{1,3},{3,1},... | collective-permute-start | bytes 786440 | tf_op jit(solution)/shard_map/ppermute | solution.py:300
  11.2 31.9 %collective-permute-start.4 = (bf16[1024,128]{1,0:T(8,128)(2,1)}, bf16[1024,128]{1,0:T(8,128)(2,1)S(1)}, u32[]{:S(2)}, u32[]{:S(2)}) collective-permute-start(bf16[1024,128]{1,0:T(8,128)(2,1)} %shard_map.65), channel_id=1, source_target_pairs={{0,10},{2,8},{4,14},{6,12},{8,2},{10,0},{12,6},{14,4},{1,11},{3,9}... | collective-permute-start | bytes 786440 | tf_op jit(solution)/shard_map/ppermute | solution.py:300
  12.9 30.2 %collective-permute-start.2 = (bf16[1024,128]{1,0:T(8,128)(2,1)}, bf16[1024,128]{1,0:T(8,128)(2,1)S(1)}, u32[]{:S(2)}, u32[]{:S(2)}) collective-permute-start(bf16[1024,128]{1,0:T(8,128)(2,1)} %shard_map.63), channel_id=1, source_target_pairs={{0,4},{2,6},{4,0},{6,2},{8,12},{10,14},{12,8},{14,10},{1,5},{3,7},... | collective-permute-start | bytes 786440 | tf_op jit(solution)/shard_map/ppermute | solution.py:300
  16.5 26.8 %collective-permute-start.5 = (bf16[1024,128]{1,0:T(8,128)(2,1)}, bf16[1024,128]{1,0:T(8,128)(2,1)S(1)}, u32[]{:S(2)}, u32[]{:S(2)}) collective-permute-start(bf16[1024,128]{1,0:T(8,128)(2,1)} %shard_map.66), channel_id=1, source_target_pairs={{0,12},{2,14},{4,8},{6,10},{8,4},{10,6},{12,0},{14,2},{1,13},{3,15... | collective-permute-start | bytes 786440 | tf_op jit(solution)/shard_map/ppermute | solution.py:300
  25.1 40.4 %collective-permute-start.6 = (bf16[1024,128]{1,0:T(8,128)(2,1)S(1)}, bf16[1024,128]{1,0:T(8,128)(2,1)S(1)}, u32[]{:S(2)}, u32[]{:S(2)}) collective-permute-start(bf16[1024,128]{1,0:T(8,128)(2,1)S(1)} %copy-done.12), channel_id=1, source_target_pairs={{0,14},{2,12},{4,10},{6,8},{8,6},{10,4},{12,2},{14,0},{1,15},{3,13... | collective-permute-start | bytes 786440 | tf_op jit(solution)/shard_map/ppermute | solution.py:300
  29.8 37.2 %collective-permute-start.3 = (bf16[1024,128]{1,0:T(8,128)(2,1)}, bf16[1024,128]{1,0:T(8,128)(2,1)S(1)}, u32[]{:S(2)}, u32[]{:S(2)}) collective-permute-start(bf16[1024,128]{1,0:T(8,128)(2,1)} %shard_map.64), channel_id=1, source_target_pairs={{0,6},{2,4},{4,2},{6,0},{8,14},{10,12},{12,10},{14,8},{1,7},{3,5},... | collective-permute-start | bytes 786440 | tf_op jit(solution)/shard_map/ppermute | solution.py:300
  32.9 34.7 %copy-start.1 = (bf16[1024,128]{1,0:T(8,128)(2,1)S(1)}, bf16[1024,128]{1,0:T(8,128)(2,1)}, u32[]{:S(2)}) copy-start(bf16[1024,128]{1,0:T(8,128)(2,1)} %shard_map.60.k_ref.v_ref.refs_0_) | copy-start | bytes 786436
  34.1 59.0 %copy-start.2 = (bf16[528,128]{1,0:T(8,128)(2,1)}, bf16[528,128]{1,0:T(8,128)(2,1)S(1)}, u32[]{:S(2)}) copy-start(bf16[528,128]{1,0:T(8,128)(2,1)S(1)} %get-tuple-element.22.q_ref.tile_ref.refs_0_) | copy-start | bytes 405508
  43.1 18.6 %collective-permute-start.13 = (bf16[528,128]{1,0:T(8,128)(2,1)S(1)}, bf16[528,128]{1,0:T(8,128)(2,1)S(1)}, u32[]{:S(2)}, u32[]{:S(2)}) collective-permute-start(bf16[528,128]{1,0:T(8,128)(2,1)S(1)} %get-tuple-element.32), channel_id=1, source_target_pairs={{0,8},{2,10},{4,12},{6,14},{8,0},{10,2},{12,4},{14,6},{1,9},{3,11}... | collective-permute-start | bytes 405512 | tf_op jit(solution)/shard_map/ppermute | solution.py:300
  43.1 22.4 %collective-permute-start.7 = (bf16[528,128]{1,0:T(8,128)(2,1)S(1)}, bf16[528,128]{1,0:T(8,128)(2,1)S(1)}, u32[]{:S(2)}, u32[]{:S(2)}) collective-permute-start(bf16[528,128]{1,0:T(8,128)(2,1)S(1)} %get-tuple-element.26), channel_id=1, source_target_pairs={{0,2},{2,0},{4,6},{6,4},{8,10},{10,8},{12,14},{14,12},{1,3},{3,1},... | collective-permute-start | bytes 405512 | tf_op jit(solution)/shard_map/ppermute | solution.py:300
  43.3 24.3 %collective-permute-start.15 = (bf16[528,128]{1,0:T(8,128)(2,1)S(1)}, bf16[528,128]{1,0:T(8,128)(2,1)S(1)}, u32[]{:S(2)}, u32[]{:S(2)}) collective-permute-start(bf16[528,128]{1,0:T(8,128)(2,1)S(1)} %get-tuple-element.34), channel_id=1, source_target_pairs={{0,10},{2,8},{4,14},{6,12},{8,2},{10,0},{12,6},{14,4},{1,11},{3,9}... | collective-permute-start | bytes 405512 | tf_op jit(solution)/shard_map/ppermute | solution.py:300
  61.8 12.0 %collective-permute-start.19 = (bf16[528,128]{1,0:T(8,128)(2,1)S(1)}, bf16[528,128]{1,0:T(8,128)(2,1)S(1)}, u32[]{:S(2)}, u32[]{:S(2)}) collective-permute-start(bf16[528,128]{1,0:T(8,128)(2,1)S(1)} %get-tuple-element.38), channel_id=1, source_target_pairs={{0,14},{2,12},{4,10},{6,8},{8,6},{10,4},{12,2},{14,0},{1,15},{3,13... | collective-permute-start | bytes 405512 | tf_op jit(solution)/shard_map/ppermute | solution.py:300
  65.5 10.3 %copy-start.4 = (bf16[528,128]{1,0:T(8,128)(2,1)}, bf16[528,128]{1,0:T(8,128)(2,1)S(1)}, u32[]{:S(2)}) copy-start(bf16[528,128]{1,0:T(8,128)(2,1)S(1)} %collective-permute-done.7.q_ref.tile_ref.refs_1_) | copy-start | bytes 405508
  65.5 14.1 %collective-permute-start.11 = (bf16[528,128]{1,0:T(8,128)(2,1)S(1)}, bf16[528,128]{1,0:T(8,128)(2,1)S(1)}, u32[]{:S(2)}, u32[]{:S(2)}) collective-permute-start(bf16[528,128]{1,0:T(8,128)(2,1)S(1)} %get-tuple-element.30), channel_id=1, source_target_pairs={{0,6},{2,4},{4,2},{6,0},{8,14},{10,12},{12,10},{14,8},{1,7},{3,5},... | collective-permute-start | bytes 405512 | tf_op jit(solution)/shard_map/ppermute | solution.py:300
  65.5 16.1 %collective-permute-start.17 = (bf16[528,128]{1,0:T(8,128)(2,1)S(1)}, bf16[528,128]{1,0:T(8,128)(2,1)S(1)}, u32[]{:S(2)}, u32[]{:S(2)}) collective-permute-start(bf16[528,128]{1,0:T(8,128)(2,1)S(1)} %get-tuple-element.36), channel_id=1, source_target_pairs={{0,12},{2,14},{4,8},{6,10},{8,4},{10,6},{12,0},{14,2},{1,13},{3,15... | collective-permute-start | bytes 405512 | tf_op jit(solution)/shard_map/ppermute | solution.py:300
  67.0 21.0 %collective-permute-start.9 = (bf16[528,128]{1,0:T(8,128)(2,1)S(1)}, bf16[528,128]{1,0:T(8,128)(2,1)S(1)}, u32[]{:S(2)}, u32[]{:S(2)}) collective-permute-start(bf16[528,128]{1,0:T(8,128)(2,1)S(1)} %get-tuple-element.28), channel_id=1, source_target_pairs={{0,4},{2,6},{4,0},{6,2},{8,12},{10,14},{12,8},{14,10},{1,5},{3,7},... | collective-permute-start | bytes 405512 | tf_op jit(solution)/shard_map/ppermute | solution.py:300
  69.5 21.4 %collective-permute-start.16 = (bf16[512,128]{1,0:T(8,128)(2,1)S(1)}, bf16[512,128]{1,0:T(8,128)(2,1)S(1)}, u32[]{:S(2)}, u32[]{:S(2)}) collective-permute-start(bf16[512,128]{1,0:T(8,128)(2,1)S(1)} %shard_map.73), channel_id=1, source_target_pairs={{0,10},{2,8},{4,14},{6,12},{8,2},{10,0},{12,6},{14,4},{1,11},{3,9}... | collective-permute-start | bytes 393224 | tf_op jit(solution)/shard_map/ppermute | solution.py:300
  73.8 18.6 %collective-permute-start.14 = (bf16[512,128]{1,0:T(8,128)(2,1)S(1)}, bf16[512,128]{1,0:T(8,128)(2,1)S(1)}, u32[]{:S(2)}, u32[]{:S(2)}) collective-permute-start(bf16[512,128]{1,0:T(8,128)(2,1)S(1)} %shard_map.72), channel_id=1, source_target_pairs={{0,8},{2,10},{4,12},{6,14},{8,0},{10,2},{12,4},{14,6},{1,9},{3,11}... | collective-permute-start | bytes 393224 | tf_op jit(solution)/shard_map/ppermute | solution.py:300
  79.6 16.7 %collective-permute-start.8 = (bf16[512,128]{1,0:T(8,128)(2,1)S(1)}, bf16[512,128]{1,0:T(8,128)(2,1)S(1)}, u32[]{:S(2)}, u32[]{:S(2)}) collective-permute-start(bf16[512,128]{1,0:T(8,128)(2,1)S(1)} %shard_map.69), channel_id=1, source_target_pairs={{0,2},{2,0},{4,6},{6,4},{8,10},{10,8},{12,14},{14,12},{1,3},{3,1},... | collective-permute-start | bytes 393224 | tf_op jit(solution)/shard_map/ppermute | solution.py:300
  81.7 14.6 %collective-permute-start.20 = (bf16[512,128]{1,0:T(8,128)(2,1)S(1)}, bf16[512,128]{1,0:T(8,128)(2,1)S(1)}, u32[]{:S(2)}, u32[]{:S(2)}) collective-permute-start(bf16[512,128]{1,0:T(8,128)(2,1)S(1)} %shard_map.75), channel_id=1, source_target_pairs={{0,14},{2,12},{4,10},{6,8},{8,6},{10,4},{12,2},{14,0},{1,15},{3,13... | collective-permute-start | bytes 393224 | tf_op jit(solution)/shard_map/ppermute | solution.py:300
  88.1 10.0 %collective-permute-start.12 = (bf16[512,128]{1,0:T(8,128)(2,1)S(1)}, bf16[512,128]{1,0:T(8,128)(2,1)S(1)}, u32[]{:S(2)}, u32[]{:S(2)}) collective-permute-start(bf16[512,128]{1,0:T(8,128)(2,1)S(1)} %shard_map.71), channel_id=1, source_target_pairs={{0,6},{2,4},{4,2},{6,0},{8,14},{10,12},{12,10},{14,8},{1,7},{3,5},... | collective-permute-start | bytes 393224 | tf_op jit(solution)/shard_map/ppermute | solution.py:300
  90.9 7.2 %collective-permute-start.18 = (bf16[512,128]{1,0:T(8,128)(2,1)}, bf16[512,128]{1,0:T(8,128)(2,1)S(1)}, u32[]{:S(2)}, u32[]{:S(2)}) collective-permute-start(bf16[512,128]{1,0:T(8,128)(2,1)} %shard_map.74), channel_id=1, source_target_pairs={{0,12},{2,14},{4,8},{6,10},{8,4},{10,6},{12,0},{14,2},{1,13},{3,15... | collective-permute-start | bytes 393224 | tf_op jit(solution)/shard_map/ppermute | solution.py:300
  92.4 6.6 %collective-permute-start.10 = (bf16[512,128]{1,0:T(8,128)(2,1)}, bf16[512,128]{1,0:T(8,128)(2,1)S(1)}, u32[]{:S(2)}, u32[]{:S(2)}) collective-permute-start(bf16[512,128]{1,0:T(8,128)(2,1)} %shard_map.70), channel_id=1, source_target_pairs={{0,4},{2,6},{4,0},{6,2},{8,12},{10,14},{12,8},{14,10},{1,5},{3,7},... | collective-permute-start | bytes 393224 | tf_op jit(solution)/shard_map/ppermute | solution.py:300
  (11 other events, 44.4 us)

commit v8 on v7

--- a/solution.py
+++ b/solution.py
@@ -315,14 +315,14 @@
     pooled_q, *pieces = cut_queries(
         here, after(query_rows, got[0, members // 2], packed[0]), key_rows, chosen
     )
-    exchange(pieces, 1, near, 2, near_done)
+    exchange(pieces, 1, [2, 1, 3], 2, near_done)
     exchange(pieces, 1, far[::-1], 3, far_done)
     packed = packed[:1] + [got[0, d] for d in range(1, members)]
     queries = pieces[:1] + [got[1, d] for d in range(1, members)]
     sort_logits = logits_of(here, pooled_q, queries)
 
     outputs = [None] * members
-    for d in far[::-1] + near + [0]:
+    for d in [0] + far[::-1] + near:
         outputs[d] = attend(here, d, queries[d], packed)
         if d:
             outputs[d] = send(outputs[d], d)

time: 101 us -> 99.7 us (0.987)
  transfers between devices with their start and end apart: 21 -> 21, of which waited for: 5 -> 4; matrix products, arithmetic and copies ran while one was open for 0% -> 0% of each run, Pallas kernels for 30% -> 31%
where the time goes in v8:
time: 99.7 us; the launch traced here: 99.4 us
  starting transfers between devices  41 us (41%)
  Pallas kernels  33.4 us (34%)
  waiting for transfers between devices  22.2 us (22%)
  local copies, waits for them, and re-layouts  1.92 us (2%)
    ppermute x21, starting transfers between devices, send(): return lax.ppermute(x, 'context', [(i, i ^ d) for i in range(members)])  41 us
    ppermute x21, waiting for transfers between devices, send(): return lax.ppermute(x, 'context', [(i, i ^ d) for i in range(members)])  22.2 us
    pallas_call x8, Pallas kernels, attend(): pl.pallas_call(attend_kernel, grid_spec=pltpu.PrefetchScalarGridSpec(num_...  16.4 us
    pallas_call x8, Pallas kernels, pack_head(): pl.pallas_call(pack_kernel, grid_spec=pltpu.PrefetchScalarGridSpec(num_sc...  13.7 us
  transfers between devices with their start and end apart: 21, of which 4 were waited for; matrix products, arithmetic and copies ran while one was open for 0% of the time, Pallas kernels for 31%

profile of v8, /device:TPU:0, one launch (start us, length us, event | category | flops | bytes accessed | tf_op | source)
XLA Modules:
  0.0 99.4 jit_solution(3607866133558339149)
XLA Ops:
  2.3 4.0 %collective-permute-start = (bf16[1024,128]{1,0:T(8,128)(2,1)}, bf16[1024,128]{1,0:T(8,128)(2,1)S(1)}, u32[]{:S(2)}, u32[]{:S(2)}) collective-permute-start(bf16[1024,128]{1,0:T(8,128)(2,1)} %shard_map.59), channel_id=1, source_target_pairs={{0,8},{2,10},{4,12},{6,14},{8,0},{10,2},{12,4},{14,6},{1,9},{3,11}... | collective-permute-start | bytes 786440 | tf_op jit(solution)/shard_map/ppermute | solution.py:300
  12.9 1.9 %collective-permute-start.2 = (bf16[1024,128]{1,0:T(8,128)(2,1)}, bf16[1024,128]{1,0:T(8,128)(2,1)S(1)}, u32[]{:S(2)}, u32[]{:S(2)}) collective-permute-start(bf16[1024,128]{1,0:T(8,128)(2,1)} %shard_map.63), channel_id=1, source_target_pairs={{0,4},{2,6},{4,0},{6,2},{8,12},{10,14},{12,8},{14,10},{1,5},{3,7},... | collective-permute-start | bytes 786440 | tf_op jit(solution)/shard_map/ppermute | solution.py:300
  14.8 1.7 %shard_map.66 = bf16[1024,128]{1,0:T(8,128)(2,1)} custom-call(s32[1]{0:T(128)} %bitcast.me_ref, bf16[512,1024]{1,0:T(8,128)(2,1)} %k_ref.17, bf16[512,1024]{1,0:T(8,128)(2,1)} %v_ref.15), custom_call_target="tpu_custom_call" | custom-call | bytes 524288 | tf_op jit(solution)/shard_map/pallas_call | solution.py:127
  16.5 2.5 %collective-permute-start.5 = (bf16[1024,128]{1,0:T(8,128)(2,1)}, bf16[1024,128]{1,0:T(8,128)(2,1)S(1)}, u32[]{:S(2)}, u32[]{:S(2)}) collective-permute-start(bf16[1024,128]{1,0:T(8,128)(2,1)} %shard_map.66), channel_id=1, source_target_pairs={{0,12},{2,14},{4,8},{6,10},{8,4},{10,6},{12,0},{14,2},{1,13},{3,15... | collective-permute-start | bytes 786440 | tf_op jit(solution)/shard_map/ppermute | solution.py:300
  20.7 1.7 %shard_map.64 = bf16[1024,128]{1,0:T(8,128)(2,1)} custom-call(s32[1]{0:T(128)} %bitcast.me_ref, bf16[512,1024]{1,0:T(8,128)(2,1)} %k_ref.17, bf16[512,1024]{1,0:T(8,128)(2,1)} %v_ref.15), custom_call_target="tpu_custom_call" | custom-call | bytes 524288 | tf_op jit(solution)/shard_map/pallas_call | solution.py:127
  22.4 2.7 %collective-permute-done.refs_4_.k_ref.v_ref = bf16[1024,128]{1,0:T(8,128)(2,1)S(1)} collective-permute-done((bf16[1024,128]{1,0:T(8,128)(2,1)}, bf16[1024,128]{1,0:T(8,128)(2,1)S(1)}, u32[]{:S(2)}, u32[]{:S(2)}) %collective-permute-start) | collective-permute-done | bytes 262176 | tf_op jit(solution)/shard_map/ppermute | solution.py:300
  25.1 4.6 %collective-permute-start.6 = (bf16[1024,128]{1,0:T(8,128)(2,1)S(1)}, bf16[1024,128]{1,0:T(8,128)(2,1)S(1)}, u32[]{:S(2)}, u32[]{:S(2)}) collective-permute-start(bf16[1024,128]{1,0:T(8,128)(2,1)S(1)} %copy-done.12), channel_id=1, source_target_pairs={{0,14},{2,12},{4,10},{6,8},{8,6},{10,4},{12,2},{14,0},{1,15},{3,13... | collective-permute-start | bytes 786440 | tf_op jit(solution)/shard_map/ppermute | solution.py:300
  29.8 1.8 %shard_map.60.k_ref.v_ref.refs_0_ = bf16[1024,128]{1,0:T(8,128)(2,1)} custom-call(s32[1]{0:T(128)} %bitcast.me_ref, bf16[512,1024]{1,0:T(8,128)(2,1)} %k_ref.17, bf16[512,1024]{1,0:T(8,128)(2,1)} %v_ref.15), custom_call_target="tpu_custom_call" | custom-call | bytes 524288 | tf_op jit(solution)/shard_map/pallas_call | solution.py:127
  34.1 9.0 %collective-permute-done.4.refs_5_.k_ref.v_ref = bf16[1024,128]{1,0:T(8,128)(2,1)S(1)} collective-permute-done((bf16[1024,128]{1,0:T(8,128)(2,1)}, bf16[1024,128]{1,0:T(8,128)(2,1)S(1)}, u32[]{:S(2)}, u32[]{:S(2)}) %collective-permute-start.4) | collective-permute-done | bytes 262176 | tf_op jit(solution)/shard_map/ppermute | solution.py:300
  43.1 3.0 %collective-permute-start.9 = (bf16[528,128]{1,0:T(8,128)(2,1)S(1)}, bf16[528,128]{1,0:T(8,128)(2,1)S(1)}, u32[]{:S(2)}, u32[]{:S(2)}) collective-permute-start(bf16[528,128]{1,0:T(8,128)(2,1)S(1)} %get-tuple-element.28), channel_id=1, source_target_pairs={{0,4},{2,6},{4,0},{6,2},{8,12},{10,14},{12,8},{14,10},{1,5},{3,7},... | collective-permute-start | bytes 405512 | tf_op jit(solution)/shard_map/ppermute | solution.py:300
  46.1 7.0 %collective-permute-start.15 = (bf16[528,128]{1,0:T(8,128)(2,1)S(1)}, bf16[528,128]{1,0:T(8,128)(2,1)S(1)}, u32[]{:S(2)}, u32[]{:S(2)}) collective-permute-start(bf16[528,128]{1,0:T(8,128)(2,1)S(1)} %get-tuple-element.34), channel_id=1, source_target_pairs={{0,10},{2,8},{4,14},{6,12},{8,2},{10,0},{12,6},{14,4},{1,11},{3,9}... | collective-permute-start | bytes 405512 | tf_op jit(solution)/shard_map/ppermute | solution.py:300
  53.2 8.6 %collective-permute-done.13.q_ref.tile_ref.refs_4_ = bf16[528,128]{1,0:T(8,128)(2,1)S(1)} collective-permute-done((bf16[528,128]{1,0:T(8,128)(2,1)S(1)}, bf16[528,128]{1,0:T(8,128)(2,1)S(1)}, u32[]{:S(2)}, u32[]{:S(2)}) %collective-permute-start.13) | collective-permute-done | bytes 135200 | tf_op jit(solution)/shard_map/ppermute | solution.py:300
  61.8 3.7 %collective-permute-start.19 = (bf16[528,128]{1,0:T(8,128)(2,1)S(1)}, bf16[528,128]{1,0:T(8,128)(2,1)S(1)}, u32[]{:S(2)}, u32[]{:S(2)}) collective-permute-start(bf16[528,128]{1,0:T(8,128)(2,1)S(1)} %get-tuple-element.38), channel_id=1, source_target_pairs={{0,14},{2,12},{4,10},{6,8},{8,6},{10,4},{12,2},{14,0},{1,15},{3,13... | collective-permute-start | bytes 405512 | tf_op jit(solution)/shard_map/ppermute | solution.py:300
  67.2 1.9 %shard_map.73 = bf16[512,128]{1,0:T(8,128)(2,1)S(1)} custom-call(s32[1]{0:T(128)} %bitcast.me_ref, bf16[528,128]{1,0:T(8,128)(2,1)S(1)} %collective-permute-done.15.q_ref.tile_ref.refs_5_, bf16[528,128]{1,0:T(8,128)(2,1)S(1)} %collective-permute-done.15.q_ref.tile_ref.refs_5_, bf16[1024,128]{1,0:T(8,128)(2,1)S(1)} %collective-permute-done.4.refs_5_.k_ref.v_ref, ...), custom_call_target="tpu_custom_call" | custom-call | flops 268435456 | bytes 786432 | tf_op jit(solution)/shard_map/pallas_call | solution.py:236
  69.0 3.4 %collective-permute-start.16 = (bf16[512,128]{1,0:T(8,128)(2,1)S(1)}, bf16[512,128]{1,0:T(8,128)(2,1)S(1)}, u32[]{:S(2)}, u32[]{:S(2)}) collective-permute-start(bf16[512,128]{1,0:T(8,128)(2,1)S(1)} %shard_map.73), channel_id=1, source_target_pairs={{0,10},{2,8},{4,14},{6,12},{8,2},{10,0},{12,6},{14,4},{1,11},{3,9}... | collective-permute-start | bytes 393224 | tf_op jit(solution)/shard_map/ppermute | solution.py:300
  72.4 1.9 %shard_map.72 = bf16[512,128]{1,0:T(8,128)(2,1)S(1)} custom-call(s32[1]{0:T(128)} %bitcast.me_ref, bf16[528,128]{1,0:T(8,128)(2,1)S(1)} %collective-permute-done.13.q_ref.tile_ref.refs_4_, bf16[528,128]{1,0:T(8,128)(2,1)S(1)} %collective-permute-done.13.q_ref.tile_ref.refs_4_, bf16[1024,128]{1,0:T(8,128)(2,1)S(1)} %collective-permute-done.refs_4_.k_ref.v_ref, ...), custom_call_target="tpu_custom_call" | custom-call | flops 268435456 | bytes 786432 | tf_op jit(solution)/shard_map/pallas_call | solution.py:236
  75.3 1.9 %shard_map.70 = bf16[512,128]{1,0:T(8,128)(2,1)S(1)} custom-call(s32[1]{0:T(128)} %bitcast.me_ref, bf16[528,128]{1,0:T(8,128)(2,1)S(1)} %collective-permute-done.9.q_ref.tile_ref.refs_2_, bf16[528,128]{1,0:T(8,128)(2,1)S(1)} %collective-permute-done.9.q_ref.tile_ref.refs_2_, bf16[1024,128]{1,0:T(8,128)(2,1)S(1)} %collective-permute-done.2.refs_2_.k_ref.v_ref, ...), custom_call_target="tpu_custom_call" | custom-call | flops 268435456 | bytes 786432 | tf_op jit(solution)/shard_map/pallas_call | solution.py:236
  77.2 1.9 %shard_map.75 = bf16[512,128]{1,0:T(8,128)(2,1)S(1)} custom-call(s32[1]{0:T(128)} %bitcast.me_ref, bf16[528,128]{1,0:T(8,128)(2,1)S(1)} %collective-permute-done.19.q_ref.tile_ref.refs_7_, bf16[528,128]{1,0:T(8,128)(2,1)S(1)} %collective-permute-done.19.q_ref.tile_ref.refs_7_, bf16[1024,128]{1,0:T(8,128)(2,1)S(1)} %collective-permute-done.6.refs_7_.k_ref.v_ref, ...), custom_call_target="tpu_custom_call" | custom-call | flops 268435456 | bytes 786432 | tf_op jit(solution)/shard_map/pallas_call | solution.py:236
  79.8 1.9 %shard_map.71 = bf16[512,128]{1,0:T(8,128)(2,1)S(1)} custom-call(s32[1]{0:T(128)} %bitcast.me_ref, bf16[528,128]{1,0:T(8,128)(2,1)S(1)} %collective-permute-done.11.q_ref.tile_ref.refs_3_, bf16[528,128]{1,0:T(8,128)(2,1)S(1)} %collective-permute-done.11.q_ref.tile_ref.refs_3_, bf16[1024,128]{1,0:T(8,128)(2,1)S(1)} %collective-permute-done.3.refs_3_.k_ref.v_ref, ...), custom_call_target="tpu_custom_call" | custom-call | flops 268435456 | bytes 786432 | tf_op jit(solution)/shard_map/pallas_call | solution.py:236
  81.7 3.8 %collective-permute-start.20 = (bf16[512,128]{1,0:T(8,128)(2,1)S(1)}, bf16[512,128]{1,0:T(8,128)(2,1)S(1)}, u32[]{:S(2)}, u32[]{:S(2)}) collective-permute-start(bf16[512,128]{1,0:T(8,128)(2,1)S(1)} %shard_map.75), channel_id=1, source_target_pairs={{0,14},{2,12},{4,10},{6,8},{8,6},{10,4},{12,2},{14,0},{1,15},{3,13... | collective-permute-start | bytes 393224 | tf_op jit(solution)/shard_map/ppermute | solution.py:300
  85.5 2.5 %shard_map.74 = bf16[512,128]{1,0:T(8,128)(2,1)} custom-call(s32[1]{0:T(128)} %bitcast.me_ref, bf16[528,128]{1,0:T(8,128)(2,1)S(1)} %collective-permute-done.17.q_ref.tile_ref.refs_6_, bf16[528,128]{1,0:T(8,128)(2,1)S(1)} %collective-permute-done.17.q_ref.tile_ref.refs_6_, bf16[1024,128]{1,0:T(8,128)(2,1)S(1)} %collective-permute-done.5.refs_6_.k_ref.v_ref, ...), custom_call_target="tpu_custom_call" | custom-call | flops 268435456 | bytes 786432 | tf_op jit(solution)/shard_map/pallas_call | solution.py:236
  88.2 2.7 %shard_map.69 = bf16[512,128]{1,0:T(8,128)(2,1)} custom-call(s32[1]{0:T(128)} %bitcast.me_ref, bf16[528,128]{1,0:T(8,128)(2,1)S(1)} %collective-permute-done.7.q_ref.tile_ref.refs_1_, bf16[528,128]{1,0:T(8,128)(2,1)S(1)} %collective-permute-done.7.q_ref.tile_ref.refs_1_, bf16[1024,128]{1,0:T(8,128)(2,1)S(1)} %collective-permute-done.1.refs_1_.k_ref.v_ref, ...), custom_call_target="tpu_custom_call" | custom-call | flops 268435456 | bytes 786432 | tf_op jit(solution)/shard_map/pallas_call | solution.py:236
  93.0 1.9 %shard_map.68.refs_0_ = bf16[512,128]{1,0:T(8,128)(2,1)S(1)} custom-call(s32[1]{0:T(128)} %bitcast.me_ref, bf16[528,128]{1,0:T(8,128)(2,1)S(1)} %get-tuple-element.22.q_ref.tile_ref.refs_0_, bf16[528,128]{1,0:T(8,128)(2,1)S(1)} %get-tuple-element.22.q_ref.tile_ref.refs_0_, bf16[1024,128]{1,0:T(8,128)(2,1)S(1)} %copy-done.1, bf16[1024,128]{1,0:T(8,128)(2,1)S(1)} %copy-done.1, ...), custom_call_target="tpu_custom_call" | custom-call | flops 268435456 | bytes 786432 | tf_op jit(solution)/shard_map/pallas_call | solution.py:236
  96.3 1.8 %collective-permute-done.18.refs_6_ = bf16[512,128]{1,0:T(8,128)(2,1)S(1)} collective-permute-done((bf16[512,128]{1,0:T(8,128)(2,1)}, bf16[512,128]{1,0:T(8,128)(2,1)S(1)}, u32[]{:S(2)}, u32[]{:S(2)}) %collective-permute-start.18) | collective-permute-done | bytes 131104 | tf_op jit(solution)/shard_map/ppermute | solution.py:300
  (67 shorter events, 20.7 us)
Async XLA Ops:
  2.3 22.8 %collective-permute-start = (bf16[1024,128]{1,0:T(8,128)(2,1)}, bf16[1024,128]{1,0:T(8,128)(2,1)S(1)}, u32[]{:S(2)}, u32[]{:S(2)}) collective-permute-start(bf16[1024,128]{1,0:T(8,128)(2,1)} %shard_map.59), channel_id=1, source_target_pairs={{0,8},{2,10},{4,12},{6,14},{8,0},{10,2},{12,4},{14,6},{1,9},{3,11}... | collective-permute-start | bytes 786440 | tf_op jit(solution)/shard_map/ppermute | solution.py:300
  8.1 21.7 %collective-permute-start.1 = (bf16[1024,128]{1,0:T(8,128)(2,1)}, bf16[1024,128]{1,0:T(8,128)(2,1)S(1)}, u32[]{:S(2)}, u32[]{:S(2)}) collective-permute-start(bf16[1024,128]{1,0:T(8,128)(2,1)} %shard_map.62), channel_id=1, source_target_pairs={{0,2},{2,0},{4,6},{6,4},{8,10},{10,8},{12,14},{14,12},{1,3},{3,1},... | collective-permute-start | bytes 786440 | tf_op jit(solution)/shard_map/ppermute | solution.py:300
  11.2 31.9 %collective-permute-start.4 = (bf16[1024,128]{1,0:T(8,128)(2,1)}, bf16[1024,128]{1,0:T(8,128)(2,1)S(1)}, u32[]{:S(2)}, u32[]{:S(2)}) collective-permute-start(bf16[1024,128]{1,0:T(8,128)(2,1)} %shard_map.65), channel_id=1, source_target_pairs={{0,10},{2,8},{4,14},{6,12},{8,2},{10,0},{12,6},{14,4},{1,11},{3,9}... | collective-permute-start | bytes 786440 | tf_op jit(solution)/shard_map/ppermute | solution.py:300
  12.9 30.2 %collective-permute-start.2 = (bf16[1024,128]{1,0:T(8,128)(2,1)}, bf16[1024,128]{1,0:T(8,128)(2,1)S(1)}, u32[]{:S(2)}, u32[]{:S(2)}) collective-permute-start(bf16[1024,128]{1,0:T(8,128)(2,1)} %shard_map.63), channel_id=1, source_target_pairs={{0,4},{2,6},{4,0},{6,2},{8,12},{10,14},{12,8},{14,10},{1,5},{3,7},... | collective-permute-start | bytes 786440 | tf_op jit(solution)/shard_map/ppermute | solution.py:300
  16.5 29.6 %collective-permute-start.5 = (bf16[1024,128]{1,0:T(8,128)(2,1)}, bf16[1024,128]{1,0:T(8,128)(2,1)S(1)}, u32[]{:S(2)}, u32[]{:S(2)}) collective-permute-start(bf16[1024,128]{1,0:T(8,128)(2,1)} %shard_map.66), channel_id=1, source_target_pairs={{0,12},{2,14},{4,8},{6,10},{8,4},{10,6},{12,0},{14,2},{1,13},{3,15... | collective-permute-start | bytes 786440 | tf_op jit(solution)/shard_map/ppermute | solution.py:300
  25.1 40.4 %collective-permute-start.6 = (bf16[1024,128]{1,0:T(8,128)(2,1)S(1)}, bf16[1024,128]{1,0:T(8,128)(2,1)S(1)}, u32[]{:S(2)}, u32[]{:S(2)}) collective-permute-start(bf16[1024,128]{1,0:T(8,128)(2,1)S(1)} %copy-done.12), channel_id=1, source_target_pairs={{0,14},{2,12},{4,10},{6,8},{8,6},{10,4},{12,2},{14,0},{1,15},{3,13... | collective-permute-start | bytes 786440 | tf_op jit(solution)/shard_map/ppermute | solution.py:300
  29.8 37.2 %collective-permute-start.3 = (bf16[1024,128]{1,0:T(8,128)(2,1)}, bf16[1024,128]{1,0:T(8,128)(2,1)S(1)}, u32[]{:S(2)}, u32[]{:S(2)}) collective-permute-start(bf16[1024,128]{1,0:T(8,128)(2,1)} %shard_map.64), channel_id=1, source_target_pairs={{0,6},{2,4},{4,2},{6,0},{8,14},{10,12},{12,10},{14,8},{1,7},{3,5},... | collective-permute-start | bytes 786440 | tf_op jit(solution)/shard_map/ppermute | solution.py:300
  32.9 34.3 %copy-start.1 = (bf16[1024,128]{1,0:T(8,128)(2,1)S(1)}, bf16[1024,128]{1,0:T(8,128)(2,1)}, u32[]{:S(2)}) copy-start(bf16[1024,128]{1,0:T(8,128)(2,1)} %shard_map.60.k_ref.v_ref.refs_0_) | copy-start | bytes 786436
  34.1 58.9 %copy-start.2 = (bf16[528,128]{1,0:T(8,128)(2,1)}, bf16[528,128]{1,0:T(8,128)(2,1)S(1)}, u32[]{:S(2)}) copy-start(bf16[528,128]{1,0:T(8,128)(2,1)S(1)} %get-tuple-element.22.q_ref.tile_ref.refs_0_) | copy-start | bytes 405508
  43.1 18.6 %collective-permute-start.13 = (bf16[528,128]{1,0:T(8,128)(2,1)S(1)}, bf16[528,128]{1,0:T(8,128)(2,1)S(1)}, u32[]{:S(2)}, u32[]{:S(2)}) collective-permute-start(bf16[528,128]{1,0:T(8,128)(2,1)S(1)} %get-tuple-element.32), channel_id=1, source_target_pairs={{0,8},{2,10},{4,12},{6,14},{8,0},{10,2},{12,4},{14,6},{1,9},{3,11}... | collective-permute-start | bytes 405512 | tf_op jit(solution)/shard_map/ppermute | solution.py:300
  43.1 22.4 %collective-permute-start.9 = (bf16[528,128]{1,0:T(8,128)(2,1)S(1)}, bf16[528,128]{1,0:T(8,128)(2,1)S(1)}, u32[]{:S(2)}, u32[]{:S(2)}) collective-permute-start(bf16[528,128]{1,0:T(8,128)(2,1)S(1)} %get-tuple-element.28), channel_id=1, source_target_pairs={{0,4},{2,6},{4,0},{6,2},{8,12},{10,14},{12,8},{14,10},{1,5},{3,7},... | collective-permute-start | bytes 405512 | tf_op jit(solution)/shard_map/ppermute | solution.py:300
  46.1 21.0 %collective-permute-start.15 = (bf16[528,128]{1,0:T(8,128)(2,1)S(1)}, bf16[528,128]{1,0:T(8,128)(2,1)S(1)}, u32[]{:S(2)}, u32[]{:S(2)}) collective-permute-start(bf16[528,128]{1,0:T(8,128)(2,1)S(1)} %get-tuple-element.34), channel_id=1, source_target_pairs={{0,10},{2,8},{4,14},{6,12},{8,2},{10,0},{12,6},{14,4},{1,11},{3,9}... | collective-permute-start | bytes 405512 | tf_op jit(solution)/shard_map/ppermute | solution.py:300
  61.8 10.6 %copy-start.3 = (bf16[528,128]{1,0:T(8,128)(2,1)}, bf16[528,128]{1,0:T(8,128)(2,1)S(1)}, u32[]{:S(2)}) copy-start(bf16[528,128]{1,0:T(8,128)(2,1)S(1)} %collective-permute-done.13.q_ref.tile_ref.refs_4_) | copy-start | bytes 405508
  61.8 12.5 %collective-permute-start.19 = (bf16[528,128]{1,0:T(8,128)(2,1)S(1)}, bf16[528,128]{1,0:T(8,128)(2,1)S(1)}, u32[]{:S(2)}, u32[]{:S(2)}) collective-permute-start(bf16[528,128]{1,0:T(8,128)(2,1)S(1)} %get-tuple-element.38), channel_id=1, source_target_pairs={{0,14},{2,12},{4,10},{6,8},{8,6},{10,4},{12,2},{14,0},{1,15},{3,13... | collective-permute-start | bytes 405512 | tf_op jit(solution)/shard_map/ppermute | solution.py:300
  65.5 13.5 %collective-permute-start.11 = (bf16[528,128]{1,0:T(8,128)(2,1)S(1)}, bf16[528,128]{1,0:T(8,128)(2,1)S(1)}, u32[]{:S(2)}, u32[]{:S(2)}) collective-permute-start(bf16[528,128]{1,0:T(8,128)(2,1)S(1)} %get-tuple-element.30), channel_id=1, source_target_pairs={{0,6},{2,4},{4,2},{6,0},{8,14},{10,12},{12,10},{14,8},{1,7},{3,5},... | collective-permute-start | bytes 405512 | tf_op jit(solution)/shard_map/ppermute | solution.py:300
  65.5 16.2 %collective-permute-start.17 = (bf16[528,128]{1,0:T(8,128)(2,1)S(1)}, bf16[528,128]{1,0:T(8,128)(2,1)S(1)}, u32[]{:S(2)}, u32[]{:S(2)}) collective-permute-start(bf16[528,128]{1,0:T(8,128)(2,1)S(1)} %get-tuple-element.36), channel_id=1, source_target_pairs={{0,12},{2,14},{4,8},{6,10},{8,4},{10,6},{12,0},{14,2},{1,13},{3,15... | collective-permute-start | bytes 405512 | tf_op jit(solution)/shard_map/ppermute | solution.py:300
  67.0 21.1 %collective-permute-start.7 = (bf16[528,128]{1,0:T(8,128)(2,1)S(1)}, bf16[528,128]{1,0:T(8,128)(2,1)S(1)}, u32[]{:S(2)}, u32[]{:S(2)}) collective-permute-start(bf16[528,128]{1,0:T(8,128)(2,1)S(1)} %get-tuple-element.26), channel_id=1, source_target_pairs={{0,2},{2,0},{4,6},{6,4},{8,10},{10,8},{12,14},{14,12},{1,3},{3,1},... | collective-permute-start | bytes 405512 | tf_op jit(solution)/shard_map/ppermute | solution.py:300
  69.0 21.9 %collective-permute-start.16 = (bf16[512,128]{1,0:T(8,128)(2,1)S(1)}, bf16[512,128]{1,0:T(8,128)(2,1)S(1)}, u32[]{:S(2)}, u32[]{:S(2)}) collective-permute-start(bf16[512,128]{1,0:T(8,128)(2,1)S(1)} %shard_map.73), channel_id=1, source_target_pairs={{0,10},{2,8},{4,14},{6,12},{8,2},{10,0},{12,6},{14,4},{1,11},{3,9}... | collective-permute-start | bytes 393224 | tf_op jit(solution)/shard_map/ppermute | solution.py:300
  74.3 18.1 %collective-permute-start.14 = (bf16[512,128]{1,0:T(8,128)(2,1)S(1)}, bf16[512,128]{1,0:T(8,128)(2,1)S(1)}, u32[]{:S(2)}, u32[]{:S(2)}) collective-permute-start(bf16[512,128]{1,0:T(8,128)(2,1)S(1)} %shard_map.72), channel_id=1, source_target_pairs={{0,8},{2,10},{4,12},{6,14},{8,0},{10,2},{12,4},{14,6},{1,9},{3,11}... | collective-permute-start | bytes 393224 | tf_op jit(solution)/shard_map/ppermute | solution.py:300
  79.1 17.2 %collective-permute-start.10 = (bf16[512,128]{1,0:T(8,128)(2,1)S(1)}, bf16[512,128]{1,0:T(8,128)(2,1)S(1)}, u32[]{:S(2)}, u32[]{:S(2)}) collective-permute-start(bf16[512,128]{1,0:T(8,128)(2,1)S(1)} %shard_map.70), channel_id=1, source_target_pairs={{0,4},{2,6},{4,0},{6,2},{8,12},{10,14},{12,8},{14,10},{1,5},{3,7},... | collective-permute-start | bytes 393224 | tf_op jit(solution)/shard_map/ppermute | solution.py:300
  81.7 14.6 %collective-permute-start.20 = (bf16[512,128]{1,0:T(8,128)(2,1)S(1)}, bf16[512,128]{1,0:T(8,128)(2,1)S(1)}, u32[]{:S(2)}, u32[]{:S(2)}) collective-permute-start(bf16[512,128]{1,0:T(8,128)(2,1)S(1)} %shard_map.75), channel_id=1, source_target_pairs={{0,14},{2,12},{4,10},{6,8},{8,6},{10,4},{12,2},{14,0},{1,15},{3,13... | collective-permute-start | bytes 393224 | tf_op jit(solution)/shard_map/ppermute | solution.py:300
  88.1 8.2 %collective-permute-start.12 = (bf16[512,128]{1,0:T(8,128)(2,1)S(1)}, bf16[512,128]{1,0:T(8,128)(2,1)S(1)}, u32[]{:S(2)}, u32[]{:S(2)}) collective-permute-start(bf16[512,128]{1,0:T(8,128)(2,1)S(1)} %shard_map.71), channel_id=1, source_target_pairs={{0,6},{2,4},{4,2},{6,0},{8,14},{10,12},{12,10},{14,8},{1,7},{3,5},... | collective-permute-start | bytes 393224 | tf_op jit(solution)/shard_map/ppermute | solution.py:300
  90.9 7.2 %collective-permute-start.18 = (bf16[512,128]{1,0:T(8,128)(2,1)}, bf16[512,128]{1,0:T(8,128)(2,1)S(1)}, u32[]{:S(2)}, u32[]{:S(2)}) collective-permute-start(bf16[512,128]{1,0:T(8,128)(2,1)} %shard_map.74), channel_id=1, source_target_pairs={{0,12},{2,14},{4,8},{6,10},{8,4},{10,6},{12,0},{14,2},{1,13},{3,15... | collective-permute-start | bytes 393224 | tf_op jit(solution)/shard_map/ppermute | solution.py:300
  92.4 5.7 %collective-permute-start.8 = (bf16[512,128]{1,0:T(8,128)(2,1)}, bf16[512,128]{1,0:T(8,128)(2,1)S(1)}, u32[]{:S(2)}, u32[]{:S(2)}) collective-permute-start(bf16[512,128]{1,0:T(8,128)(2,1)} %shard_map.69), channel_id=1, source_target_pairs={{0,2},{2,0},{4,6},{6,4},{8,10},{10,8},{12,14},{14,12},{1,3},{3,1},... | collective-permute-start | bytes 393224 | tf_op jit(solution)/shard_map/ppermute | solution.py:300
  (11 other events, 43.5 us)

commit v9 on v8

--- a/solution.py
+++ b/solution.py
@@ -152,15 +152,19 @@
     for d in range(heads):
         first = pl.multiple_of((me_ref[0] ^ d) * DH, DH)
         pieces[d][pl.ds(0, BS), :] = q_ref[:, pl.ds(first, DH)]
-        pieces[d][pl.ds(BS, heads), :] = pooled_keys
-        pieces[d][pl.ds(BS + heads, TILE), :] = chosen_ref[me_ref[0] ^ d]
+        row = lax.broadcasted_iota(jnp.int32, pooled_keys.shape, 0)
+        pieces[d][pl.ds(BS, heads), :] = jnp.where(
+            row == (me_ref[0] ^ d),
+            chosen_ref[me_ref[0] ^ d].astype(F32),
+            pooled_keys.astype(F32),
+        ).astype(BF16)
 
 
 def cut_queries(me, q, k, chosen):
     tok, width = q.shape
     heads = width // DH
     whole = pl.BlockSpec((tok, width), lambda i, m: (0, 0))
-    piece = pl.BlockSpec((tok + heads + TILE, DH), lambda i, m: (0, 0))
+    piece = pl.BlockSpec((tok + heads, DH), lambda i, m: (0, 0))
     return pl.pallas_call(
         functools.partial(cut_kernel, heads),
         grid_spec=pltpu.PrefetchScalarGridSpec(
@@ -170,7 +174,7 @@
             out_specs=[pl.BlockSpec((heads, DH), lambda i, m: (0, 0))] + [piece] * heads,
         ),
         out_shape=[jax.ShapeDtypeStruct((heads, DH), BF16)]
-        + [jax.ShapeDtypeStruct((tok + heads + TILE, DH), BF16)] * heads,
+        + [jax.ShapeDtypeStruct((tok + heads, DH), BF16)] * heads,
         compiler_params=pltpu.CompilerParams(vmem_limit_bytes=24 << 20),
         cost_estimate=pl.CostEstimate(
             flops=2 * tok * width, transcendentals=0, bytes_accessed=6 * tok * width
@@ -179,17 +183,20 @@
 
 
 def logits_kernel(heads, me_ref, pooled_ref, *refs):
-    pieces, out_ref = refs[:heads], refs[heads]
+    pieces, keys, out_ref = refs[:heads], refs[heads:-1], refs[-1]
+    row = lax.broadcasted_iota(jnp.int32, (heads, DH), 0)
     q = pooled_ref[...].astype(F32)
     lane = lax.broadcasted_iota(jnp.int32, (heads, heads), 1)
     logits = jnp.zeros((heads, heads), F32)
     for d in range(heads):
-        one = jnp.sum(q * pieces[d][...].astype(F32), axis=1, keepdims=True)
+        rebuilt = keys[d][...].astype(F32)
+        pooled_keys = jnp.where(row == me_ref[0], rebuilt, pieces[d][...].astype(F32))
+        one = jnp.sum(q * pooled_keys, axis=1, keepdims=True)
         logits = jnp.where(lane == (me_ref[0] ^ d), one / math.sqrt(DH), logits)
     out_ref[...] = logits
 
 
-def logits_of(me, pooled_q, pieces):
+def logits_of(me, pooled_q, pieces, packed):
     heads = len(pieces)
     rows = pl.BlockSpec((heads, DH), lambda i, m: (BS // heads, 0))
     return pl.pallas_call(
@@ -197,16 +204,20 @@
         grid_spec=pltpu.PrefetchScalarGridSpec(
             num_scalar_prefetch=1,
             grid=(1,),
-            in_specs=[pl.BlockSpec((heads, DH), lambda i, m: (0, 0))] + [rows] * heads,
+            in_specs=[pl.BlockSpec((heads, DH), lambda i, m: (0, 0))]
+            + [rows] * heads
+            + [pl.BlockSpec((heads, DH), lambda i, m: (0, 0))] * heads,
             out_specs=pl.BlockSpec((heads, heads), lambda i, m: (0, 0)),
         ),
         out_shape=jax.ShapeDtypeStruct((heads, heads), F32),
-    )(me, pooled_q, *pieces)
+    )(me, pooled_q, *pieces, *packed)
 
 
 def attend_kernel(me_ref, q_ref, tile_ref, k_ref, v_ref, *refs):
-    packed, (out_ref, far_ref, sem) = refs[:-3], refs[-3:]
-    source = me_ref[0] ^ jnp.max(tile_ref[...].astype(F32)).astype(jnp.int32)
+    packed, (out_ref, pooled_ref, far_ref, sem) = refs[:-4], refs[-4:]
+    row = lax.broadcasted_iota(jnp.int32, tile_ref.shape, 0)
+    chosen = jnp.where(row == me_ref[0], tile_ref[...].astype(F32), -1.0)
+    source = me_ref[0] ^ jnp.max(chosen).astype(jnp.int32)
     copies = [pltpu.make_async_copy(one, far_ref, sem) for one in packed]
     for n, copy in enumerate(copies):
         pl.when(source == n)(copy.start)
@@ -219,6 +230,9 @@
         total = jnp.sum(w.astype(F32), axis=1, keepdims=True)
         return top, total, jnp.dot(w, values, preferred_element_type=F32)
 
+    ones = jnp.ones((TILE, BS), BF16)
+    sums = jnp.dot(ones, k_ref[...], preferred_element_type=F32)
+    pooled_ref[...] = (sums / math.sqrt(BS)).astype(BF16)
     own_max, own_total, own_sum = part(k_ref[...], v_ref[...])
     copies[0].wait()
     far_max, far_total, far_sum = part(far_ref[pl.ds(0, BS), :], far_ref[pl.ds(BS, BS), :])
@@ -245,10 +259,13 @@
                 rows(1),
             ]
             + [pl.BlockSpec(memory_space=pl.ANY)] * len(packed),
-            out_specs=rows(0),
+            out_specs=[rows(0), pl.BlockSpec((TILE, DH), lambda i, m: (0, 0))],
             scratch_shapes=[pltpu.VMEM((2 * BS, DH), BF16), pltpu.SemaphoreType.DMA],
         ),
-        out_shape=jax.ShapeDtypeStruct((BS, DH), BF16),
+        out_shape=[
+            jax.ShapeDtypeStruct((BS, DH), BF16),
+            jax.ShapeDtypeStruct((TILE, DH), BF16),
+        ],
         compiler_params=pltpu.CompilerParams(vmem_limit_bytes=16 << 20),
         cost_estimate=pl.CostEstimate(
             flops=8 * BS * BS * DH, transcendentals=2 * BS * BS, bytes_accessed=12 * BS * DH
@@ -319,14 +336,13 @@
     exchange(pieces, 1, far[::-1], 3, far_done)
     packed = packed[:1] + [got[0, d] for d in range(1, members)]
     queries = pieces[:1] + [got[1, d] for d in range(1, members)]
-    sort_logits = logits_of(here, pooled_q, queries)
-
-    outputs = [None] * members
+    outputs, rebuilt = [None] * members, [None] * members
     for d in [0] + far[::-1] + near:
-        outputs[d] = attend(here, d, queries[d], packed)
+        outputs[d], rebuilt[d] = attend(here, d, queries[d], packed)
         if d:
             outputs[d] = send(outputs[d], d)
     attended = join_heads(here, outputs)
+    sort_logits = logits_of(here, pooled_q, queries, rebuilt)
     return attended, sort_logits.reshape(heads, 1, members)
 
 

time: 99.7 us -> 99.8 us (level)
    unnamed x28 -> x44, local copies, waits for them, and re-layouts: 1.85 us -> 2.47 us
where the time goes in v9:
time: 99.8 us; the launch traced here: 99.5 us
  starting transfers between devices  41 us (41%)
  Pallas kernels  33.6 us (34%)
  waiting for transfers between devices  21.4 us (21%)
  local copies, waits for them, and re-layouts  2.54 us (3%)
  between operations  1.01 us (1%)
    ppermute x21, starting transfers between devices, send(): return lax.ppermute(x, 'context', [(i, i ^ d) for i in range(members)])  41 us
    ppermute x21, waiting for transfers between devices, send(): return lax.ppermute(x, 'context', [(i, i ^ d) for i in range(members)])  21.4 us
    pallas_call x8, Pallas kernels, attend(): pl.pallas_call(attend_kernel, grid_spec=pltpu.PrefetchScalarGridSpec(num_...  16.6 us
    pallas_call x8, Pallas kernels, pack_head(): pl.pallas_call(pack_kernel, grid_spec=pltpu.PrefetchScalarGridSpec(num_sc...  13.7 us
    unnamed x44, local copies, waits for them, and re-layouts  2.47 us
  transfers between devices with their start and end apart: 21, of which 4 were waited for; matrix products, arithmetic and copies ran while one was open for 0% of the time, Pallas kernels for 31%

profile of v9, /device:TPU:0, one launch (start us, length us, event | category | flops | bytes accessed | tf_op | source)
XLA Modules:
  0.0 99.5 jit_solution(13456781093180521983)
XLA Ops:
  2.3 4.0 %collective-permute-start = (bf16[1024,128]{1,0:T(8,128)(2,1)}, bf16[1024,128]{1,0:T(8,128)(2,1)S(1)}, u32[]{:S(2)}, u32[]{:S(2)}) collective-permute-start(bf16[1024,128]{1,0:T(8,128)(2,1)} %shard_map.59), channel_id=1, source_target_pairs={{0,8},{2,10},{4,12},{6,14},{8,0},{10,2},{12,4},{14,6},{1,9},{3,11}... | collective-permute-start | bytes 786440 | tf_op jit(solution)/shard_map/ppermute | solution.py:317
  9.6 1.7 %shard_map.65 = bf16[1024,128]{1,0:T(8,128)(2,1)} custom-call(s32[1]{0:T(128)} %bitcast.me_ref, bf16[512,1024]{1,0:T(8,128)(2,1)} %k_ref.17, bf16[512,1024]{1,0:T(8,128)(2,1)} %v_ref.15), custom_call_target="tpu_custom_call" | custom-call | bytes 524288 | tf_op jit(solution)/shard_map/pallas_call | solution.py:127
  13.0 1.9 %collective-permute-start.2 = (bf16[1024,128]{1,0:T(8,128)(2,1)}, bf16[1024,128]{1,0:T(8,128)(2,1)S(1)}, u32[]{:S(2)}, u32[]{:S(2)}) collective-permute-start(bf16[1024,128]{1,0:T(8,128)(2,1)} %shard_map.63), channel_id=1, source_target_pairs={{0,4},{2,6},{4,0},{6,2},{8,12},{10,14},{12,8},{14,10},{1,5},{3,7},... | collective-permute-start | bytes 786440 | tf_op jit(solution)/shard_map/ppermute | solution.py:317
  16.5 2.5 %collective-permute-start.5 = (bf16[1024,128]{1,0:T(8,128)(2,1)}, bf16[1024,128]{1,0:T(8,128)(2,1)S(1)}, u32[]{:S(2)}, u32[]{:S(2)}) collective-permute-start(bf16[1024,128]{1,0:T(8,128)(2,1)} %shard_map.66), channel_id=1, source_target_pairs={{0,12},{2,14},{4,8},{6,10},{8,4},{10,6},{12,0},{14,2},{1,13},{3,15... | collective-permute-start | bytes 786440 | tf_op jit(solution)/shard_map/ppermute | solution.py:317
  19.0 1.7 %shard_map.67 = bf16[1024,128]{1,0:T(8,128)(2,1)} custom-call(s32[1]{0:T(128)} %bitcast.me_ref, bf16[512,1024]{1,0:T(8,128)(2,1)} %k_ref.17, bf16[512,1024]{1,0:T(8,128)(2,1)} %v_ref.15), custom_call_target="tpu_custom_call" | custom-call | bytes 524288 | tf_op jit(solution)/shard_map/pallas_call | solution.py:127
  20.7 1.7 %shard_map.64 = bf16[1024,128]{1,0:T(8,128)(2,1)} custom-call(s32[1]{0:T(128)} %bitcast.me_ref, bf16[512,1024]{1,0:T(8,128)(2,1)} %k_ref.17, bf16[512,1024]{1,0:T(8,128)(2,1)} %v_ref.15), custom_call_target="tpu_custom_call" | custom-call | bytes 524288 | tf_op jit(solution)/shard_map/pallas_call | solution.py:127
  22.4 2.7 %collective-permute-done.refs_4_.k_ref.v_ref = bf16[1024,128]{1,0:T(8,128)(2,1)S(1)} collective-permute-done((bf16[1024,128]{1,0:T(8,128)(2,1)}, bf16[1024,128]{1,0:T(8,128)(2,1)S(1)}, u32[]{:S(2)}, u32[]{:S(2)}) %collective-permute-start) | collective-permute-done | bytes 262176 | tf_op jit(solution)/shard_map/ppermute | solution.py:317
  25.1 4.6 %collective-permute-start.6 = (bf16[1024,128]{1,0:T(8,128)(2,1)S(1)}, bf16[1024,128]{1,0:T(8,128)(2,1)S(1)}, u32[]{:S(2)}, u32[]{:S(2)}) collective-permute-start(bf16[1024,128]{1,0:T(8,128)(2,1)S(1)} %copy-done.20), channel_id=1, source_target_pairs={{0,14},{2,12},{4,10},{6,8},{8,6},{10,4},{12,2},{14,0},{1,15},{3,13... | collective-permute-start | bytes 786440 | tf_op jit(solution)/shard_map/ppermute | solution.py:317
  29.8 1.8 %shard_map.60.k_ref.v_ref.refs_0_ = bf16[1024,128]{1,0:T(8,128)(2,1)} custom-call(s32[1]{0:T(128)} %bitcast.me_ref, bf16[512,1024]{1,0:T(8,128)(2,1)} %k_ref.17, bf16[512,1024]{1,0:T(8,128)(2,1)} %v_ref.15), custom_call_target="tpu_custom_call" | custom-call | bytes 524288 | tf_op jit(solution)/shard_map/pallas_call | solution.py:127
  34.1 9.1 %collective-permute-done.4.refs_5_.k_ref.v_ref = bf16[1024,128]{1,0:T(8,128)(2,1)S(1)} collective-permute-done((bf16[1024,128]{1,0:T(8,128)(2,1)}, bf16[1024,128]{1,0:T(8,128)(2,1)S(1)}, u32[]{:S(2)}, u32[]{:S(2)}) %collective-permute-start.4) | collective-permute-done | bytes 262176 | tf_op jit(solution)/shard_map/ppermute | solution.py:317
  43.1 3.0 %collective-permute-start.9 = (bf16[520,128]{1,0:T(8,128)(2,1)S(1)}, bf16[520,128]{1,0:T(8,128)(2,1)S(1)}, u32[]{:S(2)}, u32[]{:S(2)}) collective-permute-start(bf16[520,128]{1,0:T(8,128)(2,1)S(1)} %get-tuple-element.46), channel_id=1, source_target_pairs={{0,4},{2,6},{4,0},{6,2},{8,12},{10,14},{12,8},{14,10},{1,5},{3,7},... | collective-permute-start | bytes 399368 | tf_op jit(solution)/shard_map/ppermute | solution.py:317
  46.1 7.0 %collective-permute-start.15 = (bf16[520,128]{1,0:T(8,128)(2,1)S(1)}, bf16[520,128]{1,0:T(8,128)(2,1)S(1)}, u32[]{:S(2)}, u32[]{:S(2)}) collective-permute-start(bf16[520,128]{1,0:T(8,128)(2,1)S(1)} %get-tuple-element.55), channel_id=1, source_target_pairs={{0,10},{2,8},{4,14},{6,12},{8,2},{10,0},{12,6},{14,4},{1,11},{3,9}... | collective-permute-start | bytes 399368 | tf_op jit(solution)/shard_map/ppermute | solution.py:317
  53.1 8.5 %collective-permute-done.13.q_ref.tile_ref.refs_4_ = bf16[520,128]{1,0:T(8,128)(2,1)S(1)} collective-permute-done((bf16[520,128]{1,0:T(8,128)(2,1)S(1)}, bf16[520,128]{1,0:T(8,128)(2,1)S(1)}, u32[]{:S(2)}, u32[]{:S(2)}) %collective-permute-start.13) | collective-permute-done | bytes 133152 | tf_op jit(solution)/shard_map/ppermute | solution.py:317
  61.6 3.7 %collective-permute-start.19 = (bf16[520,128]{1,0:T(8,128)(2,1)S(1)}, bf16[520,128]{1,0:T(8,128)(2,1)S(1)}, u32[]{:S(2)}, u32[]{:S(2)}) collective-permute-start(bf16[520,128]{1,0:T(8,128)(2,1)S(1)} %get-tuple-element.61), channel_id=1, source_target_pairs={{0,14},{2,12},{4,10},{6,8},{8,6},{10,4},{12,2},{14,0},{1,15},{3,13... | collective-permute-start | bytes 399368 | tf_op jit(solution)/shard_map/ppermute | solution.py:317
  67.0 1.9 %shard_map.73 = (bf16[512,128]{1,0:T(8,128)(2,1)S(1)}, bf16[8,128]{1,0:T(8,128)(2,1)S(1)}) custom-call(s32[1]{0:T(128)} %bitcast.me_ref, bf16[520,128]{1,0:T(8,128)(2,1)S(1)} %collective-permute-done.15.q_ref.tile_ref.refs_5_, bf16[520,128]{1,0:T(8,128)(2,1)S(1)} %collective-permute-done.15.q_ref.tile_ref.refs_5_, ...), custom_call_target="tpu_custom_call" | custom-call | flops 268435456 | bytes 786432 | tf_op jit(solution)/shard_map/pallas_call | solution.py:250
  68.9 3.4 %collective-permute-start.16 = (bf16[512,128]{1,0:T(8,128)(2,1)S(1)}, bf16[512,128]{1,0:T(8,128)(2,1)S(1)}, u32[]{:S(2)}, u32[]{:S(2)}) collective-permute-start(bf16[512,128]{1,0:T(8,128)(2,1)S(1)} %get-tuple-element.56), channel_id=1, source_target_pairs={{0,10},{2,8},{4,14},{6,12},{8,2},{10,0},{12,6},{14,4},{1,11},{3,9}... | collective-permute-start | bytes 393224 | tf_op jit(solution)/shard_map/ppermute | solution.py:317
  72.3 1.9 %shard_map.72 = (bf16[512,128]{1,0:T(8,128)(2,1)S(1)}, bf16[8,128]{1,0:T(8,128)(2,1)S(1)}) custom-call(s32[1]{0:T(128)} %bitcast.me_ref, bf16[520,128]{1,0:T(8,128)(2,1)S(1)} %collective-permute-done.13.q_ref.tile_ref.refs_4_, bf16[520,128]{1,0:T(8,128)(2,1)S(1)} %collective-permute-done.13.q_ref.tile_ref.refs_4_, ...), custom_call_target="tpu_custom_call" | custom-call | flops 268435456 | bytes 786432 | tf_op jit(solution)/shard_map/pallas_call | solution.py:250
  75.2 1.9 %shard_map.70 = (bf16[512,128]{1,0:T(8,128)(2,1)S(1)}, bf16[8,128]{1,0:T(8,128)(2,1)S(1)}) custom-call(s32[1]{0:T(128)} %bitcast.me_ref, bf16[520,128]{1,0:T(8,128)(2,1)S(1)} %collective-permute-done.9.q_ref.tile_ref.refs_2_, bf16[520,128]{1,0:T(8,128)(2,1)S(1)} %collective-permute-done.9.q_ref.tile_ref.refs_2_, ...), custom_call_target="tpu_custom_call" | custom-call | flops 268435456 | bytes 786432 | tf_op jit(solution)/shard_map/pallas_call | solution.py:250
  77.1 1.9 %shard_map.75 = (bf16[512,128]{1,0:T(8,128)(2,1)S(1)}, bf16[8,128]{1,0:T(8,128)(2,1)S(1)}) custom-call(s32[1]{0:T(128)} %bitcast.me_ref, bf16[520,128]{1,0:T(8,128)(2,1)S(1)} %collective-permute-done.19.q_ref.tile_ref.refs_7_, bf16[520,128]{1,0:T(8,128)(2,1)S(1)} %collective-permute-done.19.q_ref.tile_ref.refs_7_, ...), custom_call_target="tpu_custom_call" | custom-call | flops 268435456 | bytes 786432 | tf_op jit(solution)/shard_map/pallas_call | solution.py:250
  79.8 1.9 %shard_map.71 = (bf16[512,128]{1,0:T(8,128)(2,1)S(1)}, bf16[8,128]{1,0:T(8,128)(2,1)S(1)}) custom-call(s32[1]{0:T(128)} %bitcast.me_ref, bf16[520,128]{1,0:T(8,128)(2,1)S(1)} %collective-permute-done.11.q_ref.tile_ref.refs_3_, bf16[520,128]{1,0:T(8,128)(2,1)S(1)} %collective-permute-done.11.q_ref.tile_ref.refs_3_, ...), custom_call_target="tpu_custom_call" | custom-call | flops 268435456 | bytes 786432 | tf_op jit(solution)/shard_map/pallas_call | solution.py:250
  81.7 3.8 %collective-permute-start.20 = (bf16[512,128]{1,0:T(8,128)(2,1)S(1)}, bf16[512,128]{1,0:T(8,128)(2,1)S(1)}, u32[]{:S(2)}, u32[]{:S(2)}) collective-permute-start(bf16[512,128]{1,0:T(8,128)(2,1)S(1)} %get-tuple-element.62), channel_id=1, source_target_pairs={{0,14},{2,12},{4,10},{6,8},{8,6},{10,4},{12,2},{14,0},{1,15},{3,13... | collective-permute-start | bytes 393224 | tf_op jit(solution)/shard_map/ppermute | solution.py:317
  85.5 2.5 %shard_map.74 = (bf16[512,128]{1,0:T(8,128)(2,1)}, bf16[8,128]{1,0:T(8,128)(2,1)S(1)}) custom-call(s32[1]{0:T(128)} %bitcast.me_ref, bf16[520,128]{1,0:T(8,128)(2,1)S(1)} %collective-permute-done.17.q_ref.tile_ref.refs_6_, bf16[520,128]{1,0:T(8,128)(2,1)S(1)} %collective-permute-done.17.q_ref.tile_ref.refs_6_, ...), custom_call_target="tpu_custom_call" | custom-call | flops 268435456 | bytes 786432 | tf_op jit(solution)/shard_map/pallas_call | solution.py:250
  88.3 2.7 %shard_map.69 = (bf16[512,128]{1,0:T(8,128)(2,1)}, bf16[8,128]{1,0:T(8,128)(2,1)S(1)}) custom-call(s32[1]{0:T(128)} %bitcast.me_ref, bf16[520,128]{1,0:T(8,128)(2,1)S(1)} %collective-permute-done.7.q_ref.tile_ref.refs_1_, bf16[520,128]{1,0:T(8,128)(2,1)S(1)} %collective-permute-done.7.q_ref.tile_ref.refs_1_, ...), custom_call_target="tpu_custom_call" | custom-call | flops 268435456 | bytes 786432 | tf_op jit(solution)/shard_map/pallas_call | solution.py:250
  93.1 1.9 %shard_map.68 = (bf16[512,128]{1,0:T(8,128)(2,1)S(1)}, bf16[8,128]{1,0:T(8,128)(2,1)S(1)}) custom-call(s32[1]{0:T(128)} %bitcast.me_ref, bf16[520,128]{1,0:T(8,128)(2,1)S(1)} %get-tuple-element.38.q_ref.tile_ref.refs_0_, bf16[520,128]{1,0:T(8,128)(2,1)S(1)} %get-tuple-element.38.q_ref.tile_ref.refs_0_, bf16[1024,128]{1,0:T(8,128)(2,1)S(1)} %copy-done.1, ...), custom_call_target="tpu_custom_call" | custom-call | flops 268435456 | bytes 786432 | tf_op jit(solution)/shard_map/pallas_call | solution.py:250
  (83 shorter events, 20.8 us)
Async XLA Ops:
  2.3 22.8 %collective-permute-start = (bf16[1024,128]{1,0:T(8,128)(2,1)}, bf16[1024,128]{1,0:T(8,128)(2,1)S(1)}, u32[]{:S(2)}, u32[]{:S(2)}) collective-permute-start(bf16[1024,128]{1,0:T(8,128)(2,1)} %shard_map.59), channel_id=1, source_target_pairs={{0,8},{2,10},{4,12},{6,14},{8,0},{10,2},{12,4},{14,6},{1,9},{3,11}... | collective-permute-start | bytes 786440 | tf_op jit(solution)/shard_map/ppermute | solution.py:317
  8.1 21.7 %collective-permute-start.1 = (bf16[1024,128]{1,0:T(8,128)(2,1)}, bf16[1024,128]{1,0:T(8,128)(2,1)S(1)}, u32[]{:S(2)}, u32[]{:S(2)}) collective-permute-start(bf16[1024,128]{1,0:T(8,128)(2,1)} %shard_map.62), channel_id=1, source_target_pairs={{0,2},{2,0},{4,6},{6,4},{8,10},{10,8},{12,14},{14,12},{1,3},{3,1},... | collective-permute-start | bytes 786440 | tf_op jit(solution)/shard_map/ppermute | solution.py:317
  11.3 31.9 %collective-permute-start.4 = (bf16[1024,128]{1,0:T(8,128)(2,1)}, bf16[1024,128]{1,0:T(8,128)(2,1)S(1)}, u32[]{:S(2)}, u32[]{:S(2)}) collective-permute-start(bf16[1024,128]{1,0:T(8,128)(2,1)} %shard_map.65), channel_id=1, source_target_pairs={{0,10},{2,8},{4,14},{6,12},{8,2},{10,0},{12,6},{14,4},{1,11},{3,9}... | collective-permute-start | bytes 786440 | tf_op jit(solution)/shard_map/ppermute | solution.py:317
  13.0 30.2 %collective-permute-start.2 = (bf16[1024,128]{1,0:T(8,128)(2,1)}, bf16[1024,128]{1,0:T(8,128)(2,1)S(1)}, u32[]{:S(2)}, u32[]{:S(2)}) collective-permute-start(bf16[1024,128]{1,0:T(8,128)(2,1)} %shard_map.63), channel_id=1, source_target_pairs={{0,4},{2,6},{4,0},{6,2},{8,12},{10,14},{12,8},{14,10},{1,5},{3,7},... | collective-permute-start | bytes 786440 | tf_op jit(solution)/shard_map/ppermute | solution.py:317
  16.5 29.6 %collective-permute-start.5 = (bf16[1024,128]{1,0:T(8,128)(2,1)}, bf16[1024,128]{1,0:T(8,128)(2,1)S(1)}, u32[]{:S(2)}, u32[]{:S(2)}) collective-permute-start(bf16[1024,128]{1,0:T(8,128)(2,1)} %shard_map.66), channel_id=1, source_target_pairs={{0,12},{2,14},{4,8},{6,10},{8,4},{10,6},{12,0},{14,2},{1,13},{3,15... | collective-permute-start | bytes 786440 | tf_op jit(solution)/shard_map/ppermute | solution.py:317
  25.1 40.3 %collective-permute-start.6 = (bf16[1024,128]{1,0:T(8,128)(2,1)S(1)}, bf16[1024,128]{1,0:T(8,128)(2,1)S(1)}, u32[]{:S(2)}, u32[]{:S(2)}) collective-permute-start(bf16[1024,128]{1,0:T(8,128)(2,1)S(1)} %copy-done.20), channel_id=1, source_target_pairs={{0,14},{2,12},{4,10},{6,8},{8,6},{10,4},{12,2},{14,0},{1,15},{3,13... | collective-permute-start | bytes 786440 | tf_op jit(solution)/shard_map/ppermute | solution.py:317
  29.8 37.1 %collective-permute-start.3 = (bf16[1024,128]{1,0:T(8,128)(2,1)}, bf16[1024,128]{1,0:T(8,128)(2,1)S(1)}, u32[]{:S(2)}, u32[]{:S(2)}) collective-permute-start(bf16[1024,128]{1,0:T(8,128)(2,1)} %shard_map.64), channel_id=1, source_target_pairs={{0,6},{2,4},{4,2},{6,0},{8,14},{10,12},{12,10},{14,8},{1,7},{3,5},... | collective-permute-start | bytes 786440 | tf_op jit(solution)/shard_map/ppermute | solution.py:317
  32.9 34.1 %copy-start.1 = (bf16[1024,128]{1,0:T(8,128)(2,1)S(1)}, bf16[1024,128]{1,0:T(8,128)(2,1)}, u32[]{:S(2)}) copy-start(bf16[1024,128]{1,0:T(8,128)(2,1)} %shard_map.60.k_ref.v_ref.refs_0_) | copy-start | bytes 786436
  34.1 59.0 %copy-start.2 = (bf16[520,128]{1,0:T(8,128)(2,1)}, bf16[520,128]{1,0:T(8,128)(2,1)S(1)}, u32[]{:S(2)}) copy-start(bf16[520,128]{1,0:T(8,128)(2,1)S(1)} %get-tuple-element.38.q_ref.tile_ref.refs_0_) | copy-start | bytes 399364
  43.1 18.5 %collective-permute-start.13 = (bf16[520,128]{1,0:T(8,128)(2,1)S(1)}, bf16[520,128]{1,0:T(8,128)(2,1)S(1)}, u32[]{:S(2)}, u32[]{:S(2)}) collective-permute-start(bf16[520,128]{1,0:T(8,128)(2,1)S(1)} %get-tuple-element.52), channel_id=1, source_target_pairs={{0,8},{2,10},{4,12},{6,14},{8,0},{10,2},{12,4},{14,6},{1,9},{3,11}... | collective-permute-start | bytes 399368 | tf_op jit(solution)/shard_map/ppermute | solution.py:317
  43.1 22.2 %collective-permute-start.9 = (bf16[520,128]{1,0:T(8,128)(2,1)S(1)}, bf16[520,128]{1,0:T(8,128)(2,1)S(1)}, u32[]{:S(2)}, u32[]{:S(2)}) collective-permute-start(bf16[520,128]{1,0:T(8,128)(2,1)S(1)} %get-tuple-element.46), channel_id=1, source_target_pairs={{0,4},{2,6},{4,0},{6,2},{8,12},{10,14},{12,8},{14,10},{1,5},{3,7},... | collective-permute-start | bytes 399368 | tf_op jit(solution)/shard_map/ppermute | solution.py:317
  46.1 20.9 %collective-permute-start.15 = (bf16[520,128]{1,0:T(8,128)(2,1)S(1)}, bf16[520,128]{1,0:T(8,128)(2,1)S(1)}, u32[]{:S(2)}, u32[]{:S(2)}) collective-permute-start(bf16[520,128]{1,0:T(8,128)(2,1)S(1)} %get-tuple-element.55), channel_id=1, source_target_pairs={{0,10},{2,8},{4,14},{6,12},{8,2},{10,0},{12,6},{14,4},{1,11},{3,9}... | collective-permute-start | bytes 399368 | tf_op jit(solution)/shard_map/ppermute | solution.py:317
  61.6 10.7 %copy-start.3 = (bf16[520,128]{1,0:T(8,128)(2,1)}, bf16[520,128]{1,0:T(8,128)(2,1)S(1)}, u32[]{:S(2)}) copy-start(bf16[520,128]{1,0:T(8,128)(2,1)S(1)} %collective-permute-done.13.q_ref.tile_ref.refs_4_) | copy-start | bytes 399364
  61.6 12.6 %collective-permute-start.19 = (bf16[520,128]{1,0:T(8,128)(2,1)S(1)}, bf16[520,128]{1,0:T(8,128)(2,1)S(1)}, u32[]{:S(2)}, u32[]{:S(2)}) collective-permute-start(bf16[520,128]{1,0:T(8,128)(2,1)S(1)} %get-tuple-element.61), channel_id=1, source_target_pairs={{0,14},{2,12},{4,10},{6,8},{8,6},{10,4},{12,2},{14,0},{1,15},{3,13... | collective-permute-start | bytes 399368 | tf_op jit(solution)/shard_map/ppermute | solution.py:317
  65.4 13.7 %collective-permute-start.11 = (bf16[520,128]{1,0:T(8,128)(2,1)S(1)}, bf16[520,128]{1,0:T(8,128)(2,1)S(1)}, u32[]{:S(2)}, u32[]{:S(2)}) collective-permute-start(bf16[520,128]{1,0:T(8,128)(2,1)S(1)} %get-tuple-element.49), channel_id=1, source_target_pairs={{0,6},{2,4},{4,2},{6,0},{8,14},{10,12},{12,10},{14,8},{1,7},{3,5},... | collective-permute-start | bytes 399368 | tf_op jit(solution)/shard_map/ppermute | solution.py:317
  65.4 16.3 %collective-permute-start.17 = (bf16[520,128]{1,0:T(8,128)(2,1)S(1)}, bf16[520,128]{1,0:T(8,128)(2,1)S(1)}, u32[]{:S(2)}, u32[]{:S(2)}) collective-permute-start(bf16[520,128]{1,0:T(8,128)(2,1)S(1)} %get-tuple-element.58), channel_id=1, source_target_pairs={{0,12},{2,14},{4,8},{6,10},{8,4},{10,6},{12,0},{14,2},{1,13},{3,15... | collective-permute-start | bytes 399368 | tf_op jit(solution)/shard_map/ppermute | solution.py:317
  66.8 21.3 %collective-permute-start.7 = (bf16[520,128]{1,0:T(8,128)(2,1)S(1)}, bf16[520,128]{1,0:T(8,128)(2,1)S(1)}, u32[]{:S(2)}, u32[]{:S(2)}) collective-permute-start(bf16[520,128]{1,0:T(8,128)(2,1)S(1)} %get-tuple-element.43), channel_id=1, source_target_pairs={{0,2},{2,0},{4,6},{6,4},{8,10},{10,8},{12,14},{14,12},{1,3},{3,1},... | collective-permute-start | bytes 399368 | tf_op jit(solution)/shard_map/ppermute | solution.py:317
  68.9 22.1 %collective-permute-start.16 = (bf16[512,128]{1,0:T(8,128)(2,1)S(1)}, bf16[512,128]{1,0:T(8,128)(2,1)S(1)}, u32[]{:S(2)}, u32[]{:S(2)}) collective-permute-start(bf16[512,128]{1,0:T(8,128)(2,1)S(1)} %get-tuple-element.56), channel_id=1, source_target_pairs={{0,10},{2,8},{4,14},{6,12},{8,2},{10,0},{12,6},{14,4},{1,11},{3,9}... | collective-permute-start | bytes 393224 | tf_op jit(solution)/shard_map/ppermute | solution.py:317
  74.2 18.3 %collective-permute-start.14 = (bf16[512,128]{1,0:T(8,128)(2,1)S(1)}, bf16[512,128]{1,0:T(8,128)(2,1)S(1)}, u32[]{:S(2)}, u32[]{:S(2)}) collective-permute-start(bf16[512,128]{1,0:T(8,128)(2,1)S(1)} %get-tuple-element.53), channel_id=1, source_target_pairs={{0,8},{2,10},{4,12},{6,14},{8,0},{10,2},{12,4},{14,6},{1,9},{3,11}... | collective-permute-start | bytes 393224 | tf_op jit(solution)/shard_map/ppermute | solution.py:317
  79.1 18.0 %collective-permute-start.10 = (bf16[512,128]{1,0:T(8,128)(2,1)S(1)}, bf16[512,128]{1,0:T(8,128)(2,1)S(1)}, u32[]{:S(2)}, u32[]{:S(2)}) collective-permute-start(bf16[512,128]{1,0:T(8,128)(2,1)S(1)} %get-tuple-element.47), channel_id=1, source_target_pairs={{0,4},{2,6},{4,0},{6,2},{8,12},{10,14},{12,8},{14,10},{1,5},{3,7},... | collective-permute-start | bytes 393224 | tf_op jit(solution)/shard_map/ppermute | solution.py:317
  81.7 15.3 %collective-permute-start.20 = (bf16[512,128]{1,0:T(8,128)(2,1)S(1)}, bf16[512,128]{1,0:T(8,128)(2,1)S(1)}, u32[]{:S(2)}, u32[]{:S(2)}) collective-permute-start(bf16[512,128]{1,0:T(8,128)(2,1)S(1)} %get-tuple-element.62), channel_id=1, source_target_pairs={{0,14},{2,12},{4,10},{6,8},{8,6},{10,4},{12,2},{14,0},{1,15},{3,13... | collective-permute-start | bytes 393224 | tf_op jit(solution)/shard_map/ppermute | solution.py:317
  88.1 8.9 %collective-permute-start.12 = (bf16[512,128]{1,0:T(8,128)(2,1)S(1)}, bf16[512,128]{1,0:T(8,128)(2,1)S(1)}, u32[]{:S(2)}, u32[]{:S(2)}) collective-permute-start(bf16[512,128]{1,0:T(8,128)(2,1)S(1)} %get-tuple-element.50), channel_id=1, source_target_pairs={{0,6},{2,4},{4,2},{6,0},{8,14},{10,12},{12,10},{14,8},{1,7},{3,5},... | collective-permute-start | bytes 393224 | tf_op jit(solution)/shard_map/ppermute | solution.py:317
  91.1 7.2 %collective-permute-start.18 = (bf16[512,128]{1,0:T(8,128)(2,1)}, bf16[512,128]{1,0:T(8,128)(2,1)S(1)}, u32[]{:S(2)}, u32[]{:S(2)}) collective-permute-start(bf16[512,128]{1,0:T(8,128)(2,1)} %get-tuple-element.59), channel_id=1, source_target_pairs={{0,12},{2,14},{4,8},{6,10},{8,4},{10,6},{12,0},{14,2},{1,13},{3,15... | collective-permute-start | bytes 393224 | tf_op jit(solution)/shard_map/ppermute | solution.py:317
  92.5 5.7 %collective-permute-start.8 = (bf16[512,128]{1,0:T(8,128)(2,1)}, bf16[512,128]{1,0:T(8,128)(2,1)S(1)}, u32[]{:S(2)}, u32[]{:S(2)}) collective-permute-start(bf16[512,128]{1,0:T(8,128)(2,1)} %get-tuple-element.44), channel_id=1, source_target_pairs={{0,2},{2,0},{4,6},{6,4},{8,10},{10,8},{12,14},{14,12},{1,3},{3,1},... | collective-permute-start | bytes 393224 | tf_op jit(solution)/shard_map/ppermute | solution.py:317
  (19 other events, 68.3 us)

commit v10 on v8

--- a/solution.py
+++ b/solution.py
@@ -300,6 +300,10 @@
         return lax.ppermute(x, "context", [(i, i ^ d) for i in range(members)])
 
     packed = [pack_head(here, d, key_rows, value_rows) for d in range(members)]
+    column = (me ^ (members // 2)) * DH
+    packed[members // 2] = jnp.concatenate(
+        [lax.dynamic_slice_in_dim(x, column, DH, axis=1) for x in (key_rows, value_rows)]
+    )
     got = {}
 
     def exchange(pieces, kind, ds, window, done):

time: 99.7 us -> 98.9 us (level)
  Pallas kernels: 33.4 us -> 31.6 us
  local copies, waits for them, and re-layouts: 1.92 us -> 2.92 us
    pallas_call x8 -> x7, Pallas kernels: 13.7 us -> 12 us  [pack_head(): pl.pallas_call(pack_kernel, grid_spec=pltpu.PrefetchScalarGridSpec(num_sc...]
where the time goes in v10:
time: 98.9 us; the launch traced here: 98.5 us
  starting transfers between devices  41.2 us (42%)
  Pallas kernels  31.6 us (32%)
  waiting for transfers between devices  21.8 us (22%)
  local copies, waits for them, and re-layouts  2.92 us (3%)
    ppermute x21, starting transfers between devices, send(): return lax.ppermute(x, 'context', [(i, i ^ d) for i in range(members)])  41.2 us
    ppermute x21, waiting for transfers between devices, send(): return lax.ppermute(x, 'context', [(i, i ^ d) for i in range(members)])  21.8 us
    pallas_call x8, Pallas kernels, attend(): pl.pallas_call(attend_kernel, grid_spec=pltpu.PrefetchScalarGridSpec(num_...  16.4 us
    pallas_call x7, Pallas kernels, pack_head(): pl.pallas_call(pack_kernel, grid_spec=pltpu.PrefetchScalarGridSpec(num_sc...  12 us
  transfers between devices with their start and end apart: 21, of which 4 were waited for; matrix products, arithmetic and copies ran while one was open for 0% of the time, Pallas kernels for 31%

profile of v10, /device:TPU:0, one launch (start us, length us, event | category | flops | bytes accessed | tf_op | source)
XLA Modules:
  0.0 98.5 jit_solution(9085367326528622202)
XLA Ops:
  1.7 4.1 %collective-permute-start = (bf16[1024,128]{1,0:T(8,128)(2,1)S(1)}, bf16[1024,128]{1,0:T(8,128)(2,1)S(1)}, u32[]{:S(2)}, u32[]{:S(2)}) collective-permute-start(bf16[1024,128]{1,0:T(8,128)(2,1)S(1)} %pad_maximum_fusion), channel_id=1, source_target_pairs={{0,8},{2,10},{4,12},{6,14},{8,0},{10,2},{12,4},{14,6},{1,9},{3,11}... | collective-permute-start | bytes 786440 | tf_op jit(solution)/shard_map/ppermute | solution.py:300
  12.3 1.9 %collective-permute-start.2 = (bf16[1024,128]{1,0:T(8,128)(2,1)}, bf16[1024,128]{1,0:T(8,128)(2,1)S(1)}, u32[]{:S(2)}, u32[]{:S(2)}) collective-permute-start(bf16[1024,128]{1,0:T(8,128)(2,1)} %shard_map.62), channel_id=1, source_target_pairs={{0,4},{2,6},{4,0},{6,2},{8,12},{10,14},{12,8},{14,10},{1,5},{3,7},... | collective-permute-start | bytes 786440 | tf_op jit(solution)/shard_map/ppermute | solution.py:300
  14.2 1.7 %shard_map.65 = bf16[1024,128]{1,0:T(8,128)(2,1)} custom-call(s32[1]{0:T(128)} %bitcast.me_ref, bf16[512,1024]{1,0:T(8,128)(2,1)} %k_ref.15, bf16[512,1024]{1,0:T(8,128)(2,1)} %v_ref.13), custom_call_target="tpu_custom_call" | custom-call | bytes 524288 | tf_op jit(solution)/shard_map/pallas_call | solution.py:127
  15.9 2.5 %collective-permute-start.5 = (bf16[1024,128]{1,0:T(8,128)(2,1)}, bf16[1024,128]{1,0:T(8,128)(2,1)S(1)}, u32[]{:S(2)}, u32[]{:S(2)}) collective-permute-start(bf16[1024,128]{1,0:T(8,128)(2,1)} %shard_map.65), channel_id=1, source_target_pairs={{0,12},{2,14},{4,8},{6,10},{8,4},{10,6},{12,0},{14,2},{1,13},{3,15... | collective-permute-start | bytes 786440 | tf_op jit(solution)/shard_map/ppermute | solution.py:300
  20.1 1.7 %shard_map.63 = bf16[1024,128]{1,0:T(8,128)(2,1)} custom-call(s32[1]{0:T(128)} %bitcast.me_ref, bf16[512,1024]{1,0:T(8,128)(2,1)} %k_ref.15, bf16[512,1024]{1,0:T(8,128)(2,1)} %v_ref.13), custom_call_target="tpu_custom_call" | custom-call | bytes 524288 | tf_op jit(solution)/shard_map/pallas_call | solution.py:127
  21.8 2.3 %collective-permute-done.refs_4_.k_ref.v_ref = bf16[1024,128]{1,0:T(8,128)(2,1)S(1)} collective-permute-done((bf16[1024,128]{1,0:T(8,128)(2,1)S(1)}, bf16[1024,128]{1,0:T(8,128)(2,1)S(1)}, u32[]{:S(2)}, u32[]{:S(2)}) %collective-permute-start) | collective-permute-done | bytes 262176 | tf_op jit(solution)/shard_map/ppermute | solution.py:300
  24.1 4.8 %collective-permute-start.6 = (bf16[1024,128]{1,0:T(8,128)(2,1)S(1)}, bf16[1024,128]{1,0:T(8,128)(2,1)S(1)}, u32[]{:S(2)}, u32[]{:S(2)}) collective-permute-start(bf16[1024,128]{1,0:T(8,128)(2,1)S(1)} %copy-done.12), channel_id=1, source_target_pairs={{0,14},{2,12},{4,10},{6,8},{8,6},{10,4},{12,2},{14,0},{1,15},{3,13... | collective-permute-start | bytes 786440 | tf_op jit(solution)/shard_map/ppermute | solution.py:300
  28.9 1.8 %shard_map.59.k_ref.v_ref.refs_0_ = bf16[1024,128]{1,0:T(8,128)(2,1)} custom-call(s32[1]{0:T(128)} %bitcast.me_ref, bf16[512,1024]{1,0:T(8,128)(2,1)} %k_ref.15, bf16[512,1024]{1,0:T(8,128)(2,1)} %v_ref.13), custom_call_target="tpu_custom_call" | custom-call | bytes 524288 | tf_op jit(solution)/shard_map/pallas_call | solution.py:127
  33.2 9.1 %collective-permute-done.4.refs_5_.k_ref.v_ref = bf16[1024,128]{1,0:T(8,128)(2,1)S(1)} collective-permute-done((bf16[1024,128]{1,0:T(8,128)(2,1)}, bf16[1024,128]{1,0:T(8,128)(2,1)S(1)}, u32[]{:S(2)}, u32[]{:S(2)}) %collective-permute-start.4) | collective-permute-done | bytes 262176 | tf_op jit(solution)/shard_map/ppermute | solution.py:300
  42.3 3.0 %collective-permute-start.9 = (bf16[528,128]{1,0:T(8,128)(2,1)S(1)}, bf16[528,128]{1,0:T(8,128)(2,1)S(1)}, u32[]{:S(2)}, u32[]{:S(2)}) collective-permute-start(bf16[528,128]{1,0:T(8,128)(2,1)S(1)} %get-tuple-element.28), channel_id=1, source_target_pairs={{0,4},{2,6},{4,0},{6,2},{8,12},{10,14},{12,8},{14,10},{1,5},{3,7},... | collective-permute-start | bytes 405512 | tf_op jit(solution)/shard_map/ppermute | solution.py:300
  45.3 7.0 %collective-permute-start.15 = (bf16[528,128]{1,0:T(8,128)(2,1)S(1)}, bf16[528,128]{1,0:T(8,128)(2,1)S(1)}, u32[]{:S(2)}, u32[]{:S(2)}) collective-permute-start(bf16[528,128]{1,0:T(8,128)(2,1)S(1)} %get-tuple-element.34), channel_id=1, source_target_pairs={{0,10},{2,8},{4,14},{6,12},{8,2},{10,0},{12,6},{14,4},{1,11},{3,9}... | collective-permute-start | bytes 405512 | tf_op jit(solution)/shard_map/ppermute | solution.py:300
  52.4 8.6 %collective-permute-done.13.q_ref.tile_ref.refs_4_ = bf16[528,128]{1,0:T(8,128)(2,1)S(1)} collective-permute-done((bf16[528,128]{1,0:T(8,128)(2,1)S(1)}, bf16[528,128]{1,0:T(8,128)(2,1)S(1)}, u32[]{:S(2)}, u32[]{:S(2)}) %collective-permute-start.13) | collective-permute-done | bytes 135200 | tf_op jit(solution)/shard_map/ppermute | solution.py:300
  61.0 3.7 %collective-permute-start.19 = (bf16[528,128]{1,0:T(8,128)(2,1)S(1)}, bf16[528,128]{1,0:T(8,128)(2,1)S(1)}, u32[]{:S(2)}, u32[]{:S(2)}) collective-permute-start(bf16[528,128]{1,0:T(8,128)(2,1)S(1)} %get-tuple-element.38), channel_id=1, source_target_pairs={{0,14},{2,12},{4,10},{6,8},{8,6},{10,4},{12,2},{14,0},{1,15},{3,13... | collective-permute-start | bytes 405512 | tf_op jit(solution)/shard_map/ppermute | solution.py:300
  66.3 1.9 %shard_map.72 = bf16[512,128]{1,0:T(8,128)(2,1)S(1)} custom-call(s32[1]{0:T(128)} %bitcast.me_ref, bf16[528,128]{1,0:T(8,128)(2,1)S(1)} %collective-permute-done.15.q_ref.tile_ref.refs_5_, bf16[528,128]{1,0:T(8,128)(2,1)S(1)} %collective-permute-done.15.q_ref.tile_ref.refs_5_, bf16[1024,128]{1,0:T(8,128)(2,1)S(1)} %collective-permute-done.4.refs_5_.k_ref.v_ref, ...), custom_call_target="tpu_custom_call" | custom-call | flops 268435456 | bytes 786432 | tf_op jit(solution)/shard_map/pallas_call | solution.py:236
  68.2 3.4 %collective-permute-start.16 = (bf16[512,128]{1,0:T(8,128)(2,1)S(1)}, bf16[512,128]{1,0:T(8,128)(2,1)S(1)}, u32[]{:S(2)}, u32[]{:S(2)}) collective-permute-start(bf16[512,128]{1,0:T(8,128)(2,1)S(1)} %shard_map.72), channel_id=1, source_target_pairs={{0,10},{2,8},{4,14},{6,12},{8,2},{10,0},{12,6},{14,4},{1,11},{3,9}... | collective-permute-start | bytes 393224 | tf_op jit(solution)/shard_map/ppermute | solution.py:300
  71.6 1.9 %shard_map.71 = bf16[512,128]{1,0:T(8,128)(2,1)S(1)} custom-call(s32[1]{0:T(128)} %bitcast.me_ref, bf16[528,128]{1,0:T(8,128)(2,1)S(1)} %collective-permute-done.13.q_ref.tile_ref.refs_4_, bf16[528,128]{1,0:T(8,128)(2,1)S(1)} %collective-permute-done.13.q_ref.tile_ref.refs_4_, bf16[1024,128]{1,0:T(8,128)(2,1)S(1)} %collective-permute-done.refs_4_.k_ref.v_ref, ...), custom_call_target="tpu_custom_call" | custom-call | flops 268435456 | bytes 786432 | tf_op jit(solution)/shard_map/pallas_call | solution.py:236
  74.5 1.9 %shard_map.69 = bf16[512,128]{1,0:T(8,128)(2,1)S(1)} custom-call(s32[1]{0:T(128)} %bitcast.me_ref, bf16[528,128]{1,0:T(8,128)(2,1)S(1)} %collective-permute-done.9.q_ref.tile_ref.refs_2_, bf16[528,128]{1,0:T(8,128)(2,1)S(1)} %collective-permute-done.9.q_ref.tile_ref.refs_2_, bf16[1024,128]{1,0:T(8,128)(2,1)S(1)} %collective-permute-done.2.refs_2_.k_ref.v_ref, ...), custom_call_target="tpu_custom_call" | custom-call | flops 268435456 | bytes 786432 | tf_op jit(solution)/shard_map/pallas_call | solution.py:236
  76.3 1.9 %shard_map.74 = bf16[512,128]{1,0:T(8,128)(2,1)S(1)} custom-call(s32[1]{0:T(128)} %bitcast.me_ref, bf16[528,128]{1,0:T(8,128)(2,1)S(1)} %collective-permute-done.19.q_ref.tile_ref.refs_7_, bf16[528,128]{1,0:T(8,128)(2,1)S(1)} %collective-permute-done.19.q_ref.tile_ref.refs_7_, bf16[1024,128]{1,0:T(8,128)(2,1)S(1)} %collective-permute-done.6.refs_7_.k_ref.v_ref, ...), custom_call_target="tpu_custom_call" | custom-call | flops 268435456 | bytes 786432 | tf_op jit(solution)/shard_map/pallas_call | solution.py:236
  79.0 1.9 %shard_map.70 = bf16[512,128]{1,0:T(8,128)(2,1)S(1)} custom-call(s32[1]{0:T(128)} %bitcast.me_ref, bf16[528,128]{1,0:T(8,128)(2,1)S(1)} %collective-permute-done.11.q_ref.tile_ref.refs_3_, bf16[528,128]{1,0:T(8,128)(2,1)S(1)} %collective-permute-done.11.q_ref.tile_ref.refs_3_, bf16[1024,128]{1,0:T(8,128)(2,1)S(1)} %collective-permute-done.3.refs_3_.k_ref.v_ref, ...), custom_call_target="tpu_custom_call" | custom-call | flops 268435456 | bytes 786432 | tf_op jit(solution)/shard_map/pallas_call | solution.py:236
  80.9 3.8 %collective-permute-start.20 = (bf16[512,128]{1,0:T(8,128)(2,1)S(1)}, bf16[512,128]{1,0:T(8,128)(2,1)S(1)}, u32[]{:S(2)}, u32[]{:S(2)}) collective-permute-start(bf16[512,128]{1,0:T(8,128)(2,1)S(1)} %shard_map.74), channel_id=1, source_target_pairs={{0,14},{2,12},{4,10},{6,8},{8,6},{10,4},{12,2},{14,0},{1,15},{3,13... | collective-permute-start | bytes 393224 | tf_op jit(solution)/shard_map/ppermute | solution.py:300
  84.7 2.5 %shard_map.73 = bf16[512,128]{1,0:T(8,128)(2,1)} custom-call(s32[1]{0:T(128)} %bitcast.me_ref, bf16[528,128]{1,0:T(8,128)(2,1)S(1)} %collective-permute-done.17.q_ref.tile_ref.refs_6_, bf16[528,128]{1,0:T(8,128)(2,1)S(1)} %collective-permute-done.17.q_ref.tile_ref.refs_6_, bf16[1024,128]{1,0:T(8,128)(2,1)S(1)} %collective-permute-done.5.refs_6_.k_ref.v_ref, ...), custom_call_target="tpu_custom_call" | custom-call | flops 268435456 | bytes 786432 | tf_op jit(solution)/shard_map/pallas_call | solution.py:236
  87.4 2.7 %shard_map.68 = bf16[512,128]{1,0:T(8,128)(2,1)} custom-call(s32[1]{0:T(128)} %bitcast.me_ref, bf16[528,128]{1,0:T(8,128)(2,1)S(1)} %collective-permute-done.7.q_ref.tile_ref.refs_1_, bf16[528,128]{1,0:T(8,128)(2,1)S(1)} %collective-permute-done.7.q_ref.tile_ref.refs_1_, bf16[1024,128]{1,0:T(8,128)(2,1)S(1)} %collective-permute-done.1.refs_1_.k_ref.v_ref, ...), custom_call_target="tpu_custom_call" | custom-call | flops 268435456 | bytes 786432 | tf_op jit(solution)/shard_map/pallas_call | solution.py:236
  92.1 1.9 %shard_map.67.refs_0_ = bf16[512,128]{1,0:T(8,128)(2,1)S(1)} custom-call(s32[1]{0:T(128)} %bitcast.me_ref, bf16[528,128]{1,0:T(8,128)(2,1)S(1)} %get-tuple-element.22.q_ref.tile_ref.refs_0_, bf16[528,128]{1,0:T(8,128)(2,1)S(1)} %get-tuple-element.22.q_ref.tile_ref.refs_0_, bf16[1024,128]{1,0:T(8,128)(2,1)S(1)} %copy-done.1, bf16[1024,128]{1,0:T(8,128)(2,1)S(1)} %copy-done.1, ...), custom_call_target="tpu_custom_call" | custom-call | flops 268435456 | bytes 786432 | tf_op jit(solution)/shard_map/pallas_call | solution.py:236
  95.4 1.8 %collective-permute-done.18.refs_6_ = bf16[512,128]{1,0:T(8,128)(2,1)S(1)} collective-permute-done((bf16[512,128]{1,0:T(8,128)(2,1)}, bf16[512,128]{1,0:T(8,128)(2,1)S(1)}, u32[]{:S(2)}, u32[]{:S(2)}) %collective-permute-start.18) | collective-permute-done | bytes 131104 | tf_op jit(solution)/shard_map/ppermute | solution.py:300
  (68 shorter events, 20.0 us)
Async XLA Ops:
  1.7 22.5 %collective-permute-start = (bf16[1024,128]{1,0:T(8,128)(2,1)S(1)}, bf16[1024,128]{1,0:T(8,128)(2,1)S(1)}, u32[]{:S(2)}, u32[]{:S(2)}) collective-permute-start(bf16[1024,128]{1,0:T(8,128)(2,1)S(1)} %pad_maximum_fusion), channel_id=1, source_target_pairs={{0,8},{2,10},{4,12},{6,14},{8,0},{10,2},{12,4},{14,6},{1,9},{3,11}... | collective-permute-start | bytes 786440 | tf_op jit(solution)/shard_map/ppermute | solution.py:300
  7.5 21.4 %collective-permute-start.1 = (bf16[1024,128]{1,0:T(8,128)(2,1)}, bf16[1024,128]{1,0:T(8,128)(2,1)S(1)}, u32[]{:S(2)}, u32[]{:S(2)}) collective-permute-start(bf16[1024,128]{1,0:T(8,128)(2,1)} %shard_map.61), channel_id=1, source_target_pairs={{0,2},{2,0},{4,6},{6,4},{8,10},{10,8},{12,14},{14,12},{1,3},{3,1},... | collective-permute-start | bytes 786440 | tf_op jit(solution)/shard_map/ppermute | solution.py:300
  10.6 31.7 %collective-permute-start.4 = (bf16[1024,128]{1,0:T(8,128)(2,1)}, bf16[1024,128]{1,0:T(8,128)(2,1)S(1)}, u32[]{:S(2)}, u32[]{:S(2)}) collective-permute-start(bf16[1024,128]{1,0:T(8,128)(2,1)} %shard_map.64), channel_id=1, source_target_pairs={{0,10},{2,8},{4,14},{6,12},{8,2},{10,0},{12,6},{14,4},{1,11},{3,9}... | collective-permute-start | bytes 786440 | tf_op jit(solution)/shard_map/ppermute | solution.py:300
  12.3 30.0 %collective-permute-start.2 = (bf16[1024,128]{1,0:T(8,128)(2,1)}, bf16[1024,128]{1,0:T(8,128)(2,1)S(1)}, u32[]{:S(2)}, u32[]{:S(2)}) collective-permute-start(bf16[1024,128]{1,0:T(8,128)(2,1)} %shard_map.62), channel_id=1, source_target_pairs={{0,4},{2,6},{4,0},{6,2},{8,12},{10,14},{12,8},{14,10},{1,5},{3,7},... | collective-permute-start | bytes 786440 | tf_op jit(solution)/shard_map/ppermute | solution.py:300
  15.9 29.4 %collective-permute-start.5 = (bf16[1024,128]{1,0:T(8,128)(2,1)}, bf16[1024,128]{1,0:T(8,128)(2,1)S(1)}, u32[]{:S(2)}, u32[]{:S(2)}) collective-permute-start(bf16[1024,128]{1,0:T(8,128)(2,1)} %shard_map.65), channel_id=1, source_target_pairs={{0,12},{2,14},{4,8},{6,10},{8,4},{10,6},{12,0},{14,2},{1,13},{3,15... | collective-permute-start | bytes 786440 | tf_op jit(solution)/shard_map/ppermute | solution.py:300
  24.1 40.6 %collective-permute-start.6 = (bf16[1024,128]{1,0:T(8,128)(2,1)S(1)}, bf16[1024,128]{1,0:T(8,128)(2,1)S(1)}, u32[]{:S(2)}, u32[]{:S(2)}) collective-permute-start(bf16[1024,128]{1,0:T(8,128)(2,1)S(1)} %copy-done.12), channel_id=1, source_target_pairs={{0,14},{2,12},{4,10},{6,8},{8,6},{10,4},{12,2},{14,0},{1,15},{3,13... | collective-permute-start | bytes 786440 | tf_op jit(solution)/shard_map/ppermute | solution.py:300
  28.9 37.2 %collective-permute-start.3 = (bf16[1024,128]{1,0:T(8,128)(2,1)}, bf16[1024,128]{1,0:T(8,128)(2,1)S(1)}, u32[]{:S(2)}, u32[]{:S(2)}) collective-permute-start(bf16[1024,128]{1,0:T(8,128)(2,1)} %shard_map.63), channel_id=1, source_target_pairs={{0,6},{2,4},{4,2},{6,0},{8,14},{10,12},{12,10},{14,8},{1,7},{3,5},... | collective-permute-start | bytes 786440 | tf_op jit(solution)/shard_map/ppermute | solution.py:300
  32.0 34.3 %copy-start.1 = (bf16[1024,128]{1,0:T(8,128)(2,1)S(1)}, bf16[1024,128]{1,0:T(8,128)(2,1)}, u32[]{:S(2)}) copy-start(bf16[1024,128]{1,0:T(8,128)(2,1)} %shard_map.59.k_ref.v_ref.refs_0_) | copy-start | bytes 786436
  33.2 58.9 %copy-start.2 = (bf16[528,128]{1,0:T(8,128)(2,1)}, bf16[528,128]{1,0:T(8,128)(2,1)S(1)}, u32[]{:S(2)}) copy-start(bf16[528,128]{1,0:T(8,128)(2,1)S(1)} %get-tuple-element.22.q_ref.tile_ref.refs_0_) | copy-start | bytes 405508
  42.3 18.7 %collective-permute-start.13 = (bf16[528,128]{1,0:T(8,128)(2,1)S(1)}, bf16[528,128]{1,0:T(8,128)(2,1)S(1)}, u32[]{:S(2)}, u32[]{:S(2)}) collective-permute-start(bf16[528,128]{1,0:T(8,128)(2,1)S(1)} %get-tuple-element.32), channel_id=1, source_target_pairs={{0,8},{2,10},{4,12},{6,14},{8,0},{10,2},{12,4},{14,6},{1,9},{3,11}... | collective-permute-start | bytes 405512 | tf_op jit(solution)/shard_map/ppermute | solution.py:300
  42.3 22.4 %collective-permute-start.9 = (bf16[528,128]{1,0:T(8,128)(2,1)S(1)}, bf16[528,128]{1,0:T(8,128)(2,1)S(1)}, u32[]{:S(2)}, u32[]{:S(2)}) collective-permute-start(bf16[528,128]{1,0:T(8,128)(2,1)S(1)} %get-tuple-element.28), channel_id=1, source_target_pairs={{0,4},{2,6},{4,0},{6,2},{8,12},{10,14},{12,8},{14,10},{1,5},{3,7},... | collective-permute-start | bytes 405512 | tf_op jit(solution)/shard_map/ppermute | solution.py:300
  45.3 21.0 %collective-permute-start.15 = (bf16[528,128]{1,0:T(8,128)(2,1)S(1)}, bf16[528,128]{1,0:T(8,128)(2,1)S(1)}, u32[]{:S(2)}, u32[]{:S(2)}) collective-permute-start(bf16[528,128]{1,0:T(8,128)(2,1)S(1)} %get-tuple-element.34), channel_id=1, source_target_pairs={{0,10},{2,8},{4,14},{6,12},{8,2},{10,0},{12,6},{14,4},{1,11},{3,9}... | collective-permute-start | bytes 405512 | tf_op jit(solution)/shard_map/ppermute | solution.py:300
  61.0 10.6 %copy-start.3 = (bf16[528,128]{1,0:T(8,128)(2,1)}, bf16[528,128]{1,0:T(8,128)(2,1)S(1)}, u32[]{:S(2)}) copy-start(bf16[528,128]{1,0:T(8,128)(2,1)S(1)} %collective-permute-done.13.q_ref.tile_ref.refs_4_) | copy-start | bytes 405508
  61.0 12.5 %collective-permute-start.19 = (bf16[528,128]{1,0:T(8,128)(2,1)S(1)}, bf16[528,128]{1,0:T(8,128)(2,1)S(1)}, u32[]{:S(2)}, u32[]{:S(2)}) collective-permute-start(bf16[528,128]{1,0:T(8,128)(2,1)S(1)} %get-tuple-element.38), channel_id=1, source_target_pairs={{0,14},{2,12},{4,10},{6,8},{8,6},{10,4},{12,2},{14,0},{1,15},{3,13... | collective-permute-start | bytes 405512 | tf_op jit(solution)/shard_map/ppermute | solution.py:300
  64.7 13.5 %collective-permute-start.11 = (bf16[528,128]{1,0:T(8,128)(2,1)S(1)}, bf16[528,128]{1,0:T(8,128)(2,1)S(1)}, u32[]{:S(2)}, u32[]{:S(2)}) collective-permute-start(bf16[528,128]{1,0:T(8,128)(2,1)S(1)} %get-tuple-element.30), channel_id=1, source_target_pairs={{0,6},{2,4},{4,2},{6,0},{8,14},{10,12},{12,10},{14,8},{1,7},{3,5},... | collective-permute-start | bytes 405512 | tf_op jit(solution)/shard_map/ppermute | solution.py:300
  64.7 16.2 %collective-permute-start.17 = (bf16[528,128]{1,0:T(8,128)(2,1)S(1)}, bf16[528,128]{1,0:T(8,128)(2,1)S(1)}, u32[]{:S(2)}, u32[]{:S(2)}) collective-permute-start(bf16[528,128]{1,0:T(8,128)(2,1)S(1)} %get-tuple-element.36), channel_id=1, source_target_pairs={{0,12},{2,14},{4,8},{6,10},{8,4},{10,6},{12,0},{14,2},{1,13},{3,15... | collective-permute-start | bytes 405512 | tf_op jit(solution)/shard_map/ppermute | solution.py:300
  66.1 21.1 %collective-permute-start.7 = (bf16[528,128]{1,0:T(8,128)(2,1)S(1)}, bf16[528,128]{1,0:T(8,128)(2,1)S(1)}, u32[]{:S(2)}, u32[]{:S(2)}) collective-permute-start(bf16[528,128]{1,0:T(8,128)(2,1)S(1)} %get-tuple-element.26), channel_id=1, source_target_pairs={{0,2},{2,0},{4,6},{6,4},{8,10},{10,8},{12,14},{14,12},{1,3},{3,1},... | collective-permute-start | bytes 405512 | tf_op jit(solution)/shard_map/ppermute | solution.py:300
  68.2 21.9 %collective-permute-start.16 = (bf16[512,128]{1,0:T(8,128)(2,1)S(1)}, bf16[512,128]{1,0:T(8,128)(2,1)S(1)}, u32[]{:S(2)}, u32[]{:S(2)}) collective-permute-start(bf16[512,128]{1,0:T(8,128)(2,1)S(1)} %shard_map.72), channel_id=1, source_target_pairs={{0,10},{2,8},{4,14},{6,12},{8,2},{10,0},{12,6},{14,4},{1,11},{3,9}... | collective-permute-start | bytes 393224 | tf_op jit(solution)/shard_map/ppermute | solution.py:300
  73.5 18.1 %collective-permute-start.14 = (bf16[512,128]{1,0:T(8,128)(2,1)S(1)}, bf16[512,128]{1,0:T(8,128)(2,1)S(1)}, u32[]{:S(2)}, u32[]{:S(2)}) collective-permute-start(bf16[512,128]{1,0:T(8,128)(2,1)S(1)} %shard_map.71), channel_id=1, source_target_pairs={{0,8},{2,10},{4,12},{6,14},{8,0},{10,2},{12,4},{14,6},{1,9},{3,11}... | collective-permute-start | bytes 393224 | tf_op jit(solution)/shard_map/ppermute | solution.py:300
  78.2 17.2 %collective-permute-start.10 = (bf16[512,128]{1,0:T(8,128)(2,1)S(1)}, bf16[512,128]{1,0:T(8,128)(2,1)S(1)}, u32[]{:S(2)}, u32[]{:S(2)}) collective-permute-start(bf16[512,128]{1,0:T(8,128)(2,1)S(1)} %shard_map.69), channel_id=1, source_target_pairs={{0,4},{2,6},{4,0},{6,2},{8,12},{10,14},{12,8},{14,10},{1,5},{3,7},... | collective-permute-start | bytes 393224 | tf_op jit(solution)/shard_map/ppermute | solution.py:300
  80.9 14.5 %collective-permute-start.20 = (bf16[512,128]{1,0:T(8,128)(2,1)S(1)}, bf16[512,128]{1,0:T(8,128)(2,1)S(1)}, u32[]{:S(2)}, u32[]{:S(2)}) collective-permute-start(bf16[512,128]{1,0:T(8,128)(2,1)S(1)} %shard_map.74), channel_id=1, source_target_pairs={{0,14},{2,12},{4,10},{6,8},{8,6},{10,4},{12,2},{14,0},{1,15},{3,13... | collective-permute-start | bytes 393224 | tf_op jit(solution)/shard_map/ppermute | solution.py:300
  87.2 8.2 %collective-permute-start.12 = (bf16[512,128]{1,0:T(8,128)(2,1)S(1)}, bf16[512,128]{1,0:T(8,128)(2,1)S(1)}, u32[]{:S(2)}, u32[]{:S(2)}) collective-permute-start(bf16[512,128]{1,0:T(8,128)(2,1)S(1)} %shard_map.70), channel_id=1, source_target_pairs={{0,6},{2,4},{4,2},{6,0},{8,14},{10,12},{12,10},{14,8},{1,7},{3,5},... | collective-permute-start | bytes 393224 | tf_op jit(solution)/shard_map/ppermute | solution.py:300
  90.1 7.1 %collective-permute-start.18 = (bf16[512,128]{1,0:T(8,128)(2,1)}, bf16[512,128]{1,0:T(8,128)(2,1)S(1)}, u32[]{:S(2)}, u32[]{:S(2)}) collective-permute-start(bf16[512,128]{1,0:T(8,128)(2,1)} %shard_map.73), channel_id=1, source_target_pairs={{0,12},{2,14},{4,8},{6,10},{8,4},{10,6},{12,0},{14,2},{1,13},{3,15... | collective-permute-start | bytes 393224 | tf_op jit(solution)/shard_map/ppermute | solution.py:300
  91.5 5.7 %collective-permute-start.8 = (bf16[512,128]{1,0:T(8,128)(2,1)}, bf16[512,128]{1,0:T(8,128)(2,1)S(1)}, u32[]{:S(2)}, u32[]{:S(2)}) collective-permute-start(bf16[512,128]{1,0:T(8,128)(2,1)} %shard_map.68), channel_id=1, source_target_pairs={{0,2},{2,0},{4,6},{6,4},{8,10},{10,8},{12,14},{14,12},{1,3},{3,1},... | collective-permute-start | bytes 393224 | tf_op jit(solution)/shard_map/ppermute | solution.py:300
  (11 other events, 42.9 us)
